TPU v7x, 32 devices: a whole 2x2x4 slice. The times are simulated.
32 devices in a mesh: dp: 4 (over x, core), seq: 8 (over z, y).
Axes of the slice: x: 2, y: 2, z: 4, core: 2. Of those that a mesh axis runs over, the one named last changes fastest.
Arguments:
- inputs: bfloat16 [4, 1024, 2048], P('dp', 'seq'), may hold values from -6 to 6
- attention_gain: bfloat16 [2048], P(('dp', 'seq')), may hold values from 0.5 to 1.5
- query_weight: bfloat16 [2048, 2048], P(('dp', 'seq')), may hold values from -0.125 to 0.125
- key_weight: bfloat16 [2048, 256], P(('dp', 'seq')), may hold values from -0.125 to 0.125
- value_weight: bfloat16 [2048, 256], P(('dp', 'seq')), may hold values from -0.125 to 0.125
- output_weight: bfloat16 [2048, 2048], P(('dp', 'seq')), may hold values from -0.5 to 0.5
- feedforward_gain: bfloat16 [2048], P(('dp', 'seq')), may hold values from 0.5 to 1.5
- gate_weight: bfloat16 [2048, 5632], P(('dp', 'seq')), may hold values from -0.125 to 0.125
- up_weight: bfloat16 [2048, 5632], P(('dp', 'seq')), may hold values from -0.125 to 0.125
- down_weight: bfloat16 [5632, 2048], P(('dp', 'seq')), may hold values from -0.078125 to 0.078125
- cotangent: bfloat16 [4, 1024, 2048], P('dp', 'seq'), may hold values from -6 to 6
Outputs:
- layer_output: bfloat16 [4, 1024, 2048], P('dp', 'seq')
- input_grad: float32 [4, 1024, 2048], P('dp', 'seq')
- attention_gain_grad: float32 [2048], P(('dp', 'seq'))
- query_grad: float32 [2048, 2048], P(('dp', 'seq'))
- key_grad: float32 [2048, 256], P(('dp', 'seq'))
- value_grad: float32 [2048, 256], P(('dp', 'seq'))
- output_grad: float32 [2048, 2048], P(('dp', 'seq'))
- feedforward_gain_grad: float32 [2048], P(('dp', 'seq'))
- gate_grad: float32 [2048, 5632], P(('dp', 'seq'))
- up_grad: float32 [2048, 5632], P(('dp', 'seq'))
- down_grad: float32 [5632, 2048], P(('dp', 'seq'))
All inputs are finite; a program needn't handle non-finite values.
Results may differ from a plain program's by a relative error of at most 0.02.
Values may be sent and summed in bfloat16 or wider, within the bound.
A program may use at most 384 MiB of HBM per device.

v0:
```python
import jax
import jax.numpy as jnp
from jax import lax
from jax.sharding import PartitionSpec as P

H = 32
KV = 4
HEAD = 64


epsilon = 1e-05
masked = -1e30


def rope_tables(positions):
    half_width = HEAD // 2
    frequency = 10000.0 ** (-(jnp.arange(half_width, dtype=jnp.float32) * 2.0) / HEAD)
    angles = positions[:, None] * frequency[None, :]
    return (jnp.cos(angles), jnp.sin(angles))


def rotate(values, cosine_part, sine_part):
    half_width = HEAD // 2
    front_half = values[..., :half_width]
    back_half = values[..., half_width:]
    cosine_part = cosine_part[:, None, :]
    sine_part = sine_part[:, None, :]
    return jnp.concatenate(
        [
            front_half * cosine_part - back_half * sine_part,
            back_half * cosine_part + front_half * sine_part,
        ],
        axis=-1,
    )


def unrotate(values, cosine_part, sine_part):
    half_width = HEAD // 2
    front_half = values[..., :half_width]
    back_half = values[..., half_width:]
    cosine_part = cosine_part[:, None, :]
    sine_part = sine_part[:, None, :]
    return jnp.concatenate(
        [
            front_half * cosine_part + back_half * sine_part,
            back_half * cosine_part - front_half * sine_part,
        ],
        axis=-1,
    )


def rms_scale(values):
    return lax.rsqrt(jnp.mean(values * values, axis=-1, keepdims=True) + epsilon)


def norm_back(grad_normed, scaled, scale_rows, gain_vector):
    upstream = grad_normed * gain_vector
    return scale_rows * (upstream - scaled * jnp.mean(upstream * scaled, axis=-1, keepdims=True))


def times_transposed(left_side, right_side):
    return lax.dot_general(
        left_side, right_side, (((1,), (1,)), ((), ())), preferred_element_type=jnp.float32
    )


def transposed_times(left_side, right_side):
    return lax.dot_general(
        left_side, right_side, (((0,), (0,)), ((), ())), preferred_element_type=jnp.float32
    )


def causal_mask(offset, block_rows, block_end):
    return jnp.arange(block_end)[None, :] <= (offset + jnp.arange(block_rows))[:, None]


def gather_attention(gain_vector, query_weight, key_weight, value_weight, output_weight):
    return (
        lax.all_gather(gain_vector, ("dp", "seq"), axis=0, tiled=True),
        lax.all_gather(query_weight, ("dp", "seq"), axis=0, tiled=True),
        lax.all_gather(key_weight, ("dp", "seq"), axis=0, tiled=True),
        lax.all_gather(value_weight, ("dp", "seq"), axis=0, tiled=True),
        lax.all_gather(output_weight, ("dp", "seq"), axis=0, tiled=True),
    )


def gather_feedforward(gain_vector, gate_weight, up_weight, down_weight):
    return (
        lax.all_gather(gain_vector, ("dp", "seq"), axis=0, tiled=True),
        lax.all_gather(gate_weight, ("dp", "seq"), axis=0, tiled=True),
        lax.all_gather(up_weight, ("dp", "seq"), axis=0, tiled=True),
        lax.all_gather(down_weight, ("dp", "seq"), axis=0, tiled=True),
    )


def to_heads(packed):
    return lax.all_to_all(packed, "seq", split_axis=2, concat_axis=1, tiled=True)


def to_tokens(packed):
    return lax.all_to_all(packed, "seq", split_axis=1, concat_axis=2, tiled=True)


def weight_gradient(left_rows, right_rows, rows_dev):
    left_all, right_all = (
        lax.all_gather(left_rows, "dp", axis=0, tiled=True),
        lax.all_gather(right_rows, "dp", axis=0, tiled=True),
    )
    base_row = lax.axis_index("dp") * (rows_dev * lax.axis_size("seq"))
    return lax.psum_scatter(
        transposed_times(
            lax.dynamic_slice_in_dim(left_all, base_row, lax.axis_size("seq") * rows_dev, 1),
            right_all,
        ).astype(jnp.bfloat16),
        "seq",
        scatter_dimension=0,
        tiled=True,
    ).astype(jnp.float32)


def attention_forward(queries, key_heads, value_heads, block_rows, score_scale):
    outputs = []
    totals = []
    for block_index in range(queries.shape[1] // block_rows):
        offset = block_index * block_rows
        block_end = offset + block_rows
        scores = (
            jnp.einsum(
                "sqhd,skd->shqk",
                queries[:, offset:block_end],
                key_heads[:, :block_end],
                preferred_element_type=jnp.float32,
            )
            * score_scale
        )
        scores = jnp.where(causal_mask(offset, block_rows, block_end), scores, masked)
        row_max = jnp.max(scores, axis=-1, keepdims=True)
        log_total = row_max + jnp.log(jnp.sum(jnp.exp(scores - row_max), axis=-1, keepdims=True))
        probs_low = jnp.exp(scores - log_total).astype(jnp.bfloat16)
        outputs.append(
            jnp.einsum(
                "shqk,skd->sqhd",
                probs_low,
                value_heads[:, :block_end],
                preferred_element_type=jnp.float32,
            ).astype(jnp.bfloat16)
        )
        totals.append(log_total)
    return (jnp.concatenate(outputs, axis=1), jnp.concatenate(totals, axis=2))


def attention_backward(
    queries, key_heads, value_heads, grad_heads, totals, block_rows, score_scale
):
    length = key_heads.shape[1]
    key_sum = jnp.zeros(key_heads.shape, jnp.float32)
    value_sum = jnp.zeros(value_heads.shape, jnp.float32)
    query_parts = []
    for block_index in range(length // block_rows):
        offset = block_index * block_rows
        block_end = offset + block_rows
        query_block = queries[:, offset:block_end]
        key_block = key_heads[:, :block_end]
        value_block = value_heads[:, :block_end]
        grad_block = grad_heads[:, offset:block_end]
        scores = (
            jnp.einsum("sqhd,skd->shqk", query_block, key_block, preferred_element_type=jnp.float32)
            * score_scale
        )
        scores = jnp.where(causal_mask(offset, block_rows, block_end), scores, masked)
        probabilities = jnp.exp(scores - totals[:, :, offset:block_end])
        probs_low = probabilities.astype(jnp.bfloat16)
        grad_probs = jnp.einsum(
            "sqhd,skd->shqk", grad_block, value_block, preferred_element_type=jnp.float32
        )
        row_inner = jnp.sum(probabilities * grad_probs, axis=-1, keepdims=True)
        grad_scores = (probabilities * (grad_probs - row_inner)).astype(jnp.bfloat16)
        query_parts.append(
            (
                jnp.einsum(
                    "shqk,skd->sqhd", grad_scores, key_block, preferred_element_type=jnp.float32
                )
                * score_scale
            ).astype(jnp.bfloat16)
        )
        padding = ((0, 0), (0, length - block_end), (0, 0))
        key_sum = key_sum + jnp.pad(
            jnp.einsum(
                "shqk,sqhd->skd", grad_scores, query_block, preferred_element_type=jnp.float32
            )
            * score_scale,
            padding,
        )
        value_sum = value_sum + jnp.pad(
            jnp.einsum("shqk,sqhd->skd", probs_low, grad_block, preferred_element_type=jnp.float32),
            padding,
        )
    return (
        jnp.concatenate(query_parts, axis=1),
        key_sum.astype(jnp.bfloat16),
        value_sum.astype(jnp.bfloat16),
    )


def forward(
    inputs, attention_weights, feedforward_weights, cosine_part, sine_part, block_rows, score_scale
):
    gain_one, query_full, key_full, value_full, output_full = attention_weights
    gain_two, gate_full, up_full, down_full = feedforward_weights
    sequences, tokens, model_width = inputs.shape
    groups = lax.axis_size("seq")
    heads_dev = H // groups
    repeats = groups // KV
    split_at = heads_dev * HEAD
    flattened = inputs.reshape(sequences * tokens, model_width).astype(jnp.float32)
    scale_one = rms_scale(flattened)
    scaled_one = flattened * scale_one
    normed_one = (scaled_one * gain_one.astype(jnp.float32)).astype(jnp.bfloat16)
    query_raw = jnp.dot(normed_one, query_full, preferred_element_type=jnp.float32)
    key_raw = jnp.dot(normed_one, key_full, preferred_element_type=jnp.float32)
    value_part = jnp.dot(normed_one, value_full, preferred_element_type=jnp.float32).astype(
        jnp.bfloat16
    )
    queries = rotate(query_raw.reshape(sequences, tokens, H, HEAD), cosine_part, sine_part).astype(
        jnp.bfloat16
    )
    key_rotated = rotate(
        key_raw.reshape(sequences, tokens, KV, HEAD), cosine_part, sine_part
    ).astype(jnp.bfloat16)
    packed = jnp.concatenate(
        [
            queries.reshape(sequences, tokens, groups, split_at),
            jnp.repeat(key_rotated, repeats, axis=2),
            jnp.repeat(value_part.reshape(sequences, tokens, KV, HEAD), repeats, axis=2),
        ],
        axis=3,
    )
    arrived = to_heads(packed)[:, :, 0, :]
    head_queries = arrived[..., :split_at].reshape(sequences, -1, heads_dev, HEAD)
    key_heads = arrived[..., split_at : split_at + HEAD]
    value_heads = arrived[..., split_at + HEAD :]
    attended, totals = attention_forward(
        head_queries, key_heads, value_heads, block_rows, score_scale
    )
    regrouped = to_tokens(attended.reshape(sequences, -1, 1, split_at)).reshape(
        sequences * tokens, model_width
    )
    middle = flattened + jnp.dot(regrouped, output_full, preferred_element_type=jnp.float32)
    scale_two = rms_scale(middle)
    scaled_two = middle * scale_two
    normed_two = (scaled_two * gain_two.astype(jnp.float32)).astype(jnp.bfloat16)
    gate_values = jnp.dot(normed_two, gate_full, preferred_element_type=jnp.float32)
    up_values = jnp.dot(normed_two, up_full, preferred_element_type=jnp.float32)
    hidden = (jax.nn.silu(gate_values) * up_values).astype(jnp.bfloat16)
    output = (
        (middle + jnp.dot(hidden, down_full, preferred_element_type=jnp.float32))
        .astype(jnp.bfloat16)
        .reshape(sequences, tokens, model_width)
    )
    saved = (
        scale_one,
        scaled_one,
        normed_one,
        head_queries,
        key_heads,
        value_heads,
        totals,
        regrouped,
        scale_two,
        scaled_two,
        normed_two,
        gate_values,
        up_values,
        hidden,
    )
    return (output, saved)


def shards(
    inputs,
    attention_gain,
    query_weight,
    key_weight,
    value_weight,
    output_weight,
    feedforward_gain,
    gate_weight,
    up_weight,
    down_weight,
    cotangent,
):
    sequences, tokens, model_width = inputs.shape
    groups = lax.axis_size("seq")
    heads_dev = H // groups
    split_at = heads_dev * HEAD
    length = tokens * groups
    block_rows = min(length, max(512, length // 8))
    score_scale = HEAD ** (-0.5)
    positions = (lax.axis_index("seq") * tokens + jnp.arange(tokens, dtype=jnp.int32)).astype(
        jnp.float32
    )
    cosine_part, sine_part = rope_tables(positions)
    attention_weights = gather_attention(
        attention_gain, query_weight, key_weight, value_weight, output_weight
    )
    feedforward_weights = gather_feedforward(feedforward_gain, gate_weight, up_weight, down_weight)
    output, saved = forward(
        inputs,
        attention_weights,
        feedforward_weights,
        cosine_part,
        sine_part,
        block_rows,
        score_scale,
    )
    barriered = lax.optimization_barrier(
        (
            inputs,
            attention_gain,
            query_weight,
            key_weight,
            value_weight,
            output_weight,
            feedforward_gain,
            gate_weight,
            up_weight,
            down_weight,
            output,
        )
    )
    attention_weights = gather_attention(
        barriered[1], barriered[2], barriered[3], barriered[4], barriered[5]
    )
    feedforward_weights = gather_feedforward(barriered[6], barriered[7], barriered[8], barriered[9])
    unused, saved = forward(
        barriered[0],
        attention_weights,
        feedforward_weights,
        cosine_part,
        sine_part,
        block_rows,
        score_scale,
    )
    (
        scale_one,
        scaled_one,
        normed_one,
        head_queries,
        key_heads,
        value_heads,
        totals,
        regrouped,
        scale_two,
        scaled_two,
        normed_two,
        gate_values,
        up_values,
        hidden,
    ) = saved
    gain_one, query_full, key_full, value_full, output_full = attention_weights
    gain_two, gate_full, up_full, down_full = feedforward_weights
    width_rows = attention_gain.shape[0]
    down_rows = down_weight.shape[0]
    hidden_units = gate_weight.shape[1]
    kv_width = KV * HEAD
    row_count = sequences * tokens
    grad_out = cotangent.reshape(row_count, model_width)
    down_sum = weight_gradient(hidden, grad_out, down_rows)
    grad_hidden = times_transposed(grad_out, down_full)
    sigmoid_gate = jax.nn.sigmoid(gate_values)
    grad_gate = (
        grad_hidden * up_values * sigmoid_gate * (1.0 + gate_values * (1.0 - sigmoid_gate))
    ).astype(jnp.bfloat16)
    grad_up = (grad_hidden * (gate_values * sigmoid_gate)).astype(jnp.bfloat16)
    grad_both = jnp.concatenate([grad_gate, grad_up], axis=1)
    feedforward_sum = weight_gradient(normed_two, grad_both, width_rows)
    grad_normed_two = times_transposed(grad_gate, gate_full) + times_transposed(grad_up, up_full)
    gain_two_part = jnp.sum(grad_normed_two * scaled_two, axis=0)
    grad_middle = grad_out.astype(jnp.float32) + norm_back(
        grad_normed_two, scaled_two, scale_two, gain_two.astype(jnp.float32)
    )
    middle_low = grad_middle.astype(jnp.bfloat16)
    output_sum = weight_gradient(regrouped, middle_low, width_rows)
    grad_attended = times_transposed(middle_low, output_full).astype(jnp.bfloat16)
    grad_heads = to_heads(grad_attended.reshape(sequences, tokens, groups, split_at))[
        :, :, 0, :
    ].reshape(sequences, length, heads_dev, HEAD)
    query_part, key_part, value_part = attention_backward(
        head_queries, key_heads, value_heads, grad_heads, totals, block_rows, score_scale
    )
    packed = jnp.concatenate(
        [
            query_part.reshape(sequences, length, 1, split_at),
            key_part[:, :, None, :],
            value_part[:, :, None, :],
        ],
        axis=3,
    )
    returned = to_tokens(packed)
    grad_queries = returned[..., :split_at].reshape(sequences, tokens, H, HEAD).astype(jnp.float32)
    grad_keys = jnp.sum(
        returned[..., split_at : split_at + HEAD]
        .astype(jnp.float32)
        .reshape(sequences, tokens, KV, groups // KV, HEAD),
        axis=3,
    )
    grad_values = (
        jnp.sum(
            returned[..., split_at + HEAD :]
            .astype(jnp.float32)
            .reshape(sequences, tokens, KV, groups // KV, HEAD),
            axis=3,
        )
        .astype(jnp.bfloat16)
        .reshape(row_count, kv_width)
    )
    grad_query_raw = (
        unrotate(grad_queries, cosine_part, sine_part)
        .astype(jnp.bfloat16)
        .reshape(row_count, model_width)
    )
    grad_key_raw = (
        unrotate(grad_keys, cosine_part, sine_part)
        .astype(jnp.bfloat16)
        .reshape(row_count, kv_width)
    )
    grad_three = jnp.concatenate([grad_query_raw, grad_key_raw, grad_values], axis=1)
    attention_sum = weight_gradient(normed_one, grad_three, width_rows)
    grad_normed_one = (
        times_transposed(grad_query_raw, query_full)
        + times_transposed(grad_key_raw, key_full)
        + times_transposed(grad_values, value_full)
    )
    gain_one_part = jnp.sum(grad_normed_one * scaled_one, axis=0)
    input_grad = grad_middle + norm_back(
        grad_normed_one, scaled_one, scale_one, gain_one.astype(jnp.float32)
    )
    gain_one_grad, gain_two_grad = (
        lax.psum_scatter(gain_one_part, ("dp", "seq"), scatter_dimension=0, tiled=True),
        lax.psum_scatter(gain_two_part, ("dp", "seq"), scatter_dimension=0, tiled=True),
    )
    return (
        output,
        input_grad.reshape(sequences, tokens, model_width),
        gain_one_grad,
        attention_sum[:, :model_width],
        attention_sum[:, model_width : model_width + kv_width],
        attention_sum[:, model_width + kv_width :],
        output_sum,
        gain_two_grad,
        feedforward_sum[:, :hidden_units],
        feedforward_sum[:, hidden_units:],
        down_sum,
    )


def solution(mesh):
    in_specs = (
        P("dp", "seq", None),
        P(("dp", "seq")),
        P(("dp", "seq"), None),
        P(("dp", "seq"), None),
        P(("dp", "seq"), None),
        P(("dp", "seq"), None),
        P(("dp", "seq")),
        P(("dp", "seq"), None),
        P(("dp", "seq"), None),
        P(("dp", "seq"), None),
        P("dp", "seq", None),
    )
    out_specs = (
        P("dp", "seq", None),
        P("dp", "seq", None),
        P(("dp", "seq")),
        P(("dp", "seq"), None),
        P(("dp", "seq"), None),
        P(("dp", "seq"), None),
        P(("dp", "seq"), None),
        P(("dp", "seq")),
        P(("dp", "seq"), None),
        P(("dp", "seq"), None),
        P(("dp", "seq"), None),
    )
    return jax.shard_map(shards, mesh=mesh, in_specs=in_specs, out_specs=out_specs, check_vma=False)
```

profile of v0, /device:TPU:26, one launch (start us, length us, event | category | flops | bytes accessed | tf_op | source)
XLA Modules:
  0.0 2306.8 jit_solution(6046675401421668106)
XLA Ops:
  13.6 40.1 %all-reduce.10 = (bf16[2048]{0:T(1024)(128)(2,1)S(1)}, bf16[2048]{0:T(1024)(128)(2,1)S(1)}) all-reduce(bf16[2048]{0:T(1024)(128)(2,1)S(1)} %dynamic-update-slice, bf16[2048]{0:T(1024)(128)(2,1)S(1)} %dynamic-update-slice.1), channel_id=1, replica_groups=mesh['dp'=4,'seq'=8] {'dp','seq'}, use_global_device_ids=true, to_apply=%add.2 | all-reduce | flops 4096 | bytes 16384
  66.6 54.0 %all-gather.26.cloned.1.call-done = bf16[2048,256]{1,0:T(8,128)(2,1)} async-done(((bf16[64,256]{1,0:T(8,128)(2,1)}), bf16[2048,256]{1,0:T(8,128)(2,1)}) %all-gather.26.cloned.1.call-update) | async-done | bytes 1048592 | tf_op jit(solution)/shard_map/all_gather | solution.py:81
  122.6 76.8 %all-gather.24.cloned.1.call-done = bf16[2048,2048]{1,0:T(8,128)(2,1)} async-done(((bf16[64,2048]{1,0:T(8,128)(2,1)}), bf16[2048,2048]{1,0:T(8,128)(2,1)}) %all-gather.24.cloned.1.call-update) | async-done | bytes 8388624 | tf_op jit(solution)/shard_map/all_gather | solution.py:80
  224.8 29.3 %all-to-all-done = bf16[1,128,8,384]{1,3,0,2:T(8,128)(2,1)S(1)} async-done(((bf16[1,128,8,384]{1,3,0,2:T(8,128)(2,1)}), bf16[1,128,8,384]{1,3,0,2:T(8,128)(2,1)S(1)}, u32[]{:S(2)}, u32[]{:S(2)}) %all-to-all-start) | async-done | bytes 786464 | tf_op jit(solution)/shard_map/all_to_all | solution.py:97
  276.1 19.6 all-to-all-done.1
  303.2 137.9 %all-gather.32.cloned.1.call-done = bf16[2048,5632]{1,0:T(8,128)(2,1)} async-done(((bf16[64,5632]{1,0:T(8,128)(2,1)}), bf16[2048,5632]{1,0:T(8,128)(2,1)}) %all-gather.32.cloned.1.call-update) | async-done | bytes 23068688 | tf_op jit(solution)/shard_map/all_gather | solution.py:90
  453.6 132.4 %all-gather.36.cloned.1.call-done = bf16[5632,2048]{1,0:T(8,128)(2,1)} async-done(((bf16[176,2048]{1,0:T(8,128)(2,1)}), bf16[5632,2048]{1,0:T(8,128)(2,1)}) %all-gather.36.cloned.1.call-update) | async-done | bytes 23068688 | tf_op jit(solution)/shard_map/all_gather | solution.py:92
  586.0 145.0 %all-gather.34.cloned.1.call-done = bf16[2048,5632]{1,0:T(8,128)(2,1)} async-done(((bf16[64,5632]{1,0:T(8,128)(2,1)}), bf16[2048,5632]{1,0:T(8,128)(2,1)}) %all-gather.34.cloned.1.call-update) | async-done | bytes 23068688 | tf_op jit(solution)/shard_map/all_gather | solution.py:91
  731.0 19.4 fusion.20
  754.9 40.5 %all-reduce.9 = (bf16[2048]{0:T(1024)(128)(2,1)S(1)}, bf16[2048]{0:T(1024)(128)(2,1)S(1)}) all-reduce(bf16[2048]{0:T(1024)(128)(2,1)S(1)} %dynamic-update-slice.2, bf16[2048]{0:T(1024)(128)(2,1)S(1)} %dynamic-update-slice.3), channel_id=1, replica_groups=mesh['dp'=4,'seq'=8] {'dp','seq'}, use_global_device_ids=true, to_apply=%add.4 | all-reduce | flops 4096 | bytes 16384
  805.3 54.2 %all-gather.40.cloned.1.call-done = bf16[2048,256]{1,0:T(8,128)(2,1)} async-done(((bf16[64,256]{1,0:T(8,128)(2,1)}), bf16[2048,256]{1,0:T(8,128)(2,1)}) %all-gather.40.cloned.1.call-update) | async-done | bytes 1048592 | tf_op jit(solution)/shard_map/all_gather | solution.py:81
  861.5 76.6 %all-gather.38.cloned.1.call-done = bf16[2048,2048]{1,0:T(8,128)(2,1)} async-done(((bf16[64,2048]{1,0:T(8,128)(2,1)}), bf16[2048,2048]{1,0:T(8,128)(2,1)}) %all-gather.38.cloned.1.call-update) | async-done | bytes 8388624 | tf_op jit(solution)/shard_map/all_gather | solution.py:80
  956.7 34.1 %all_to_all.93 = bf16[1,128,8,384]{1,3,0,2:T(8,128)(2,1)S(1)} all-to-all(bf16[1,128,8,384]{1,3,0,2:T(8,128)(2,1)S(1)} %pad_maximum_fusion.3), channel_id=1, replica_groups=mesh['dp'=4,'seq'=8] {'seq'}, dimensions={2} | all-to-all | bytes 1572864 | tf_op jit(solution)/shard_map/all_to_all | solution.py:97
  1012.7 19.8 all-to-all-done.3
  1039.0 139.0 %all-gather.50.cloned.1.call-done = bf16[2048,5632]{1,0:T(8,128)(2,1)} async-done(((bf16[64,5632]{1,0:T(8,128)(2,1)}), bf16[2048,5632]{1,0:T(8,128)(2,1)}) %all-gather.50.cloned.1.call-update) | async-done | bytes 23068688 | tf_op jit(solution)/shard_map/all_gather | solution.py:90
  1190.3 132.7 %all-gather.46.cloned.1.call-done = bf16[5632,2048]{1,0:T(8,128)(2,1)} async-done(((bf16[176,2048]{1,0:T(8,128)(2,1)}), bf16[5632,2048]{1,0:T(8,128)(2,1)}) %all-gather.46.cloned.1.call-update) | async-done | bytes 23068688 | tf_op jit(solution)/shard_map/all_gather | solution.py:92
  1339.8 128.1 %all-gather.48.cloned.1.call-done = bf16[2048,5632]{1,0:T(8,128)(2,1)} async-done(((bf16[64,5632]{1,0:T(8,128)(2,1)}), bf16[2048,5632]{1,0:T(8,128)(2,1)}) %all-gather.48.cloned.1.call-update) | async-done | bytes 23068688 | tf_op jit(solution)/shard_map/all_gather | solution.py:91
  1603.0 24.0 %all_to_all.94 = bf16[8,2,24576]{2,1,0:T(2,128)(2,1)} all-to-all(bf16[8,2,24576]{2,1,0:T(2,128)(2,1)} %reshape.677), channel_id=1, replica_groups=mesh['dp'=4,'seq'=8] {'seq'}, dimensions={0} | all-to-all | bytes 1572864 | tf_op jit(solution)/shard_map/all_to_all | solution.py:101
  1695.8 45.4 %all-gather.64.cloned.1.call-done = bf16[512,5632]{1,0:T(8,128)(2,1)} async-done(((bf16[128,5632]{1,0:T(8,128)(2,1)}), bf16[512,5632]{1,0:T(8,128)(2,1)}) %all-gather.64.cloned.1.call-update) | async-done | bytes 5767184 | tf_op jit(solution)/shard_map/all_gather | solution.py:106
  1766.0 77.7 %all-gather.62.cloned.1.call-done = bf16[512,11264]{1,0:T(8,128)(2,1)} async-done(((bf16[128,11264]{1,0:T(8,128)(2,1)}), bf16[512,11264]{1,0:T(8,128)(2,1)}) %all-gather.62.cloned.1.call-update) | async-done | bytes 11534352 | tf_op jit(solution)/shard_map/all_gather | solution.py:107
  1864.0 40.2 %all-reduce.8 = (f32[2048]{0:T(1024)S(1)}, f32[2048]{0:T(1024)S(1)}) all-reduce(f32[2048]{0:T(1024)S(1)} %get-tuple-element.33, f32[2048]{0:T(1024)S(1)} %copy-done.36), channel_id=3, replica_groups=mesh['dp'=4,'seq'=8] {'dp','seq'}, use_global_device_ids=true, to_apply=%region_19.20.clone | all-reduce | flops 4096 | bytes 32768
  1917.1 71.3 %reduce-scatter.5.cloned.1.call-done = bf16[64,2560]{1,0:T(8,128)(2,1)} async-done(((bf16[512,2560]{1,0:T(8,128)(2,1)}), bf16[64,2560]{1,0:T(8,128)(2,1)}) %reduce-scatter.5.cloned.1.call-update) | async-done | bytes 327696 | tf_op jit(solution)/shard_map/reduce_scatter | solution.py:110
  1991.5 110.0 %reduce-scatter.11.cloned.1.call-done = bf16[176,2048]{1,0:T(8,128)(2,1)} async-done(((bf16[1408,2048]{1,0:T(8,128)(2,1)}), bf16[176,2048]{1,0:T(8,128)(2,1)}) %reduce-scatter.11.cloned.1.call-update) | async-done | bytes 720912 | tf_op jit(solution)/shard_map/reduce_scatter | solution.py:110
  2103.9 193.0 %reduce-scatter.9.cloned.1.call-done = bf16[64,11264]{1,0:T(8,128)(2,1)} async-done(((bf16[512,11264]{1,0:T(8,128)(2,1)}), bf16[64,11264]{1,0:T(8,128)(2,1)}) %reduce-scatter.9.cloned.1.call-update) | async-done | bytes 1441808 | tf_op jit(solution)/shard_map/reduce_scatter | solution.py:110
  (317 shorter events, 450.3 us)
Async XLA Ops:
  7.9 112.6 %all-gather.26.cloned.1.call-start = ((), (), s32[]{:S(2)}) async-start(), calls=%async_computation.11 | async-start | bytes 1081344 | tf_op jit(solution)/shard_map/all_gather | solution.py:81
  8.7 190.7 %all-gather.24.cloned.1.call-start = ((), (), s32[]{:S(2)}) async-start(), calls=%async_computation.10 | async-start | bytes 8650752 | tf_op jit(solution)/shard_map/all_gather | solution.py:80
  9.4 289.1 %all-gather.30.cloned.1.call-start = ((), (), s32[]{:S(2)}) async-start(), calls=%async_computation.13 | async-start | bytes 8650752 | tf_op jit(solution)/shard_map/all_gather | solution.py:83
  10.0 431.1 %all-gather.32.cloned.1.call-start = ((), (), s32[]{:S(2)}) async-start(), calls=%async_computation.14 | async-start | bytes 23789568 | tf_op jit(solution)/shard_map/all_gather | solution.py:90
  10.6 575.4 %all-gather.36.cloned.1.call-start = ((), (), s32[]{:S(2)}) async-start(), calls=%async_computation.16 | async-start | bytes 23789568 | tf_op jit(solution)/shard_map/all_gather | solution.py:92
  11.1 719.8 %all-gather.34.cloned.1.call-start = ((), (), s32[]{:S(2)}) async-start(), calls=%async_computation.15 | async-start | bytes 23789568 | tf_op jit(solution)/shard_map/all_gather | solution.py:91
  276.1 527.5 %all-gather.42.cloned.1.call-start = ((), (), s32[]{:S(2)}) async-start(), calls=%async_computation.19 | async-start | bytes 1081344 | tf_op jit(solution)/shard_map/all_gather | solution.py:82
  750.4 109.0 %all-gather.40.cloned.1.call-start = ((), (), s32[]{:S(2)}) async-start(), calls=%async_computation.18 | async-start | bytes 1081344 | tf_op jit(solution)/shard_map/all_gather | solution.py:81
  751.2 186.9 %all-gather.38.cloned.1.call-start = ((), (), s32[]{:S(2)}) async-start(), calls=%async_computation.17 | async-start | bytes 8650752 | tf_op jit(solution)/shard_map/all_gather | solution.py:80
  751.8 281.7 %all-gather.44.cloned.1.call-start = ((), (), s32[]{:S(2)}) async-start(), calls=%async_computation.20 | async-start | bytes 8650752 | tf_op jit(solution)/shard_map/all_gather | solution.py:83
  752.5 425.5 %all-gather.50.cloned.1.call-start = ((), (), s32[]{:S(2)}) async-start(), calls=%async_computation.23 | async-start | bytes 23789568 | tf_op jit(solution)/shard_map/all_gather | solution.py:90
  753.1 570.0 %all-gather.46.cloned.1.call-start = ((), (), s32[]{:S(2)}) async-start(), calls=%async_computation.21 | async-start | bytes 23789568 | tf_op jit(solution)/shard_map/all_gather | solution.py:92
  753.8 714.1 %all-gather.48.cloned.1.call-start = ((), (), s32[]{:S(2)}) async-start(), calls=%async_computation.22 | async-start | bytes 23789568 | tf_op jit(solution)/shard_map/all_gather | solution.py:91
  1012.7 638.1 %all-gather.56.cloned.1.call-start = ((), (), s32[]{:S(2)}) async-start(), calls=%async_computation.27 | async-start | bytes 2621440 | tf_op jit(solution)/shard_map/all_gather | solution.py:106
  1038.4 612.4 %all-gather.58.cloned.1.call-start = ((), (), s32[]{:S(2)}) async-start(), calls=%async_computation.28 | async-start | bytes 2621440 | tf_op jit(solution)/shard_map/all_gather | solution.py:107
  1527.6 127.8 %all-gather.52.cloned.1.call-start = ((), (), s32[]{:S(2)}) async-start(), calls=%async_computation.24 | async-start | bytes 2621440 | tf_op jit(solution)/shard_map/all_gather | solution.py:106
  1528.2 143.5 %all-gather.54.cloned.1.call-start = ((), (), s32[]{:S(2)}) async-start(), calls=%async_computation.25 | async-start | bytes 3276800 | tf_op jit(solution)/shard_map/all_gather | solution.py:107
  1646.2 95.1 %all-gather.64.cloned.1.call-start = ((), (), s32[]{:S(2)}) async-start(), calls=%async_computation.33 | async-start | bytes 7208960 | tf_op jit(solution)/shard_map/all_gather | solution.py:106
  1646.8 119.2 %all-gather.60.cloned.1.call-start = ((), (), s32[]{:S(2)}) async-start(), calls=%async_computation.30 | async-start | bytes 2621440 | tf_op jit(solution)/shard_map/all_gather | solution.py:106
  1647.5 196.2 %all-gather.62.cloned.1.call-start = ((), (), s32[]{:S(2)}) async-start(), calls=%async_computation.31 | async-start | bytes 14417920 | tf_op jit(solution)/shard_map/all_gather | solution.py:107
  1650.7 264.6 %reduce-scatter.7.cloned.1.call-start = ((), (), s32[]{:S(2)}) async-start(), calls=%async_computation.29 | async-start | bytes 2359296 | tf_op jit(solution)/shard_map/reduce_scatter | solution.py:110
  1655.4 333.0 %reduce-scatter.5.cloned.1.call-start = ((), (), s32[]{:S(2)}) async-start(), calls=%async_computation.26 | async-start | bytes 2949120 | tf_op jit(solution)/shard_map/reduce_scatter | solution.py:110
  1676.7 424.9 %reduce-scatter.11.cloned.1.call-start = ((), (), s32[]{:S(2)}) async-start(), calls=%async_computation.34 | async-start | bytes 6488064 | tf_op jit(solution)/shard_map/reduce_scatter | solution.py:110
  1749.0 547.9 %reduce-scatter.9.cloned.1.call-start = ((), (), s32[]{:S(2)}) async-start(), calls=%async_computation.32 | async-start | bytes 12976128 | tf_op jit(solution)/shard_map/reduce_scatter | solution.py:110
  (54 other events, 4072.3 us)
Sparse Core Ops, SparseCore 0:
  11.1 53.6 all-gather.27
  67.8 52.7 all-gather.25
  123.5 75.8 all-gather.23
  202.2 93.7 all-gather.29
  298.8 142.2 all-gather.31
  443.9 142.0 all-gather.35
  588.9 142.0 all-gather.33
  750.6 52.9 all-gather.41
  806.7 52.6 all-gather.39
  862.2 75.8 all-gather.37
  941.1 92.1 all-gather.43
  1036.0 141.9 all-gather.49
  1180.9 142.0 all-gather.45
  1325.8 142.0 all-gather.47
  1537.3 22.5 all-gather.51
  1645.5 26.1 all-gather.53
  1673.3 22.5 all-gather.65
  1697.8 43.3 all-gather.63
  1743.4 22.5 all-gather.59
  1767.5 76.1 all-gather.61
  1847.2 68.0 reduce-scatter.6
  1918.7 69.6 reduce-scatter.4
  1992.0 109.5 reduce-scatter.10
  2105.0 191.8 reduce-scatter.8
  (2 shorter events, 44.3 us)
where the time goes:
time: 2320 us; the launch traced here: 2310 us
  waiting for transfers between devices  1740 us (75%)
  matrix products  210 us (9%)
  blocking collectives  179 us (8%)
  local copies, waits for them, and re-layouts  76.8 us (3%)
  other arithmetic  58 us (2%)
  starting transfers between devices  26.1 us (1%)
    reduce_scatter x4, waiting for transfers between devices, weight_gradient(): lax.psum_scatter(transposed_times(lax.dynamic_slice_in_dim(left_all, base...  381 us
    all_gather x2, waiting for transfers between devices, gather_feedforward(): lax.all_gather(gate_weight, ('dp', 'seq'), axis=0, tiled=True)  277 us
    all_gather x2, waiting for transfers between devices, gather_feedforward(): lax.all_gather(up_weight, ('dp', 'seq'), axis=0, tiled=True)  273 us
    all_gather x2, waiting for transfers between devices, gather_feedforward(): lax.all_gather(down_weight, ('dp', 'seq'), axis=0, tiled=True)  265 us
    all_gather x2, waiting for transfers between devices, gather_attention(): lax.all_gather(query_weight, ('dp', 'seq'), axis=0, tiled=True)  153 us
    unnamed x3, blocking collectives  121 us
    all_gather x4, waiting for transfers between devices, weight_gradient(): lax.all_gather(right_rows, 'dp', axis=0, tiled=True)  113 us
    all_gather x2, waiting for transfers between devices, gather_attention(): lax.all_gather(key_weight, ('dp', 'seq'), axis=0, tiled=True)  108 us
  transfers between devices with their start and end apart: 30, of which 25 were waited for; matrix products, arithmetic and copies ran while one was open for 14% of the time, Pallas kernels for 0%

commit v1 on v0

v1 whole, which is shorter than its diff:
```python
import jax
import jax.numpy as jnp
from jax import lax
from jax.sharding import PartitionSpec as P

H = 32
KV = 4
HEAD = 64

epsilon = 1e-05
masked = -1e30
f32 = jnp.float32
bf16 = jnp.bfloat16


def rope_tables(length):
    half_width = HEAD // 2
    frequency = 10000.0 ** (-(jnp.arange(half_width, dtype=f32) * 2.0) / HEAD)
    angles = jnp.arange(length, dtype=f32)[:, None] * frequency[None, :]
    return (jnp.cos(angles)[:, None, :], jnp.sin(angles)[:, None, :])


def rotate(values, cosine, sine):
    front, back = values[..., : HEAD // 2], values[..., HEAD // 2 :]
    return jnp.concatenate([front * cosine - back * sine, back * cosine + front * sine], axis=-1)


def rms_scale(values):
    return lax.rsqrt(jnp.mean(values * values, axis=-1, keepdims=True) + epsilon)


def mm(a, b):
    return lax.dot_general(a, b, (((1,), (0,)), ((), ())), preferred_element_type=f32)


def mm_nt(a, b):
    return lax.dot_general(a, b, (((1,), (1,)), ((), ())), preferred_element_type=f32)


def mm_tn(a, b):
    return lax.dot_general(a, b, (((0,), (0,)), ((), ())), preferred_element_type=f32)


def gather_seq(rows):
    return lax.all_gather(rows, "seq", axis=0, tiled=True)


def scatter_seq(rows):
    return lax.psum_scatter(rows, "seq", scatter_dimension=0, tiled=True).astype(f32)


def gather_dp(rows):
    return lax.all_gather(rows, "dp", axis=0, tiled=True)


def scatter_dp(rows):
    return lax.psum_scatter(rows, "dp", scatter_dimension=0, tiled=True)


def exchange_seq(pieces):
    return lax.all_to_all(pieces, "seq", split_axis=0, concat_axis=0, tiled=True)


def causal_mask(offset, block_rows, block_end):
    return jnp.arange(block_end)[None, :] <= (offset + jnp.arange(block_rows))[:, None]


def attention_forward(queries, keys, values, block_rows):
    outputs, totals = [], []
    for offset in range(0, queries.shape[1], block_rows):
        end = offset + block_rows
        scores = jnp.einsum(
            "hqd,kd->hqk", queries[:, offset:end], keys[:end], preferred_element_type=f32
        ) * HEAD ** (-0.5)
        scores = jnp.where(causal_mask(offset, block_rows, end), scores, masked)
        row_max = jnp.max(scores, axis=-1, keepdims=True)
        total = row_max + jnp.log(jnp.sum(jnp.exp(scores - row_max), axis=-1, keepdims=True))
        probs_low = jnp.exp(scores - total).astype(bf16)
        outputs.append(
            jnp.einsum("hqk,kd->hqd", probs_low, values[:end], preferred_element_type=f32).astype(
                bf16
            )
        )
        totals.append(total)
    return jnp.concatenate(outputs, axis=1), jnp.concatenate(totals, axis=1)


def attention_backward(queries, keys, values, grads, totals, block_rows):
    length = keys.shape[0]
    scale = HEAD ** (-0.5)
    key_sum = jnp.zeros((length, HEAD), f32)
    value_sum = jnp.zeros((length, HEAD), f32)
    query_parts = []
    for offset in range(0, length, block_rows):
        end = offset + block_rows
        query_block, grad_block = queries[:, offset:end], grads[:, offset:end]
        key_block, value_block = keys[:end], values[:end]
        scores = (
            jnp.einsum("hqd,kd->hqk", query_block, key_block, preferred_element_type=f32) * scale
        )
        scores = jnp.where(causal_mask(offset, block_rows, end), scores, masked)
        probs = jnp.exp(scores - totals[:, offset:end])
        probs_low = probs.astype(bf16)
        grad_probs = jnp.einsum(
            "hqd,kd->hqk", grad_block, value_block, preferred_element_type=f32
        )
        inner = jnp.sum(probs * grad_probs, axis=-1, keepdims=True)
        grad_scores = (probs * (grad_probs - inner)).astype(bf16)
        query_parts.append(
            jnp.einsum("hqk,kd->hqd", grad_scores, key_block, preferred_element_type=f32) * scale
        )
        padding = ((0, length - end), (0, 0))
        key_sum = key_sum + jnp.pad(
            jnp.einsum("hqk,hqd->kd", grad_scores, query_block, preferred_element_type=f32)
            * scale,
            padding,
        )
        value_sum = value_sum + jnp.pad(
            jnp.einsum("hqk,hqd->kd", probs_low, grad_block, preferred_element_type=f32), padding
        )
    return jnp.concatenate(query_parts, axis=1), key_sum, value_sum


def heads_first(flat, heads):
    return jnp.transpose(flat.reshape(flat.shape[0], heads, HEAD), (1, 0, 2))


def heads_last(stacked):
    return jnp.transpose(stacked, (1, 0, 2)).reshape(stacked.shape[1], -1)


def shards(
    inputs,
    attention_gain,
    query_weight,
    key_weight,
    value_weight,
    output_weight,
    feedforward_gain,
    gate_weight,
    up_weight,
    down_weight,
    cotangent,
):
    S, Dp = lax.axis_size("seq"), lax.axis_size("dp")
    sequences, tokens, width = inputs.shape
    length = tokens * S
    rows = query_weight.shape[0]
    heads = H // S
    q_cols = heads * HEAD
    repeats = S // KV
    down_rows = down_weight.shape[0]
    hidden = down_rows * Dp
    block_rows = min(length, max(512, length // 8))

    gain_one = attention_gain.astype(f32)[:, None]
    gain_two = feedforward_gain.astype(f32)[:, None]

    def folded(weight, gain):
        return (weight.astype(f32) * gain).astype(bf16)

    def per_group_kv(weight):
        return jnp.repeat(weight.reshape(rows, KV, HEAD), repeats, axis=1)

    def per_group_hidden(weight):
        return jnp.transpose(weight.reshape(rows, Dp, S, down_rows), (2, 0, 1, 3)).reshape(
            S, rows, hidden
        )

    packed = jnp.concatenate(
        [
            folded(query_weight, gain_one).reshape(rows, S, q_cols),
            per_group_kv(folded(key_weight, gain_one)),
            per_group_kv(folded(value_weight, gain_one)),
        ],
        axis=2,
    )
    packed = jnp.transpose(packed, (1, 0, 2))
    w_qkv = gather_dp(exchange_seq(packed).reshape(S * rows, q_cols + 2 * HEAD))
    forward_perm = [(Dp * s + d, d * S + s) for s in range(S) for d in range(Dp)]
    backward_perm = [(b, a) for a, b in forward_perm]
    w_o = gather_dp(lax.ppermute(output_weight, ("dp", "seq"), forward_perm))
    packed = jnp.concatenate(
        [
            per_group_hidden(folded(gate_weight, gain_two)),
            per_group_hidden(folded(up_weight, gain_two)),
        ],
        axis=2,
    )
    w_gu = gather_dp(exchange_seq(packed).reshape(S * rows, 2 * hidden))
    w_d = gather_dp(down_weight)

    flat = inputs.reshape(tokens, width).astype(f32)
    r1 = rms_scale(flat)
    s1 = flat * r1
    s1_all = gather_seq(s1.astype(bf16))
    cosine, sine = rope_tables(length)
    qkv = mm(s1_all, w_qkv)
    queries = rotate(qkv[:, :q_cols].reshape(length, heads, HEAD), cosine, sine).astype(bf16)
    queries = jnp.transpose(queries, (1, 0, 2))
    keys = rotate(qkv[:, None, q_cols : q_cols + HEAD], cosine, sine).astype(bf16)[:, 0]
    values = qkv[:, q_cols + HEAD :].astype(bf16)
    attended, totals = attention_forward(queries, keys, values, block_rows)
    attended = heads_last(attended)
    middle = flat + scatter_seq(mm(attended, w_o).astype(bf16))
    r2 = rms_scale(middle)
    s2 = middle * r2
    s2_all = gather_seq(s2.astype(bf16))
    gate_up = mm(s2_all, w_gu)
    gate, up = gate_up[:, :hidden], gate_up[:, hidden:]
    sig = jax.nn.sigmoid(gate)
    hid = (gate * sig * up).astype(bf16)
    output = (middle + scatter_seq(mm(hid, w_d).astype(bf16))).astype(bf16)

    dy = cotangent.reshape(tokens, width)
    dy_all = gather_seq(dy)
    d_hid = mm_nt(dy_all, w_d)
    d_gate = (d_hid * up * sig * (1.0 + gate * (1.0 - sig))).astype(bf16)
    d_up = (d_hid * (gate * sig)).astype(bf16)
    d_gu = jnp.concatenate([d_gate, d_up], axis=1)
    e2 = scatter_seq(mm_nt(d_gu, w_gu).astype(bf16))
    d_middle = dy.astype(f32) + r2 * (e2 - s2 * jnp.mean(e2 * s2, axis=-1, keepdims=True))
    dm_all = gather_seq(d_middle.astype(bf16))
    d_att = heads_first(mm_nt(dm_all, w_o).astype(bf16), heads)
    d_q, d_k, d_v = attention_backward(queries, keys, values, d_att, totals, block_rows)
    d_q = jnp.transpose(d_q, (1, 0, 2))
    d_qkv = jnp.concatenate(
        [
            rotate(d_q, cosine, -sine).reshape(length, q_cols).astype(bf16),
            rotate(d_k[:, None], cosine, -sine)[:, 0].astype(bf16),
            d_v.astype(bf16),
        ],
        axis=1,
    )
    e1 = scatter_seq(mm_nt(d_qkv, w_qkv).astype(bf16))
    input_grad = d_middle + r1 * (e1 - s1 * jnp.mean(e1 * s1, axis=-1, keepdims=True))

    down_grad = scatter_dp(mm_tn(hid, dy_all).astype(bf16)).astype(f32)
    g_gu = scatter_dp(mm_tn(s2_all, d_gu).astype(bf16))
    output_grad = lax.ppermute(
        scatter_dp(mm_tn(attended, dm_all).astype(bf16)), ("dp", "seq"), backward_perm
    ).astype(f32)
    g_qkv = scatter_dp(mm_tn(s1_all, d_qkv).astype(bf16))

    g_gu = exchange_seq(g_gu.reshape(S, rows, 2 * hidden)).astype(f32)
    g_qkv = exchange_seq(g_qkv.reshape(S, rows, q_cols + 2 * HEAD)).astype(f32)

    def back_hidden(part):
        return jnp.transpose(part.reshape(S, rows, Dp, down_rows), (1, 2, 0, 3)).reshape(rows, -1)

    def back_kv(part):
        part = jnp.sum(part.reshape(KV, repeats, rows, HEAD), axis=1)
        return jnp.transpose(part, (1, 0, 2)).reshape(rows, KV * HEAD)

    g_gate, g_up = back_hidden(g_gu[..., :hidden]), back_hidden(g_gu[..., hidden:])
    g_query = jnp.transpose(g_qkv[..., :q_cols], (1, 0, 2)).reshape(rows, width)
    g_key = back_kv(g_qkv[..., q_cols : q_cols + HEAD])
    g_value = back_kv(g_qkv[..., q_cols + HEAD :])

    def row_dot(weight, grad):
        return jnp.sum(weight.astype(f32) * grad, axis=1)

    gain_two_grad = row_dot(gate_weight, g_gate) + row_dot(up_weight, g_up)
    gain_one_grad = (
        row_dot(query_weight, g_query) + row_dot(key_weight, g_key) + row_dot(value_weight, g_value)
    )
    return (
        output.reshape(sequences, tokens, width),
        input_grad.reshape(sequences, tokens, width),
        gain_one_grad,
        g_query * gain_one,
        g_key * gain_one,
        g_value * gain_one,
        output_grad,
        gain_two_grad,
        g_gate * gain_two,
        g_up * gain_two,
        down_grad,
    )


def solution(mesh):
    both = ("dp", "seq")
    tok, vec, mat = P("dp", "seq", None), P(both), P(both, None)
    in_specs = (tok, vec, mat, mat, mat, mat, vec, mat, mat, mat, tok)
    out_specs = (tok, tok, vec, mat, mat, mat, mat, vec, mat, mat, mat)
    return jax.shard_map(shards, mesh=mesh, in_specs=in_specs, out_specs=out_specs, check_vma=False)
```

time: 2320 us -> 1040 us (0.45)
  waiting for transfers between devices: 1740 us -> 730 us
  matrix products: 210 us -> 106 us
  blocking collectives: 179 us -> 76.5 us
  local copies, waits for them, and re-layouts: 76.8 us -> 40.6 us
    all_gather x22 -> x8, waiting for transfers between devices: 1270 us -> 337 us  [the longest x4 278 us: gather_seq(): return lax.all_gather(rows, 'seq', axis=0, tiled=True)]
    unnamed x3 -> x0, blocking collectives: 121 us -> none
    dot_general x39 -> x24, matrix products: 210 us -> 106 us  [the longest x4 30.6 us: mm_nt(): lax.dot_general(a, b, (((1,), (1,)), ((), ())), preferred_element_type=f32)]
    all_to_all x4 -> x2, waiting for transfers between devices: 80.8 us -> 0.01 us  [exchange_seq(): lax.all_to_all(pieces, 'seq', split_axis=0, concat_axis=0, tiled=True)]
    ppermute x0 -> x2, waiting for transfers between devices: none -> 43.9 us  [the longest x1 31.6 us: shards(): lax.ppermute(scatter_dp(mm_tn(attended, dm_all).astype(bf16)), ('dp', 'se...]
    reduce_scatter x4 -> x8, waiting for transfers between devices: 381 us -> 347 us  [the longest x4 276 us: scatter_seq(): lax.psum_scatter(rows, 'seq', scatter_dimension=0, tiled=True).astype(f32)]
    dot_general x4 -> x0, local copies, waits for them, and re-layouts: 27.6 us -> none  [the longest x2 24.7 us: forward(): jnp.dot(normed_one, query_full, preferred_element_type=jnp.float32)]
    reshape x4 -> x17, local copies, waits for them, and re-layouts: 6.55 us -> 31.2 us  [the longest x4 15.6 us: back_hidden(): part.reshape(S, rows, Dp, down_rows)]
  transfers between devices with their start and end apart: 30 -> 20, of which waited for: 25 -> 17; matrix products, arithmetic and copies ran while one was open for 14% -> 14% of each run, Pallas kernels for 0% -> 0%
where the time goes in v1:
time: 1040 us; the launch traced here: 1030 us
  waiting for transfers between devices  730 us (70%)
  matrix products  106 us (10%)
  blocking collectives  76.5 us (7%)
  other arithmetic  42.7 us (4%)
  local copies, waits for them, and re-layouts  40.6 us (4%)
  starting transfers between devices  18.9 us (2%)
  between operations  15 us (1%)
    all_gather x4, waiting for transfers between devices, gather_seq(): return lax.all_gather(rows, 'seq', axis=0, tiled=True)  278 us
    reduce_scatter x4, waiting for transfers between devices, scatter_seq(): lax.psum_scatter(rows, 'seq', scatter_dimension=0, tiled=True).astype(f32)  276 us
    all_to_all x2, blocking collectives, exchange_seq(): lax.all_to_all(pieces, 'seq', split_axis=0, concat_axis=0, tiled=True)  76.5 us
    reduce_scatter x4, waiting for transfers between devices, scatter_dp(): return lax.psum_scatter(rows, 'dp', scatter_dimension=0, tiled=True)  70.5 us
    all_gather x4, waiting for transfers between devices, gather_dp(): return lax.all_gather(rows, 'dp', axis=0, tiled=True)  59 us
    ppermute x1, waiting for transfers between devices, shards(): lax.ppermute(scatter_dp(mm_tn(attended, dm_all).astype(bf16)), ('dp', 'se...  31.6 us
    dot_general x4, matrix products, mm_nt(): lax.dot_general(a, b, (((1,), (1,)), ((), ())), preferred_element_type=f32)  30.6 us
    dot_general x4, matrix products, mm(): lax.dot_general(a, b, (((1,), (0,)), ((), ())), preferred_element_type=f32)  27.6 us
  transfers between devices with their start and end apart: 20, of which 17 were waited for; matrix products, arithmetic and copies ran while one was open for 14% of the time, Pallas kernels for 0%

profile of v1, /device:TPU:26, one launch (start us, length us, event | category | flops | bytes accessed | tf_op | source)
XLA Modules:
  0.0 1029.8 jit_solution(10178664129044107614)
XLA Ops:
  10.5 15.5 %all_to_all.20 = bf16[8,64,384]{2,1,0:T(8,128)(2,1)} all-to-all(bf16[8,64,384]{2,1,0:T(8,128)(2,1)S(1)} %copy.68), channel_id=1, replica_groups=mesh['dp'=4,'seq'=8] {'seq'}, dimensions={0} | all-to-all | bytes 786432 | tf_op jit(solution)/shard_map/all_to_all | solution.py:61
  32.4 12.3 %collective-permute-done = bf16[64,2048]{1,0:T(8,128)(2,1)S(1)} collective-permute-done((bf16[64,2048]{1,0:T(8,128)(2,1)S(1)}, bf16[64,2048]{1,0:T(8,128)(2,1)S(1)}, u32[]{:S(2)}, u32[]{:S(2)}) %collective-permute-start) | collective-permute-done | bytes 262176 | tf_op jit(solution)/shard_map/ppermute | solution.py:182
  47.1 76.4 %all-gather.10.cloned.1.call-done = bf16[1024,2048]{1,0:T(8,128)(2,1)} async-done(((bf16[128,2048]{1,0:T(8,128)(2,1)}), bf16[1024,2048]{1,0:T(8,128)(2,1)}) %all-gather.10.cloned.1.call-update) | async-done | bytes 4194320 | tf_op jit(solution)/shard_map/all_gather | solution.py:45
  159.0 61.0 %all_to_all.21 = bf16[8,64,1408]{2,1,0:T(8,128)(2,1)} all-to-all(bf16[8,64,1408]{2,1,0:T(8,128)(2,1)S(1)} %pad_maximum_fusion.3), channel_id=1, replica_groups=mesh['dp'=4,'seq'=8] {'seq'}, dimensions={0} | all-to-all | bytes 2883584 | tf_op jit(solution)/shard_map/all_to_all | solution.py:61
  220.1 41.7 %reduce-scatter.9.cloned.1.call-done = bf16[128,2048]{1,0:T(8,128)(2,1)} async-done(((bf16[1024,2048]{1,0:T(8,128)(2,1)}), bf16[128,2048]{1,0:T(8,128)(2,1)}) %reduce-scatter.9.cloned.1.call-update) | async-done | bytes 524304 | tf_op jit(solution)/shard_map/reduce_scatter | solution.py:49
  266.9 39.7 %all-gather.18.cloned.1.call-done = bf16[2048,1408]{1,0:T(8,128)(2,1)} async-done(((bf16[512,1408]{1,0:T(8,128)(2,1)}), bf16[2048,1408]{1,0:T(8,128)(2,1)}) %all-gather.18.cloned.1.call-update) | async-done | bytes 5767184 | tf_op jit(solution)/shard_map/all_gather | solution.py:53
  306.6 74.8 %all-gather.16.cloned.1.call-done = bf16[1024,2048]{1,0:T(8,128)(2,1)} async-done(((bf16[128,2048]{1,0:T(8,128)(2,1)}), bf16[1024,2048]{1,0:T(8,128)(2,1)}) %all-gather.16.cloned.1.call-update) | async-done | bytes 4194320 | tf_op jit(solution)/shard_map/all_gather | solution.py:45
  381.4 11.7 %fusion.78 = f32[1024,1408]{1,0:T(8,128)} fusion(bf16[1024,2048]{1,0:T(8,128)(2,1)} %all-gather.16.cloned.1.call-done, bf16[2048,1408]{1,0:T(8,128)(2,1)} %all-gather.18.cloned.1.call-done), kind=kOutput, calls=%fused_computation.165 | convolution fusion | flops 5905580032 | bytes 15728640 | tf_op jit(solution)/shard_map/dot_general | solution.py:33
  393.1 16.0 %all-gather.20.cloned.1.call-done = bf16[704,2048]{1,0:T(8,128)(2,1)} async-done(((bf16[176,2048]{1,0:T(8,128)(2,1)}), bf16[704,2048]{1,0:T(8,128)(2,1)}) %all-gather.20.cloned.1.call-update) | async-done | bytes 2883600 | tf_op jit(solution)/shard_map/all_gather | solution.py:53
  409.1 74.4 %all-gather.24.cloned.1.call-done = bf16[1,1024,2048]{2,1,0:T(8,128)(2,1)} async-done(((bf16[1,128,2048]{2,1,0:T(8,128)(2,1)}), bf16[1,1024,2048]{2,1,0:T(8,128)(2,1)}) %all-gather.24.cloned.1.call-update) | async-done | bytes 4194320 | tf_op jit(solution)/shard_map/all_gather | solution.py:45
  483.5 10.2 multiply_convert_fusion.3
  495.4 11.0 %convolution_convert_fusion.2 = bf16[1024,2048]{1,0:T(8,128)(2,1)} fusion(bf16[2048,1408]{1,0:T(8,128)(2,1)} %all-gather.18.cloned.1.call-done, bf16[1024,704]{1,0:T(8,128)(2,1)S(1)} %get-tuple-element.14, bf16[1024,704]{1,0:T(8,128)(2,1)S(1)} %get-tuple-element.13), kind=kOutput, calls=%fused_computation.18 | convolution fusion | flops 5913444352 | bytes 12845056 | tf_op jit(solution)/shard_map/dot_general | solution.py:37
  506.4 87.2 %reduce-scatter.13.cloned.1.call-done = bf16[128,2048]{1,0:T(8,128)(2,1)} async-done(((bf16[1024,2048]{1,0:T(8,128)(2,1)}), bf16[128,2048]{1,0:T(8,128)(2,1)}) %reduce-scatter.13.cloned.1.call-update) | async-done | bytes 524304 | tf_op jit(solution)/shard_map/reduce_scatter | solution.py:49
  597.8 11.3 %convolution_convert_fusion = bf16[2048,1408]{1,0:T(8,128)(2,1)} fusion(bf16[1024,2048]{1,0:T(8,128)(2,1)} %all-gather.16.cloned.1.call-done, bf16[1024,704]{1,0:T(8,128)(2,1)} %copy-done.38, bf16[1024,704]{1,0:T(8,128)(2,1)} %copy-done.37), kind=kOutput, calls=%fused_computation.5 | convolution fusion | flops 5914230784 | bytes 12845056 | tf_op jit(solution)/shard_map/dot_general | solution.py:41
  609.2 7.5 fusion.6
  616.9 52.8 %all-gather.22.cloned.1.call-done = bf16[1024,2048]{1,0:T(8,128)(2,1)} async-done(((bf16[128,2048]{1,0:T(8,128)(2,1)}), bf16[1024,2048]{1,0:T(8,128)(2,1)}) %all-gather.22.cloned.1.call-update) | async-done | bytes 4194320 | tf_op jit(solution)/shard_map/all_gather | solution.py:45
  710.1 6.9 convolution_convert_fusion.3
  717.0 9.7 reduce-scatter.21.cloned.1.call-done
  732.7 32.6 %reduce-scatter.23.cloned.1.call-done = bf16[176,2048]{1,0:T(8,128)(2,1)} async-done(((bf16[704,2048]{1,0:T(8,128)(2,1)}), bf16[176,2048]{1,0:T(8,128)(2,1)}) %reduce-scatter.23.cloned.1.call-update) | async-done | bytes 720912 | tf_op jit(solution)/shard_map/reduce_scatter | solution.py:57
  767.7 28.2 %reduce-scatter.17.cloned.1.call-done = bf16[512,384]{1,0:T(8,128)(2,1)} async-done(((bf16[2048,384]{1,0:T(8,128)(2,1)}), bf16[512,384]{1,0:T(8,128)(2,1)}) %reduce-scatter.17.cloned.1.call-update) | async-done | bytes 393232 | tf_op jit(solution)/shard_map/reduce_scatter | solution.py:57
  795.9 6.3 all-to-all-start.2
  832.9 31.6 %collective-permute-done.1 = bf16[64,2048]{1,0:T(8,128)(2,1)S(1)} collective-permute-done((bf16[64,2048]{1,0:T(8,128)(2,1)}, bf16[64,2048]{1,0:T(8,128)(2,1)S(1)}, u32[]{:S(2)}, u32[]{:S(2)}) %collective-permute-start.1) | collective-permute-done | bytes 262176 | tf_op jit(solution)/shard_map/ppermute | solution.py:240
  871.0 57.4 %reduce-scatter.15.cloned.1.call-done = bf16[128,2048]{1,0:T(8,128)(2,1)} async-done(((bf16[1024,2048]{1,0:T(8,128)(2,1)}), bf16[128,2048]{1,0:T(8,128)(2,1)}) %reduce-scatter.15.cloned.1.call-update) | async-done | bytes 524304 | tf_op jit(solution)/shard_map/reduce_scatter | solution.py:49
  929.8 90.1 %reduce-scatter.11.cloned.1.call-done = bf16[128,2048]{1,0:T(8,128)(2,1)} async-done(((bf16[1024,2048]{1,0:T(8,128)(2,1)}), bf16[128,2048]{1,0:T(8,128)(2,1)}) %reduce-scatter.11.cloned.1.call-update) | async-done | bytes 524304 | tf_op jit(solution)/shard_map/reduce_scatter | solution.py:49
  (216 shorter events, 148.6 us)
Async XLA Ops:
  7.2 39.9 %all-gather.12.cloned.1.call-start = ((), (), s32[]{:S(2)}) async-start(), calls=%async_computation.13 | async-start | bytes 1966080 | tf_op jit(solution)/shard_map/all_gather | solution.py:53
  26.0 97.6 %all-gather.10.cloned.1.call-start = ((), (), s32[]{:S(2)}) async-start(), calls=%async_computation.12 | async-start | bytes 4718592 | tf_op jit(solution)/shard_map/all_gather | solution.py:45
  27.9 113.7 %all-gather.14.cloned.1.call-start = ((), (), s32[]{:S(2)}) async-start(), calls=%async_computation.14 | async-start | bytes 1310720 | tf_op jit(solution)/shard_map/all_gather | solution.py:53
  27.9 16.9 %collective-permute-start = (bf16[64,2048]{1,0:T(8,128)(2,1)S(1)}, bf16[64,2048]{1,0:T(8,128)(2,1)S(1)}, u32[]{:S(2)}, u32[]{:S(2)}) collective-permute-start(bf16[64,2048]{1,0:T(8,128)(2,1)S(1)} %copy-done.34), channel_id=1, source_target_pairs={{0,0},{1,8},{2,16},{3,24},{4,1},{5,9},{6,17},{7,25},{8,2},{9,10},{... | collective-permute-start | bytes 786440 | tf_op jit(solution)/shard_map/ppermute | solution.py:182
  30.8 105.1 %copy-start.10 = (pred[512,512]{0,1:T(8,128)(4,1)}, pred[512,512]{0,1:T(8,128)(4,1)S(1)}, u32[]{:S(2)}) copy-start(pred[512,512]{0,1:T(8,128)(4,1)S(1)} %iota_compare_fusion.1) | copy-start | bytes 786436
  32.1 96.7 %copy-start.17 = (f32[1024,32]{0,1:T(8,128)}, f32[1024,32]{0,1:T(8,128)S(1)}, u32[]{:S(2)}) copy-start(f32[1024,32]{0,1:T(8,128)S(1)} %get-tuple-element.44) | copy-start | bytes 393220
  45.5 216.3 %reduce-scatter.9.cloned.1.call-start = ((), (), s32[]{:S(2)}) async-start(), calls=%async_computation.15 | async-start | bytes 4718592 | tf_op jit(solution)/shard_map/reduce_scatter | solution.py:49
  146.1 160.5 %all-gather.18.cloned.1.call-start = ((), (), s32[]{:S(2)}) async-start(), calls=%async_computation.17 | async-start | bytes 7208960 | tf_op jit(solution)/shard_map/all_gather | solution.py:53
  220.0 161.4 %all-gather.16.cloned.1.call-start = ((), (), s32[]{:S(2)}) async-start(), calls=%async_computation.16 | async-start | bytes 4718592 | tf_op jit(solution)/shard_map/all_gather | solution.py:45
  265.1 144.0 %all-gather.20.cloned.1.call-start = ((), (), s32[]{:S(2)}) async-start(), calls=%async_computation.18 | async-start | bytes 3604480 | tf_op jit(solution)/shard_map/all_gather | solution.py:53
  265.8 217.7 %all-gather.24.cloned.1.call-start = ((), (), s32[]{:S(2)}) async-start(), calls=%async_computation.27 | async-start | bytes 4718592 | tf_op jit(solution)/shard_map/all_gather | solution.py:45
  266.6 327.0 %reduce-scatter.13.cloned.1.call-start = ((), (), s32[]{:S(2)}) async-start(), calls=%async_computation.20 | async-start | bytes 4718592 | tf_op jit(solution)/shard_map/reduce_scatter | solution.py:49
  506.3 163.4 %all-gather.22.cloned.1.call-start = ((), (), s32[]{:S(2)}) async-start(), calls=%async_computation.21 | async-start | bytes 4718592 | tf_op jit(solution)/shard_map/all_gather | solution.py:45
  597.3 129.4 %reduce-scatter.21.cloned.1.call-start = ((), (), s32[]{:S(2)}) async-start(), calls=%async_computation.25 | async-start | bytes 7208960 | tf_op jit(solution)/shard_map/reduce_scatter | solution.py:57
  609.1 156.2 %reduce-scatter.23.cloned.1.call-start = ((), (), s32[]{:S(2)}) async-start(), calls=%async_computation.26 | async-start | bytes 3604480 | tf_op jit(solution)/shard_map/reduce_scatter | solution.py:57
  616.7 179.2 %reduce-scatter.17.cloned.1.call-start = ((), (), s32[]{:S(2)}) async-start(), calls=%async_computation.23 | async-start | bytes 1966080 | tf_op jit(solution)/shard_map/reduce_scatter | solution.py:57
  698.3 128.3 %reduce-scatter.19.cloned.1.call-start = ((), (), s32[]{:S(2)}) async-start(), calls=%async_computation.24 | async-start | bytes 1310720 | tf_op jit(solution)/shard_map/reduce_scatter | solution.py:57
  702.8 225.7 %reduce-scatter.15.cloned.1.call-start = ((), (), s32[]{:S(2)}) async-start(), calls=%async_computation.22 | async-start | bytes 4718592 | tf_op jit(solution)/shard_map/reduce_scatter | solution.py:49
  708.7 311.2 %reduce-scatter.11.cloned.1.call-start = ((), (), s32[]{:S(2)}) async-start(), calls=%async_computation.19 | async-start | bytes 4718592 | tf_op jit(solution)/shard_map/reduce_scatter | solution.py:49
  726.7 41.0 %all-to-all-start.3 = ((bf16[8,64,1408]{2,1,0:T(8,128)(2,1)}), bf16[8,64,1408]{2,1,0:T(8,128)(2,1)S(1)}, u32[]{:S(2)}, u32[]{:S(2)}) async-start(bf16[8,64,1408]{2,1,0:T(8,128)(2,1)} %bitcast.170), calls=%async_computation.10 | async-start | bytes 2883584 | tf_op jit(solution)/shard_map/all_to_all | solution.py:61
  795.9 69.4 %all-to-all-start.2 = ((bf16[8,64,384]{2,1,0:T(8,128)(2,1)}), bf16[8,64,384]{2,1,0:T(8,128)(2,1)S(1)}, u32[]{:S(2)}, u32[]{:S(2)}) async-start(bf16[8,64,384]{2,1,0:T(8,128)(2,1)} %bitcast.187), calls=%async_computation.7 | async-start | bytes 786432 | tf_op jit(solution)/shard_map/all_to_all | solution.py:61
  826.6 37.9 %collective-permute-start.1 = (bf16[64,2048]{1,0:T(8,128)(2,1)}, bf16[64,2048]{1,0:T(8,128)(2,1)S(1)}, u32[]{:S(2)}, u32[]{:S(2)}) collective-permute-start(bf16[64,2048]{1,0:T(8,128)(2,1)} %reduce-scatter.19.cloned.1.call-done), channel_id=1, source_target_pairs={{0,0},{8,1},{16,2},{24,3},{1,4},{9,5},{17,6},{25,7},{2,8},{10,9},{... | collective-permute-start | bytes 786440 | tf_op jit(solution)/shard_map/ppermute | solution.py:240
  832.9 186.9 %copy-start.8 = (bf16[1,128,2048]{2,1,0:T(8,128)(2,1)S(1)}, bf16[1,128,2048]{2,1,0:T(8,128)(2,1)}, u32[]{:S(2)}) copy-start(bf16[1,128,2048]{2,1,0:T(8,128)(2,1)} %param.21) | copy-start | bytes 1572868
  832.9 186.9 %copy-start.9 = (bf16[128,2048]{1,0:T(8,128)(2,1)S(1)}, bf16[128,2048]{1,0:T(8,128)(2,1)}, u32[]{:S(2)}) copy-start(bf16[128,2048]{1,0:T(8,128)(2,1)} %reduce-scatter.13.cloned.1.call-done) | copy-start | bytes 1572868
  (37 other events, 646.1 us)
Sparse Core Ops, SparseCore 0:
  26.2 20.9 all-gather.11
  49.8 73.7 all-gather.9
  125.7 15.7 all-gather.13
  146.2 115.5 reduce-scatter.8
  263.2 43.3 all-gather.17
  309.1 72.2 all-gather.15
  383.0 26.1 all-gather.19
  411.2 72.2 all-gather.23
  506.5 87.0 reduce-scatter.12
  597.4 72.2 all-gather.21
  672.2 54.4 reduce-scatter.20
  729.1 36.1 reduce-scatter.22
  767.9 27.9 reduce-scatter.16
  798.9 24.7 reduce-scatter.18
  827.2 101.2 reduce-scatter.14
  931.9 87.9 reduce-scatter.10

commit v2 on v1

--- a/solution.py
+++ b/solution.py
@@ -1,6 +1,10 @@
+import functools
+
 import jax
 import jax.numpy as jnp
 from jax import lax
+from jax.experimental import pallas as pl
+from jax.experimental.pallas import tpu as pltpu
 from jax.sharding import PartitionSpec as P
 
 H = 32
@@ -41,11 +45,158 @@
     return lax.dot_general(a, b, (((0,), (0,)), ((), ())), preferred_element_type=f32)
 
 
+def seq_place():
+    me = lax.axis_index("seq")
+    return me // 2, me % 2
+
+def greet(z, y, Z):
+    barrier = pltpu.get_barrier_semaphore()
+    def hello(peer):
+        pl.semaphore_signal(barrier, inc=1, device_id={"seq": peer}, device_id_type=pl.DeviceIdType.MESH)
+    hello(z * 2 + 1 - y)
+    @pl.when(z > 0)
+    def _(): hello(z * 2 + y - 2)
+    @pl.when(z < Z - 1)
+    def _(): hello(z * 2 + y + 2)
+    pl.semaphore_wait(barrier, 1 + (z + Z - 1) // Z + (2 * Z - 2 - z) // Z)
+
+def send(src, dst, ssem, rsem, peer):
+    return pltpu.make_async_remote_copy(src_ref=src, dst_ref=dst, send_sem=ssem, recv_sem=rsem,
+        device_id={"seq": peer}, device_id_type=pl.DeviceIdType.MESH)
+
+def gather_kernel(Z, T, x_ref, out_ref, up_sem, dn_sem, y_sem, recv_sem, own_sem):
+    z, y = seq_place()
+    greet(z, y, Z)
+    def block(zz, yy):
+        return out_ref.at[pl.ds(pl.multiple_of((zz * 2 + yy) * T, T), T)]
+    def copy(src, zz, sem, peer):
+        return send(src, block(zz, y), sem.at[zz], recv_sem.at[zz * 2 + y], peer)
+    own = pltpu.make_async_copy(x_ref, block(z, y), own_sem)
+    own.start()
+    peer_y, peer_up, peer_dn = z * 2 + 1 - y, z * 2 + y + 2, z * 2 + y - 2
+    copy(x_ref, z, y_sem, peer_y).start()
+    @pl.when(z < Z - 1)
+    def _(): copy(x_ref, z, up_sem, peer_up).start()
+    @pl.when(z > 0)
+    def _(): copy(x_ref, z, dn_sem, peer_dn).start()
+    for h in range(1, Z):
+        @pl.when(z >= h)
+        def _():
+            zz = z - h
+            copy(block(zz, y), zz, y_sem, peer_y).wait_recv()
+            @pl.when(z < Z - 1)
+            def _(): copy(block(zz, y), zz, up_sem, peer_up).start()
+            copy(block(zz, y), zz, y_sem, peer_y).start()
+        @pl.when(z + h < Z)
+        def _():
+            zz = z + h
+            copy(block(zz, y), zz, y_sem, peer_y).wait_recv()
+            @pl.when(z > 0)
+            def _(): copy(block(zz, y), zz, dn_sem, peer_dn).start()
+            copy(block(zz, y), zz, y_sem, peer_y).start()
+    own.wait()
+    for zz in range(Z):
+        b = block(zz, 1 - y)
+        send(b, b, y_sem.at[zz], recv_sem.at[zz * 2 + 1 - y], peer_y).wait_recv()
+        c = copy(block(zz, y), zz, y_sem, peer_y)
+        c.wait_send()
+        @pl.when((zz <= z) & (z < Z - 1))
+        def _(): copy(block(zz, y), zz, up_sem, peer_up).wait_send()
+        @pl.when((zz >= z) & (z > 0))
+        def _(): copy(block(zz, y), zz, dn_sem, peer_dn).wait_send()
+
+def gather_line(x, cid=1):
+    S = lax.axis_size("seq"); Z = S // 2
+    T, D = x.shape
+    return pl.pallas_call(
+        functools.partial(gather_kernel, Z, T),
+        out_shape=jax.ShapeDtypeStruct((S * T, D), x.dtype),
+        in_specs=[pl.BlockSpec(memory_space=pltpu.VMEM)],
+        out_specs=pl.BlockSpec(memory_space=pl.ANY),
+        scratch_shapes=[pltpu.SemaphoreType.DMA((Z,))] * 3 + [pltpu.SemaphoreType.DMA((S,)), pltpu.SemaphoreType.DMA],
+        compiler_params=pltpu.CompilerParams(collective_id=cid, has_side_effects=True),
+        name="gather_seq",
+    )(x)
+
+def scatter_kernel(Z, T, p_ref, out_ref, ybuf, upbuf, dnbuf, upst, dnst, up_s, dn_s, y_s, up_r, dn_r, y_r):
+    z, y = seq_place()
+    greet(z, y, Z)
+    peer_y, peer_up, peer_dn = z * 2 + 1 - y, z * 2 + y + 2, z * 2 + y - 2
+    def mine(zz, yy):
+        return p_ref.at[pl.ds(pl.multiple_of((zz * 2 + yy) * T, T), T)]
+    def y_copy(zz):
+        return send(mine(zz, 1 - y), ybuf.at[zz], y_s.at[zz], y_r.at[zz], peer_y)
+    def up_copy(zz):
+        return send(upst.at[zz], upbuf.at[zz], up_s.at[zz], up_r.at[zz], peer_up)
+    def dn_copy(zz):
+        return send(dnst.at[zz], dnbuf.at[zz], dn_s.at[zz], dn_r.at[zz], peer_dn)
+    for h in range(Z - 1, 0, -1):
+        @pl.when(z + h < Z)
+        def _(): y_copy(z + h).start()
+        @pl.when(z - h >= 0)
+        def _(): y_copy(z - h).start()
+    y_copy(z).start()
+    for h in range(Z - 1, 0, -1):
+        @pl.when(z + h < Z)
+        def _():
+            d = z + h
+            y_copy(d).wait_recv()
+            upst[d] = (mine(d, y)[...].astype(f32) + ybuf[d].astype(f32)).astype(bf16)
+            @pl.when(z > 0)
+            def _():
+                up_copy(d).wait_recv()
+                upst[d] = (mine(d, y)[...].astype(f32) + ybuf[d].astype(f32) + upbuf[d].astype(f32)).astype(bf16)
+            up_copy(d).start()
+        @pl.when(z - h >= 0)
+        def _():
+            d = z - h
+            y_copy(d).wait_recv()
+            dnst[d] = (mine(d, y)[...].astype(f32) + ybuf[d].astype(f32)).astype(bf16)
+            @pl.when(z < Z - 1)
+            def _():
+                dn_copy(d).wait_recv()
+                dnst[d] = (mine(d, y)[...].astype(f32) + ybuf[d].astype(f32) + dnbuf[d].astype(f32)).astype(bf16)
+            dn_copy(d).start()
+    y_copy(z).wait_recv()
+    out_ref[...] = mine(z, y)[...].astype(f32) + ybuf[z].astype(f32)
+    @pl.when(z > 0)
+    def _():
+        up_copy(z).wait_recv()
+        out_ref[...] += upbuf[z].astype(f32)
+    @pl.when(z < Z - 1)
+    def _():
+        dn_copy(z).wait_recv()
+        out_ref[...] += dnbuf[z].astype(f32)
+    for zz in range(Z):
+        y_copy(zz).wait_send()
+        @pl.when(zz > z)
+        def _(): up_copy(zz).wait_send()
+        @pl.when(zz < z)
+        def _(): dn_copy(zz).wait_send()
+
+def scatter_line(p, cid=2):
+    S = lax.axis_size("seq"); Z = S // 2
+    L, D = p.shape; T = L // S
+    return pl.pallas_call(
+        functools.partial(scatter_kernel, Z, T),
+        out_shape=jax.ShapeDtypeStruct((T, D), f32),
+        in_specs=[pl.BlockSpec(memory_space=pltpu.VMEM)],
+        out_specs=pl.BlockSpec(memory_space=pltpu.VMEM),
+        scratch_shapes=[pltpu.VMEM((Z, T, D), bf16)] * 5 + [pltpu.SemaphoreType.DMA((Z,))] * 6,
+        compiler_params=pltpu.CompilerParams(collective_id=cid, has_side_effects=True, vmem_limit_bytes=60 << 20),
+        name="scatter_seq",
+    )(p)
+
+
 def gather_seq(rows):
+    if lax.axis_size("seq") == 8:
+        return gather_line(rows)
     return lax.all_gather(rows, "seq", axis=0, tiled=True)
 
 
 def scatter_seq(rows):
+    if lax.axis_size("seq") == 8:
+        return scatter_line(rows)
     return lax.psum_scatter(rows, "seq", scatter_dimension=0, tiled=True).astype(f32)
 
 

time: 1040 us -> 760 us (0.73)
  waiting for transfers between devices: 730 us -> 111 us
  Pallas kernels: 0 us -> 403 us
  blocking collectives: 76.5 us -> 15.5 us
    pallas_call x0 -> x8, Pallas kernels: none -> 403 us  [the longest x4 208 us: scatter_line(): pl.pallas_call(functools.partial(scatter_kernel, Z, T), out_shape=jax.Sha...]
    all_gather x4 -> x0, waiting for transfers between devices: 278 us -> none  [gather_seq(): return lax.all_gather(rows, 'seq', axis=0, tiled=True)]
    reduce_scatter x4 -> x0, waiting for transfers between devices: 276 us -> none  [scatter_seq(): lax.psum_scatter(rows, 'seq', scatter_dimension=0, tiled=True).astype(f32)]
    all_to_all x2 -> x1, blocking collectives: 76.5 us -> 15.5 us  [exchange_seq(): lax.all_to_all(pieces, 'seq', split_axis=0, concat_axis=0, tiled=True)]
    all_gather x4, waiting for transfers between devices: 59 us -> 0.06 us  [gather_dp(): return lax.all_gather(rows, 'dp', axis=0, tiled=True)]
    ppermute x1, waiting for transfers between devices: 12.3 us -> 39.8 us  [shards(): w_o = gather_dp(lax.ppermute(output_weight, ('dp', 'seq'), forward_perm))]
    reduce_scatter x4, waiting for transfers between devices: 70.5 us -> 44.6 us  [scatter_dp(): return lax.psum_scatter(rows, 'dp', scatter_dimension=0, tiled=True)]
    ppermute x1, waiting for transfers between devices: 31.6 us -> 16.7 us  [shards(): lax.ppermute(scatter_dp(mm_tn(attended, dm_all).astype(bf16)), ('dp', 'se...]
  transfers between devices with their start and end apart: 20 -> 13, of which waited for: 17 -> 5; matrix products, arithmetic and copies ran while one was open for 14% -> 13% of each run, Pallas kernels for 0% -> 41%
where the time goes in v2:
time: 760 us; the launch traced here: 749 us
  Pallas kernels  403 us (53%)
  waiting for transfers between devices  111 us (15%)
  matrix products  103 us (14%)
  other arithmetic  38.5 us (5%)
  local copies, waits for them, and re-layouts  37.5 us (5%)
  starting transfers between devices  25.9 us (3%)
  blocking collectives  15.5 us (2%)
  between operations  15.5 us (2%)
    pallas_call x4, Pallas kernels, scatter_line(): pl.pallas_call(functools.partial(scatter_kernel, Z, T), out_shape=jax.Sha...  208 us
    pallas_call x4, Pallas kernels, gather_line(): pl.pallas_call(functools.partial(gather_kernel, Z, T), out_shape=jax.Shap...  194 us
    reduce_scatter x4, waiting for transfers between devices, scatter_dp(): return lax.psum_scatter(rows, 'dp', scatter_dimension=0, tiled=True)  44.6 us
    ppermute x1, waiting for transfers between devices, shards(): w_o = gather_dp(lax.ppermute(output_weight, ('dp', 'seq'), forward_perm))  39.8 us
    dot_general x4, matrix products, mm(): lax.dot_general(a, b, (((1,), (0,)), ((), ())), preferred_element_type=f32)  28.5 us
    dot_general x4, matrix products, mm_nt(): lax.dot_general(a, b, (((1,), (1,)), ((), ())), preferred_element_type=f32)  28.2 us
    dot_general x4, matrix products, mm_tn(): lax.dot_general(a, b, (((0,), (0,)), ((), ())), preferred_element_type=f32)  26.8 us
    all_to_all x3, starting transfers between devices, exchange_seq(): lax.all_to_all(pieces, 'seq', split_axis=0, concat_axis=0, tiled=True)  18.3 us
  transfers between devices with their start and end apart: 13, of which 5 were waited for; matrix products, arithmetic and copies ran while one was open for 13% of the time, Pallas kernels for 41%

profile of v2, /device:TPU:26, one launch (start us, length us, event | category | flops | bytes accessed | tf_op | source)
XLA Modules:
  0.0 749.2 jit_solution(9805270831640662290)
XLA Ops:
  11.3 6.1 all-to-all-start
  17.4 9.0 %all-to-all-done = bf16[8,64,384]{2,1,0:T(8,128)(2,1)S(1)} async-done(((bf16[8,64,384]{2,1,0:T(8,128)(2,1)}), bf16[8,64,384]{2,1,0:T(8,128)(2,1)S(1)}, u32[]{:S(2)}, u32[]{:S(2)}) %all-to-all-start) | async-done | bytes 393248 | tf_op jit(solution)/shard_map/all_to_all | solution.py:212
  37.6 6.3 all-to-all-start.1
  47.3 39.8 %collective-permute-done = bf16[64,2048]{1,0:T(8,128)(2,1)S(1)} collective-permute-done((bf16[64,2048]{1,0:T(8,128)(2,1)S(1)}, bf16[64,2048]{1,0:T(8,128)(2,1)S(1)}, u32[]{:S(2)}, u32[]{:S(2)}) %collective-permute-start) | collective-permute-done | bytes 262176 | tf_op jit(solution)/shard_map/ppermute | solution.py:333
  91.8 50.8 %gather_seq.4 = bf16[1024,2048]{1,0:T(8,128)(2,1)} custom-call(bf16[128,2048]{1,0:T(8,128)(2,1)} %fusion.7.x_ref), custom_call_target="tpu_custom_call" | custom-call | tf_op jit(solution)/shard_map/gather_seq/pallas_call | solution.py:111
  142.5 48.3 %gather_seq.6 = bf16[1024,2048]{1,0:T(8,128)(2,1)} custom-call(bf16[128,2048]{1,0:T(8,128)(2,1)} %bitcast.161), custom_call_target="tpu_custom_call" | custom-call | tf_op jit(solution)/shard_map/gather_seq/pallas_call | solution.py:111
  206.7 4.7 convolution_convert_fusion.4.p_ref
  211.4 48.1 %scatter_seq.4 = f32[128,2048]{1,0:T(8,128)} custom-call(bf16[1024,2048]{1,0:T(8,128)(2,1)} %convolution_convert_fusion.4.p_ref), custom_call_target="tpu_custom_call" | custom-call | tf_op jit(solution)/shard_map/scatter_seq/pallas_call | solution.py:180
  263.2 48.0 %gather_seq.5 = bf16[1024,2048]{1,0:T(8,128)(2,1)} custom-call(bf16[128,2048]{1,0:T(8,128)(2,1)} %multiply_convert_fusion.5.x_ref), custom_call_target="tpu_custom_call" | custom-call | tf_op jit(solution)/shard_map/gather_seq/pallas_call | solution.py:111
  311.2 11.7 %fusion.67 = f32[1024,1408]{1,0:T(8,128)} fusion(bf16[1024,2048]{1,0:T(8,128)(2,1)} %gather_seq.5, bf16[2048,1408]{1,0:T(8,128)(2,1)} %all-gather.9.cloned.1.call-done), kind=kOutput, calls=%fused_computation.157 | convolution fusion | flops 5905580032 | bytes 15728640 | tf_op jit(solution)/shard_map/dot_general | solution.py:37
  322.9 10.3 %multiply_convert_fusion.3 = (bf16[1024,704]{1,0:T(8,128)(2,1)S(1)}, bf16[1024,704]{1,0:T(8,128)(2,1)S(1)}, bf16[1024,704]{1,0:T(8,128)(2,1)}) fusion(f32[1024,1408]{1,0:T(8,128)} %fusion.67, bf16[1024,2048]{1,0:T(8,128)(2,1)} %gather_seq.6, bf16[704,2048]{1,0:T(8,128)(2,1)} %all-gather.11.cloned.1.call-done), kind=kOutput, calls=%fused_computation.20 | convolution fusion | flops 2963603456 | bytes 17170432 | tf_op jit(solution)/shard_map/dot_general | solution.py:41
  334.8 8.3 %convolution_convert_fusion.2.p_ref = bf16[1024,2048]{1,0:T(8,128)(2,1)} fusion(bf16[2048,1408]{1,0:T(8,128)(2,1)S(1)} %copy-done.28, bf16[1024,704]{1,0:T(8,128)(2,1)S(1)} %get-tuple-element.14, bf16[1024,704]{1,0:T(8,128)(2,1)S(1)} %get-tuple-element.13), kind=kOutput, calls=%fused_computation.14 | convolution fusion | flops 5913444352 | bytes 12845056 | tf_op jit(solution)/shard_map/dot_general | solution.py:41
  343.1 49.9 %scatter_seq.6 = f32[128,2048]{1,0:T(8,128)} custom-call(bf16[1024,2048]{1,0:T(8,128)(2,1)} %convolution_convert_fusion.2.p_ref), custom_call_target="tpu_custom_call" | custom-call | tf_op jit(solution)/shard_map/scatter_seq/pallas_call | solution.py:180
  397.0 47.4 %gather_seq.7 = bf16[1024,2048]{1,0:T(8,128)(2,1)} custom-call(bf16[128,2048]{1,0:T(8,128)(2,1)} %fusion.64.x_ref), custom_call_target="tpu_custom_call" | custom-call | tf_op jit(solution)/shard_map/gather_seq/pallas_call | solution.py:111
  471.5 11.3 %convolution_convert_fusion = bf16[2048,1408]{1,0:T(8,128)(2,1)} fusion(bf16[1024,2048]{1,0:T(8,128)(2,1)} %gather_seq.5, bf16[1024,704]{1,0:T(8,128)(2,1)} %copy-done.34, bf16[1024,704]{1,0:T(8,128)(2,1)} %copy-done.33), kind=kOutput, calls=%fused_computation.5 | convolution fusion | flops 5914230784 | bytes 12845056 | tf_op jit(solution)/shard_map/dot_general | solution.py:45
  488.5 7.5 %convolution_convert_fusion.5 = bf16[704,2048]{1,0:T(8,128)(2,1)} fusion(bf16[1024,704]{1,0:T(8,128)(2,1)} %get-tuple-element.15, bf16[1024,2048]{1,0:T(8,128)(2,1)} %gather_seq.6), kind=kOutput, calls=%fused_computation.17 | convolution fusion | flops 2954231808 | bytes 8519680 | tf_op jit(solution)/shard_map/dot_general | solution.py:45
  499.0 15.5 %all_to_all.20 = bf16[8,64,384]{2,1,0:T(8,128)(2,1)S(1)} all-to-all(bf16[8,64,384]{2,1,0:T(8,128)(2,1)} %bitcast.186), channel_id=1, replica_groups=mesh['dp'=4,'seq'=8] {'seq'}, dimensions={0} | all-to-all | bytes 786432 | tf_op jit(solution)/shard_map/all_to_all | solution.py:212
  514.5 41.6 %reduce-scatter.9.cloned.1.call-done = bf16[512,1408]{1,0:T(8,128)(2,1)} async-done(((bf16[2048,1408]{1,0:T(8,128)(2,1)}), bf16[512,1408]{1,0:T(8,128)(2,1)}) %reduce-scatter.9.cloned.1.call-update) | async-done | bytes 1441808 | tf_op jit(solution)/shard_map/reduce_scatter | solution.py:208
  556.1 6.0 all-to-all-start.3
  562.2 7.7 %convolution_convert_fusion.3.p_ref = bf16[1024,2048]{1,0:T(8,128)(2,1)} fusion(bf16[1024,704]{1,0:T(8,128)(2,1)} %get-tuple-element.15, bf16[704,2048]{1,0:T(8,128)(2,1)} %all-gather.11.cloned.1.call-done), kind=kOutput, calls=%fused_computation.15 | convolution fusion | flops 2954887168 | bytes 8519680 | tf_op jit(solution)/shard_map/dot_general | solution.py:37
  569.8 59.4 %scatter_seq.5 = f32[128,2048]{1,0:T(8,128)} custom-call(bf16[1024,2048]{1,0:T(8,128)(2,1)} %convolution_convert_fusion.3.p_ref), custom_call_target="tpu_custom_call" | custom-call | tf_op jit(solution)/shard_map/scatter_seq/pallas_call | solution.py:180
  629.2 5.8 convolution_convert_fusion.1.p_ref
  635.0 50.8 %scatter_seq.7 = f32[128,2048]{1,0:T(8,128)} custom-call(bf16[1024,2048]{1,0:T(8,128)(2,1)} %convolution_convert_fusion.1.p_ref), custom_call_target="tpu_custom_call" | custom-call | tf_op jit(solution)/shard_map/scatter_seq/pallas_call | solution.py:180
  694.4 16.7 %collective-permute-done.1 = bf16[64,2048]{1,0:T(8,128)(2,1)S(1)} collective-permute-done((bf16[64,2048]{1,0:T(8,128)(2,1)}, bf16[64,2048]{1,0:T(8,128)(2,1)S(1)}, u32[]{:S(2)}, u32[]{:S(2)}) %collective-permute-start.1) | collective-permute-done | bytes 262176 | tf_op jit(solution)/shard_map/ppermute | solution.py:391
  (193 shorter events, 123.1 us)
Async XLA Ops:
  7.2 19.9 %copy-start.13 = (bf16[64,5632]{1,0:T(8,128)(2,1)S(1)}, bf16[64,5632]{1,0:T(8,128)(2,1)}, u32[]{:S(2)}) copy-start(bf16[64,5632]{1,0:T(8,128)(2,1)} %param.19) | copy-start | bytes 2162692
  7.2 19.9 %copy-start.12 = (bf16[64,5632]{1,0:T(8,128)(2,1)S(1)}, bf16[64,5632]{1,0:T(8,128)(2,1)}, u32[]{:S(2)}) copy-start(bf16[64,5632]{1,0:T(8,128)(2,1)} %param.18) | copy-start | bytes 2162692
  11.3 15.1 %all-to-all-start = ((bf16[8,64,384]{2,1,0:T(8,128)(2,1)}), bf16[8,64,384]{2,1,0:T(8,128)(2,1)S(1)}, u32[]{:S(2)}, u32[]{:S(2)}) async-start(bf16[8,64,384]{2,1,0:T(8,128)(2,1)} %copy.68), calls=%async_computation | async-start | bytes 786432 | tf_op jit(solution)/shard_map/all_to_all | solution.py:212
  17.3 173.5 %all-gather.5.cloned.1.call-start = ((), (), s32[]{:S(2)}) async-start(), calls=%async_computation.8 | async-start | bytes 1966080 | tf_op jit(solution)/shard_map/all_gather | solution.py:204
  36.1 53.6 %copy-start.4 = (bf16[1,128,2048]{2,1,0:T(8,128)(2,1)S(1)}, bf16[1,128,2048]{2,1,0:T(8,128)(2,1)}, u32[]{:S(2)}) copy-start(bf16[1,128,2048]{2,1,0:T(8,128)(2,1)} %param.11) | copy-start | bytes 1572868
  37.6 50.2 %all-to-all-start.1 = ((bf16[8,64,1408]{2,1,0:T(8,128)(2,1)}), bf16[8,64,1408]{2,1,0:T(8,128)(2,1)S(1)}, u32[]{:S(2)}, u32[]{:S(2)}) async-start(bf16[8,64,1408]{2,1,0:T(8,128)(2,1)} %pad_maximum_fusion.3), calls=%async_computation.1 | async-start | bytes 2883584 | tf_op jit(solution)/shard_map/all_to_all | solution.py:212
  43.9 162.8 %all-gather.7.cloned.1.call-start = ((), (), s32[]{:S(2)}) async-start(), calls=%async_computation.9 | async-start | bytes 1310720 | tf_op jit(solution)/shard_map/all_gather | solution.py:204
  43.9 43.2 %collective-permute-start = (bf16[64,2048]{1,0:T(8,128)(2,1)S(1)}, bf16[64,2048]{1,0:T(8,128)(2,1)S(1)}, u32[]{:S(2)}, u32[]{:S(2)}) collective-permute-start(bf16[64,2048]{1,0:T(8,128)(2,1)S(1)} %copy-done.29), channel_id=1, source_target_pairs={{0,0},{1,8},{2,16},{3,24},{4,1},{5,9},{6,17},{7,25},{8,2},{9,10},{... | collective-permute-start | bytes 786440 | tf_op jit(solution)/shard_map/ppermute | solution.py:333
  87.8 223.4 %all-gather.9.cloned.1.call-start = ((), (), s32[]{:S(2)}) async-start(), calls=%async_computation.10 | async-start | bytes 7208960 | tf_op jit(solution)/shard_map/all_gather | solution.py:204
  89.0 233.9 %all-gather.11.cloned.1.call-start = ((), (), s32[]{:S(2)}) async-start(), calls=%async_computation.11 | async-start | bytes 3604480 | tf_op jit(solution)/shard_map/all_gather | solution.py:204
  89.5 409.5 %reduce-scatter.5.cloned.1.call-start = ((), (), s32[]{:S(2)}) async-start(), calls=%async_computation.12 | async-start | bytes 1966080 | tf_op jit(solution)/shard_map/reduce_scatter | solution.py:208
  206.7 52.9 %copy-start.10 = (bf16[4,1024,64]{1,2,0:T(8,128)(2,1)}, bf16[4,1024,64]{1,2,0:T(8,128)(2,1)S(1)}, u32[]{:S(2)}) copy-start(bf16[4,1024,64]{1,2,0:T(8,128)(2,1)S(1)} %pad_maximum_fusion.5) | copy-start | bytes 1572868
  343.1 49.9 %copy-start.1 = (f32[128,2048]{1,0:T(8,128)S(1)}, f32[128,2048]{1,0:T(8,128)}, u32[]{:S(2)}) copy-start(f32[128,2048]{1,0:T(8,128)} %scatter_seq.4) | copy-start | bytes 3145732
  343.1 51.5 %copy-start.8 = (bf16[1,128,2048]{2,1,0:T(8,128)(2,1)S(1)}, bf16[1,128,2048]{2,1,0:T(8,128)(2,1)}, u32[]{:S(2)}) copy-start(bf16[1,128,2048]{2,1,0:T(8,128)(2,1)} %param.21) | copy-start | bytes 1572868
  471.5 84.7 %reduce-scatter.9.cloned.1.call-start = ((), (), s32[]{:S(2)}) async-start(), calls=%async_computation.14 | async-start | bytes 7208960 | tf_op jit(solution)/shard_map/reduce_scatter | solution.py:208
  482.8 204.5 %reduce-scatter.7.cloned.1.call-start = ((), (), s32[]{:S(2)}) async-start(), calls=%async_computation.13 | async-start | bytes 1310720 | tf_op jit(solution)/shard_map/reduce_scatter | solution.py:208
  488.3 226.8 %reduce-scatter.11.cloned.1.call-start = ((), (), s32[]{:S(2)}) async-start(), calls=%async_computation.15 | async-start | bytes 3604480 | tf_op jit(solution)/shard_map/reduce_scatter | solution.py:208
  556.1 161.3 %all-to-all-start.3 = ((bf16[8,64,1408]{2,1,0:T(8,128)(2,1)}), bf16[8,64,1408]{2,1,0:T(8,128)(2,1)}, u32[]{:S(2)}, u32[]{:S(2)}) async-start(bf16[8,64,1408]{2,1,0:T(8,128)(2,1)} %bitcast.169), calls=%async_computation.6 | async-start | bytes 2883584 | tf_op jit(solution)/shard_map/all_to_all | solution.py:212
  569.8 59.4 %copy-start.20 = (bf16[1024,64]{0,1:T(8,128)(2,1)S(1)}, bf16[1024,64]{0,1:T(8,128)(2,1)}, u32[]{:S(2)}) copy-start(bf16[1024,64]{0,1:T(8,128)(2,1)} %copy-done.19) | copy-start | bytes 393220
  569.8 59.4 %copy-start.32 = (bf16[1024,64]{0,1:T(8,128)(2,1)S(1)}, bf16[1024,64]{0,1:T(8,128)(2,1)}, u32[]{:S(2)}) copy-start(bf16[1024,64]{0,1:T(8,128)(2,1)} %copy-done.31) | copy-start | bytes 393220
  635.0 56.1 %copy-start.5 = (f32[128,2048]{1,0:T(8,128)S(1)}, f32[128,2048]{1,0:T(8,128)}, u32[]{:S(2)}) copy-start(f32[128,2048]{1,0:T(8,128)} %scatter_seq.6) | copy-start | bytes 3145732
  687.3 23.8 %collective-permute-start.1 = (bf16[64,2048]{1,0:T(8,128)(2,1)}, bf16[64,2048]{1,0:T(8,128)(2,1)S(1)}, u32[]{:S(2)}, u32[]{:S(2)}) collective-permute-start(bf16[64,2048]{1,0:T(8,128)(2,1)} %reduce-scatter.7.cloned.1.call-done), channel_id=1, source_target_pairs={{0,0},{8,1},{16,2},{24,3},{1,4},{9,5},{17,6},{25,7},{2,8},{10,9},{... | collective-permute-start | bytes 786440 | tf_op jit(solution)/shard_map/ppermute | solution.py:391
  694.4 18.3 %copy-start.25 = (f32[64]{0:T(128)S(1)}, f32[64]{0:T(128)}, u32[]{:S(2)}) copy-start(f32[64]{0:T(128)} %copy-done.24) | copy-start | bytes 772
  694.4 19.1 %copy-start.17 = (bf16[64,2048]{1,0:T(8,128)(2,1)S(1)}, bf16[64,2048]{1,0:T(8,128)(2,1)}, u32[]{:S(2)}) copy-start(bf16[64,2048]{1,0:T(8,128)(2,1)} %param.13) | copy-start | bytes 786436
  (26 other events, 136.0 us)
Sparse Core Ops, SparseCore 0:
  27.3 19.8 all-gather.4
  87.9 15.8 all-gather.6
  106.0 43.3 all-gather.8
  150.8 27.0 all-gather.10
  471.6 27.3 reduce-scatter.4
  501.4 54.7 reduce-scatter.8
  559.2 24.7 reduce-scatter.6
  586.6 36.1 reduce-scatter.10

commit v3 on v2

--- a/solution.py
+++ b/solution.py
@@ -188,6 +188,279 @@
     )(p)
 
 
+def line_rank(i, z):
+    upper = z // 2
+    inner = (z + upper) % 2
+    base = i + inner * (1 - i // 2) * (1 - 2 * i)
+    return base + upper * (3 - 2 * base)
+
+
+def above(d, z):
+    return (d - z + 3) // 4
+
+
+def rows_of(ref, start, size):
+    return ref.at[pl.ds(pl.multiple_of(start, size), size)]
+
+
+class Gather:
+    def __init__(self, z, y, T, own, full, up_sem, dn_sem, y_sem, recv_sem, own_sem):
+        self.z, self.y, self.T, self.own, self.full = z, y, T, own, full
+        self.sems = {"up": up_sem, "dn": dn_sem, "y": y_sem}
+        self.peers = {"up": z * 2 + y + 2, "dn": z * 2 + y - 2, "y": z * 2 + 1 - y}
+        self.recv_sem, self.own_sem = recv_sem, own_sem
+
+    def block(self, zz, yy):
+        return rows_of(self.full, (zz * 2 + yy) * self.T, self.T)
+
+    def copy(self, src, zz, way):
+        return send(
+            src,
+            self.block(zz, self.y),
+            self.sems[way].at[zz],
+            self.recv_sem.at[zz * 2 + self.y],
+            self.peers[way],
+        )
+
+    def start(self):
+        z = self.z
+        pltpu.make_async_copy(self.own, self.block(z, self.y), self.own_sem).start()
+        self.copy(self.own, z, "y").start()
+
+        @pl.when(z < 3)
+        def _():
+            self.copy(self.own, z, "up").start()
+
+        @pl.when(z > 0)
+        def _():
+            self.copy(self.own, z, "dn").start()
+
+    def own_ready(self):
+        pltpu.make_async_copy(self.own, self.block(self.z, self.y), self.own_sem).wait()
+
+    def hop(self, h):
+        z = self.z
+
+        @pl.when(z >= h)
+        def _():
+            src = self.block(z - h, self.y)
+            self.copy(src, z - h, "y").wait_recv()
+
+            @pl.when(z < 3)
+            def _():
+                self.copy(src, z - h, "up").start()
+
+            self.copy(src, z - h, "y").start()
+
+        @pl.when(z + h < 4)
+        def _():
+            src = self.block(z + h, self.y)
+            self.copy(src, z + h, "y").wait_recv()
+
+            @pl.when(z > 0)
+            def _():
+                self.copy(src, z + h, "dn").start()
+
+            self.copy(src, z + h, "y").start()
+
+    def pair_ready(self, zz):
+        b = self.block(zz, 1 - self.y)
+        send(
+            b, b, self.sems["y"].at[zz], self.recv_sem.at[zz * 2 + 1 - self.y], self.peers["y"]
+        ).wait_recv()
+
+    def finish(self):
+        z = self.z
+        for zz in range(4):
+            src = self.block(zz, self.y)
+            self.copy(src, zz, "y").wait_send()
+
+            @pl.when((zz <= z) & (z < 3))
+            def _():
+                self.copy(src, zz, "up").wait_send()
+
+            @pl.when((zz >= z) & (z > 0))
+            def _():
+                self.copy(src, zz, "dn").wait_send()
+
+
+class Scatter:
+    def __init__(self, z, y, T, part, ybuf, rbuf, stage, y_s, y_r, z_s, z_r):
+        self.z, self.y, self.T, self.part = z, y, T, part
+        self.ybuf, self.rbuf, self.stage = ybuf, rbuf, stage
+        self.y_s, self.y_r, self.z_s, self.z_r = y_s, y_r, z_s, z_r
+
+    def rows(self, zz, yy):
+        return rows_of(self.part, (zz * 2 + yy) * self.T, self.T)
+
+    def y_copy(self, d):
+        peer = self.z * 2 + 1 - self.y
+        return send(
+            self.rows(d, 1 - self.y), self.ybuf.at[d], self.y_s.at[d], self.y_r.at[d], peer
+        )
+
+    def z_copy(self, d, up):
+        slot = d + up
+        peer = self.z * 2 + self.y + 4 * up - 2
+        return send(self.stage.at[d], self.rbuf.at[slot], self.z_s.at[d], self.z_r.at[slot], peer)
+
+    def start(self, d):
+        self.y_copy(d).start()
+
+    def pass_on(self, d):
+        z = self.z
+        up = above(d, z)
+        self.y_copy(d).wait_recv()
+        total = self.rows(d, self.y)[...].astype(f32) + self.ybuf[d].astype(f32)
+        inner = (z > 0) & (z < 3)
+
+        @pl.when(inner)
+        def _():
+            self.z_copy(d, up).wait_recv()
+            self.stage[d] = (total + self.rbuf[d + up].astype(f32)).astype(bf16)
+
+        @pl.when(jnp.logical_not(inner))
+        def _():
+            self.stage[d] = total.astype(bf16)
+
+        self.z_copy(d, up).start()
+
+    def finish(self, out_ref):
+        z = self.z
+        self.y_copy(z).wait_recv()
+        out_ref[...] = self.rows(z, self.y)[...].astype(f32) + self.ybuf[z].astype(f32)
+
+        @pl.when(z > 0)
+        def _():
+            self.z_copy(z, 1).wait_recv()
+            out_ref[...] += self.rbuf[z + 1].astype(f32)
+
+        @pl.when(z < 3)
+        def _():
+            self.z_copy(z, 0).wait_recv()
+            out_ref[...] += self.rbuf[z].astype(f32)
+
+        for d in range(4):
+            self.y_copy(d).wait_send()
+
+            @pl.when(z != d)
+            def _():
+                self.z_copy(d, above(d, z)).wait_send()
+
+
+def line_sems(n):
+    return [pltpu.SemaphoreType.DMA((4,))] * 3 + [
+        pltpu.SemaphoreType.DMA((8,)),
+        pltpu.SemaphoreType.DMA,
+    ]
+
+
+def sum_scratch(T, width):
+    return [
+        pltpu.VMEM((4, T, width), bf16),
+        pltpu.VMEM((5, T, width), bf16),
+        pltpu.VMEM((4, T, width), bf16),
+        pltpu.SemaphoreType.DMA((4,)),
+        pltpu.SemaphoreType.DMA((4,)),
+        pltpu.SemaphoreType.DMA((4,)),
+        pltpu.SemaphoreType.DMA((5,)),
+    ]
+
+
+def feedforward_kernel(
+    T, x_ref, dy_ref, wgu_ref, wd_ref, pout_ref, e2_ref, ggu_ref, gd_ref,
+    full, hid, dgu, part, up_sem, dn_sem, ag_y, ag_r, own_sem,
+    ybuf, rbuf, stage, y_s, y_r, z_s, z_r,
+):
+    z, y = seq_place()
+    F = hid.shape[1]
+    greet(z, y, 4)
+    gather = Gather(z, y, T, x_ref, full, up_sem, dn_sem, ag_y, ag_r, own_sem)
+    scatter = Scatter(z, y, T, part, ybuf, rbuf, stage, y_s, y_r, z_s, z_r)
+    gather.start()
+    gather.own_ready()
+
+    def compute(i, carry):
+        for h in range(1, 4):
+
+            @pl.when(i == h - 1)
+            def _():
+                gather.hop(h)
+
+        zz = line_rank(i, z)
+        gather.pair_ready(zz)
+
+        @pl.when(i == 3)
+        def _():
+            scatter.start(line_rank(2, z))
+
+        r = pl.ds(pl.multiple_of(zz * 2 * T, 2 * T), 2 * T)
+        gu = mm(full[r, :], wgu_ref[...])
+        gate, up = gu[:, :F], gu[:, F:]
+        sig = 1.0 / (1.0 + jnp.exp(-gate))
+        act = gate * sig
+        h = (act * up).astype(bf16)
+        hid[r, :] = h
+        pout_ref[r, :] = mm(h, wd_ref[...]).astype(bf16)
+        dh = mm_nt(dy_ref[r, :], wd_ref[...])
+        dgu[r, :F] = (dh * up * sig * (1.0 + gate * (1.0 - sig))).astype(bf16)
+        dgu[r, F:] = (dh * act).astype(bf16)
+        part[r, :] = mm_nt(dgu[r, :], wgu_ref[...]).astype(bf16)
+        return carry
+
+    lax.fori_loop(0, 4, compute, 0)
+    for i in (3, 1, 0):
+        scatter.start(line_rank(i, z))
+
+    def gate_up_tile(i, carry):
+        r = pl.ds(pl.multiple_of(i * 256, 256), 256)
+        ggu_ref[r, :] = mm_tn(full[:, r], dgu[...]).astype(bf16)
+        return carry
+
+    def down_tile(i, carry):
+        r = pl.ds(pl.multiple_of(i * 256, 256), 256)
+        gd_ref[r, :] = mm_tn(hid[:, r], dy_ref[...]).astype(bf16)
+        return carry
+
+    lax.fori_loop(0, 4, gate_up_tile, 0)
+    scatter.pass_on(line_rank(3, z))
+    lax.fori_loop(4, 8, gate_up_tile, 0)
+    scatter.pass_on(line_rank(2, z))
+    lax.fori_loop(0, F // 256, down_tile, 0)
+    scatter.pass_on(line_rank(1, z))
+    scatter.finish(e2_ref)
+    gather.finish()
+
+
+def feedforward(x, dy_all, w_gu, w_d, cid=3):
+    T, width = x.shape
+    L, F = dy_all.shape[0], w_d.shape[0]
+    vmem = pl.BlockSpec(memory_space=pltpu.VMEM)
+    return pl.pallas_call(
+        functools.partial(feedforward_kernel, T),
+        out_shape=(
+            jax.ShapeDtypeStruct((L, width), bf16),
+            jax.ShapeDtypeStruct((T, width), f32),
+            jax.ShapeDtypeStruct((width, 2 * F), bf16),
+            jax.ShapeDtypeStruct((F, width), bf16),
+        ),
+        in_specs=[vmem] * 4,
+        out_specs=(vmem,) * 4,
+        scratch_shapes=[
+            pltpu.VMEM((L, width), bf16),
+            pltpu.VMEM((L, F), bf16),
+            pltpu.VMEM((L, 2 * F), bf16),
+            pltpu.VMEM((L, width), bf16),
+        ]
+        + line_sems(4)
+        + sum_scratch(T, width),
+        compiler_params=pltpu.CompilerParams(
+            collective_id=cid, has_side_effects=True, vmem_limit_bytes=67000000
+        ),
+        name="feedforward",
+    )(x, dy_all, w_gu, w_d)
+
+
 def gather_seq(rows):
     if lax.axis_size("seq") == 8:
         return gather_line(rows)
@@ -198,6 +471,25 @@
     if lax.axis_size("seq") == 8:
         return scatter_line(rows)
     return lax.psum_scatter(rows, "seq", scatter_dimension=0, tiled=True).astype(f32)
+
+
+def feedforward_plain(x, dy_all, w_gu, w_d):
+    hidden = w_d.shape[0]
+    s2_all = gather_seq(x)
+    gate_up = mm(s2_all, w_gu)
+    gate, up = gate_up[:, :hidden], gate_up[:, hidden:]
+    sig = jax.nn.sigmoid(gate)
+    hid = (gate * sig * up).astype(bf16)
+    d_hid = mm_nt(dy_all, w_d)
+    d_gate = (d_hid * up * sig * (1.0 + gate * (1.0 - sig))).astype(bf16)
+    d_up = (d_hid * (gate * sig)).astype(bf16)
+    d_gu = jnp.concatenate([d_gate, d_up], axis=1)
+    return (
+        mm(hid, w_d).astype(bf16),
+        scatter_seq(mm_nt(d_gu, w_gu).astype(bf16)),
+        mm_tn(s2_all, d_gu).astype(bf16),
+        mm_tn(hid, dy_all).astype(bf16),
+    )
 
 
 def gather_dp(rows):
@@ -338,8 +630,20 @@
         ],
         axis=2,
     )
-    w_gu = gather_dp(exchange_seq(packed).reshape(S * rows, 2 * hidden))
-    w_d = gather_dp(down_weight)
+    line = S == 8
+    width_f = -(-hidden // 256) * 256 if line else hidden
+
+    def padded(part, axis):
+        pads = [(0, 0)] * part.ndim
+        pads[axis] = (0, width_f - hidden)
+        return jnp.pad(part, pads)
+
+    packed = exchange_seq(packed).reshape(S * rows, 2 * hidden)
+    packed = jnp.concatenate(
+        [padded(packed[:, :hidden], 1), padded(packed[:, hidden:], 1)], axis=1
+    )
+    w_gu = gather_dp(packed)
+    w_d = padded(gather_dp(down_weight), 0)
 
     flat = inputs.reshape(tokens, width).astype(f32)
     r1 = rms_scale(flat)
@@ -356,20 +660,12 @@
     middle = flat + scatter_seq(mm(attended, w_o).astype(bf16))
     r2 = rms_scale(middle)
     s2 = middle * r2
-    s2_all = gather_seq(s2.astype(bf16))
-    gate_up = mm(s2_all, w_gu)
-    gate, up = gate_up[:, :hidden], gate_up[:, hidden:]
-    sig = jax.nn.sigmoid(gate)
-    hid = (gate * sig * up).astype(bf16)
-    output = (middle + scatter_seq(mm(hid, w_d).astype(bf16))).astype(bf16)
-
     dy = cotangent.reshape(tokens, width)
     dy_all = gather_seq(dy)
-    d_hid = mm_nt(dy_all, w_d)
-    d_gate = (d_hid * up * sig * (1.0 + gate * (1.0 - sig))).astype(bf16)
-    d_up = (d_hid * (gate * sig)).astype(bf16)
-    d_gu = jnp.concatenate([d_gate, d_up], axis=1)
-    e2 = scatter_seq(mm_nt(d_gu, w_gu).astype(bf16))
+    block = feedforward if line else feedforward_plain
+    out_part, e2, g_gu, g_down = block(s2.astype(bf16), dy_all, w_gu, w_d)
+    output = (middle + scatter_seq(out_part)).astype(bf16)
+
     d_middle = dy.astype(f32) + r2 * (e2 - s2 * jnp.mean(e2 * s2, axis=-1, keepdims=True))
     dm_all = gather_seq(d_middle.astype(bf16))
     d_att = heads_first(mm_nt(dm_all, w_o).astype(bf16), heads)
@@ -386,8 +682,9 @@
     e1 = scatter_seq(mm_nt(d_qkv, w_qkv).astype(bf16))
     input_grad = d_middle + r1 * (e1 - s1 * jnp.mean(e1 * s1, axis=-1, keepdims=True))
 
-    down_grad = scatter_dp(mm_tn(hid, dy_all).astype(bf16)).astype(f32)
-    g_gu = scatter_dp(mm_tn(s2_all, d_gu).astype(bf16))
+    down_grad = scatter_dp(g_down[:hidden]).astype(f32)
+    g_gu = scatter_dp(g_gu)
+    g_gu = jnp.concatenate([g_gu[:, :hidden], g_gu[:, width_f : width_f + hidden]], axis=1)
     output_grad = lax.ppermute(
         scatter_dp(mm_tn(attended, dm_all).astype(bf16)), ("dp", "seq"), backward_perm
     ).astype(f32)

time: 760 us -> 752 us (0.989)
  matrix products: 103 us -> 46.2 us
  blocking collectives: 15.5 us -> 51.9 us
  Pallas kernels: 403 us -> 422 us
  starting transfers between devices: 25.9 us -> 17.2 us
    pallas_call x0 -> x1, Pallas kernels: none -> 115 us  [feedforward(): pl.pallas_call(functools.partial(feedforward_kernel, T), out_shape=(jax.S...]
    pallas_call x4 -> x3, Pallas kernels: 194 us -> 143 us  [gather_line(): pl.pallas_call(functools.partial(gather_kernel, Z, T), out_shape=jax.Shap...]
    pallas_call x4 -> x3, Pallas kernels: 208 us -> 165 us  [scatter_line(): pl.pallas_call(functools.partial(scatter_kernel, Z, T), out_shape=jax.Sha...]
    all_to_all x1 -> x2, blocking collectives: 15.5 us -> 51.9 us  [exchange_seq(): lax.all_to_all(pieces, 'seq', split_axis=0, concat_axis=0, tiled=True)]
    reduce_scatter x4, waiting for transfers between devices: 44.6 us -> 75.2 us  [scatter_dp(): return lax.psum_scatter(rows, 'dp', scatter_dimension=0, tiled=True)]
    ppermute x1, waiting for transfers between devices: 39.8 us -> 14.1 us  [shards(): w_o = gather_dp(lax.ppermute(output_weight, ('dp', 'seq'), forward_perm))]
    dot_general x4 -> x2, matrix products: 28.5 us -> 9.35 us  [mm(): lax.dot_general(a, b, (((1,), (0,)), ((), ())), preferred_element_type=f32)]
    dot_general x4 -> x2, matrix products: 28.2 us -> 9.36 us  [mm_nt(): lax.dot_general(a, b, (((1,), (1,)), ((), ())), preferred_element_type=f32)]
  transfers between devices with their start and end apart: 13 -> 12, of which waited for: 5 -> 4; matrix products, arithmetic and copies ran while one was open for 13% -> 9% of each run, Pallas kernels for 41% -> 35%
where the time goes in v3:
time: 752 us; the launch traced here: 742 us
  Pallas kernels  422 us (56%)
  waiting for transfers between devices  106 us (14%)
  blocking collectives  51.9 us (7%)
  matrix products  46.2 us (6%)
  other arithmetic  43 us (6%)
  local copies, waits for them, and re-layouts  40.1 us (5%)
  starting transfers between devices  17.2 us (2%)
  between operations  15.3 us (2%)
    pallas_call x3, Pallas kernels, scatter_line(): pl.pallas_call(functools.partial(scatter_kernel, Z, T), out_shape=jax.Sha...  165 us
    pallas_call x3, Pallas kernels, gather_line(): pl.pallas_call(functools.partial(gather_kernel, Z, T), out_shape=jax.Shap...  143 us
    pallas_call x1, Pallas kernels, feedforward(): pl.pallas_call(functools.partial(feedforward_kernel, T), out_shape=(jax.S...  115 us
    reduce_scatter x4, waiting for transfers between devices, scatter_dp(): return lax.psum_scatter(rows, 'dp', scatter_dimension=0, tiled=True)  75.2 us
    all_to_all x2, blocking collectives, exchange_seq(): lax.all_to_all(pieces, 'seq', split_axis=0, concat_axis=0, tiled=True)  51.9 us
    ppermute x1, waiting for transfers between devices, shards(): lax.ppermute(scatter_dp(mm_tn(attended, dm_all).astype(bf16)), ('dp', 'se...  15.3 us
  transfers between devices with their start and end apart: 12, of which 4 were waited for; matrix products, arithmetic and copies ran while one was open for 9% of the time, Pallas kernels for 35%

profile of v3, /device:TPU:26, one launch (start us, length us, event | category | flops | bytes accessed | tf_op | source)
XLA Modules:
  0.0 741.9 jit_solution(4560991718350302657)
XLA Ops:
  10.6 15.5 %all_to_all.20 = bf16[8,64,384]{2,1,0:T(8,128)(2,1)} all-to-all(bf16[8,64,384]{2,1,0:T(8,128)(2,1)S(1)} %copy.62), channel_id=1, replica_groups=mesh['dp'=4,'seq'=8] {'seq'}, dimensions={0} | all-to-all | bytes 786432 | tf_op jit(solution)/shard_map/all_to_all | solution.py:504
  29.0 14.1 %collective-permute-done = bf16[64,2048]{1,0:T(8,128)(2,1)S(1)} collective-permute-done((bf16[64,2048]{1,0:T(8,128)(2,1)S(1)}, bf16[64,2048]{1,0:T(8,128)(2,1)S(1)}, u32[]{:S(2)}, u32[]{:S(2)}) %collective-permute-start) | collective-permute-done | bytes 262176 | tf_op jit(solution)/shard_map/ppermute | solution.py:625
  53.9 36.4 %all_to_all.21 = bf16[8,64,1408]{2,1,0:T(8,128)(2,1)S(1)} all-to-all(bf16[8,64,1408]{2,1,0:T(8,128)(2,1)S(1)} %pad_maximum_fusion), channel_id=1, replica_groups=mesh['dp'=4,'seq'=8] {'seq'}, dimensions={0} | all-to-all | bytes 2883584 | tf_op jit(solution)/shard_map/all_to_all | solution.py:504
  93.4 49.1 %gather_seq.3 = bf16[1024,2048]{1,0:T(8,128)(2,1)} custom-call(bf16[128,2048]{1,0:T(8,128)(2,1)} %fusion.8.x_ref), custom_call_target="tpu_custom_call" | custom-call | tf_op jit(solution)/shard_map/gather_seq/pallas_call | solution.py:111
  142.5 46.9 %gather_seq.4.dy_ref = bf16[1024,2048]{1,0:T(8,128)(2,1)} custom-call(bf16[128,2048]{1,0:T(8,128)(2,1)} %bitcast.148), custom_call_target="tpu_custom_call" | custom-call | tf_op jit(solution)/shard_map/gather_seq/pallas_call | solution.py:111
  191.2 4.7 fusion.66
  206.6 4.7 convolution_convert_fusion.1.p_ref
  211.2 49.2 %scatter_seq.3 = f32[128,2048]{1,0:T(8,128)} custom-call(bf16[1024,2048]{1,0:T(8,128)(2,1)} %convolution_convert_fusion.1.p_ref), custom_call_target="tpu_custom_call" | custom-call | tf_op jit(solution)/shard_map/scatter_seq/pallas_call | solution.py:180
  264.0 4.0 pad.20.wd_ref
  268.0 114.6 %feedforward.1 = (bf16[1024,2048]{1,0:T(8,128)(2,1)}, f32[128,2048]{1,0:T(8,128)}, bf16[2048,1536]{1,0:T(8,128)(2,1)}, bf16[768,2048]{1,0:T(8,128)(2,1)}) custom-call(bf16[128,2048]{1,0:T(8,128)(2,1)} %multiply_convert_fusion.2.x_ref, bf16[1024,2048]{1,0:T(8,128)(2,1)} %gather_seq.4.dy_ref, bf16[2048,1536]{1,0:T(8,128)(2,1)} %all-gather.9.cloned.1.call-done.wgu_ref, ...), custom_call_target="tpu_custom_call" | custom-call | tf_op jit(solution)/shard_map/feedforward/pallas_call | solution.py:439
  387.7 46.8 %gather_seq.5 = bf16[1024,2048]{1,0:T(8,128)(2,1)} custom-call(bf16[128,2048]{1,0:T(8,128)(2,1)} %fusion.63.x_ref), custom_call_target="tpu_custom_call" | custom-call | tf_op jit(solution)/shard_map/gather_seq/pallas_call | solution.py:111
  444.5 3.8 multiply_reduce_fusion
  457.7 3.7 convolution_convert_fusion.2
  462.5 4.4 convolution_convert_fusion.3
  466.9 3.8 slice.118
  470.8 19.9 %reduce-scatter.5.cloned.1.call-done = bf16[512,384]{1,0:T(8,128)(2,1)} async-done(((bf16[2048,384]{1,0:T(8,128)(2,1)}), bf16[512,384]{1,0:T(8,128)(2,1)}) %reduce-scatter.5.cloned.1.call-update) | async-done | bytes 393232 | tf_op jit(solution)/shard_map/reduce_scatter | solution.py:500
  490.7 6.0 all-to-all-start.2
  496.7 55.3 %reduce-scatter.9.cloned.1.call-done = bf16[512,1536]{1,0:T(8,128)(2,1)} async-done(((bf16[2048,1536]{1,0:T(8,128)(2,1)}), bf16[512,1536]{1,0:T(8,128)(2,1)}) %reduce-scatter.9.cloned.1.call-update) | async-done | bytes 1572880 | tf_op jit(solution)/shard_map/reduce_scatter | solution.py:500
  555.7 6.0 all-to-all-start.3
  561.7 63.7 %scatter_seq.4 = f32[128,2048]{1,0:T(8,128)} custom-call(bf16[1024,2048]{1,0:T(8,128)(2,1)} %get-tuple-element.15.p_ref), custom_call_target="tpu_custom_call" | custom-call | tf_op jit(solution)/shard_map/scatter_seq/pallas_call | solution.py:180
  625.4 5.7 convolution_convert_fusion.p_ref
  631.1 52.0 %scatter_seq.5 = f32[128,2048]{1,0:T(8,128)} custom-call(bf16[1024,2048]{1,0:T(8,128)(2,1)} %convolution_convert_fusion.p_ref), custom_call_target="tpu_custom_call" | custom-call | tf_op jit(solution)/shard_map/scatter_seq/pallas_call | solution.py:180
  687.2 3.6 fusion.23
  690.9 15.3 %collective-permute-done.1 = bf16[64,2048]{1,0:T(8,128)(2,1)S(1)} collective-permute-done((bf16[64,2048]{1,0:T(8,128)(2,1)}, bf16[64,2048]{1,0:T(8,128)(2,1)S(1)}, u32[]{:S(2)}, u32[]{:S(2)}) %collective-permute-start.1) | collective-permute-done | bytes 262176 | tf_op jit(solution)/shard_map/ppermute | solution.py:688
  (196 shorter events, 97.5 us)
Async XLA Ops:
  7.2 19.0 %copy-start.35 = (bf16[64,2048]{1,0:T(8,128)(2,1)S(1)}, bf16[64,2048]{1,0:T(8,128)(2,1)}, u32[]{:S(2)}) copy-start(bf16[64,2048]{1,0:T(8,128)(2,1)} %param.16) | copy-start | bytes 786436
  7.2 37.4 %copy-start.36 = (bf16[64]{0:T(256)(128)(2,1)S(1)}, bf16[64]{0:T(256)(128)(2,1)}, u32[]{:S(2)}) copy-start(bf16[64]{0:T(256)(128)(2,1)} %param.17) | copy-start | bytes 388
  7.2 37.4 %copy-start.15 = (bf16[64,5632]{1,0:T(8,128)(2,1)S(1)}, bf16[64,5632]{1,0:T(8,128)(2,1)}, u32[]{:S(2)}) copy-start(bf16[64,5632]{1,0:T(8,128)(2,1)} %param.19) | copy-start | bytes 2162692
  7.2 37.4 %copy-start.14 = (bf16[64,5632]{1,0:T(8,128)(2,1)S(1)}, bf16[64,5632]{1,0:T(8,128)(2,1)}, u32[]{:S(2)}) copy-start(bf16[64,5632]{1,0:T(8,128)(2,1)} %param.18) | copy-start | bytes 2162692
  7.2 183.9 %all-gather.5.cloned.1.call-start = ((), (), s32[]{:S(2)}) async-start(), calls=%async_computation.8 | async-start | bytes 1966080 | tf_op jit(solution)/shard_map/all_gather | solution.py:496
  26.1 180.4 %all-gather.7.cloned.1.call-start = ((), (), s32[]{:S(2)}) async-start(), calls=%async_computation.9 | async-start | bytes 1310720 | tf_op jit(solution)/shard_map/all_gather | solution.py:496
  26.2 16.9 %collective-permute-start = (bf16[64,2048]{1,0:T(8,128)(2,1)S(1)}, bf16[64,2048]{1,0:T(8,128)(2,1)S(1)}, u32[]{:S(2)}, u32[]{:S(2)}) collective-permute-start(bf16[64,2048]{1,0:T(8,128)(2,1)S(1)} %copy-done.35), channel_id=1, source_target_pairs={{0,0},{1,8},{2,16},{3,24},{4,1},{5,9},{6,17},{7,25},{8,2},{9,10},{... | collective-permute-start | bytes 786440 | tf_op jit(solution)/shard_map/ppermute | solution.py:625
  43.8 220.3 %all-gather.11.cloned.1.call-start = ((), (), s32[]{:S(2)}) async-start(), calls=%async_computation.11 | async-start | bytes 3604480 | tf_op jit(solution)/shard_map/all_gather | solution.py:496
  44.5 223.5 %all-gather.9.cloned.1.call-start = ((), (), s32[]{:S(2)}) async-start(), calls=%async_computation.10 | async-start | bytes 7864320 | tf_op jit(solution)/shard_map/all_gather | solution.py:496
  53.5 37.3 %copy-start.34 = (pred[768]{0:T(1024)(128)(4,1)S(1)}, pred[768]{0:T(1024)(128)(4,1)}, u32[]{:S(2)}) copy-start(pred[768]{0:T(1024)(128)(4,1)} %constant.33.clone.1) | copy-start | bytes 2308
  92.2 398.5 %reduce-scatter.5.cloned.1.call-start = ((), (), s32[]{:S(2)}) async-start(), calls=%async_computation.12 | async-start | bytes 1966080 | tf_op jit(solution)/shard_map/reduce_scatter | solution.py:500
  206.5 53.9 %copy-start.12 = (bf16[4,1024,64]{1,2,0:T(8,128)(2,1)}, bf16[4,1024,64]{1,2,0:T(8,128)(2,1)S(1)}, u32[]{:S(2)}) copy-start(bf16[4,1024,64]{1,2,0:T(8,128)(2,1)S(1)} %pad_maximum_fusion.3) | copy-start | bytes 1572868
  384.6 49.9 %copy-start.33 = (f32[128]{0:T(128)}, f32[128]{0:T(128)S(1)}, u32[]{:S(2)}) copy-start(f32[128]{0:T(128)S(1)} %broadcast_multiply_fusion.6) | copy-start | bytes 1540
  384.6 49.9 %copy-start.23 = (bf16[256,2048]{1,0:T(8,128)(2,1)S(1)}, bf16[256,2048]{1,0:T(8,128)(2,1)}, u32[]{:S(2)}) copy-start(bf16[256,2048]{1,0:T(8,128)(2,1)} %all-gather.7.cloned.1.call-done) | copy-start | bytes 3145732
  461.4 90.5 %reduce-scatter.9.cloned.1.call-start = ((), (), s32[]{:S(2)}) async-start(), calls=%async_computation.14 | async-start | bytes 7864320 | tf_op jit(solution)/shard_map/reduce_scatter | solution.py:500
  462.0 223.1 %reduce-scatter.7.cloned.1.call-start = ((), (), s32[]{:S(2)}) async-start(), calls=%async_computation.13 | async-start | bytes 1310720 | tf_op jit(solution)/shard_map/reduce_scatter | solution.py:500
  466.9 243.3 %reduce-scatter.11.cloned.1.call-start = ((), (), s32[]{:S(2)}) async-start(), calls=%async_computation.15 | async-start | bytes 3604480 | tf_op jit(solution)/shard_map/reduce_scatter | solution.py:500
  490.7 64.3 %all-to-all-start.2 = ((bf16[8,64,384]{2,1,0:T(8,128)(2,1)}), bf16[8,64,384]{2,1,0:T(8,128)(2,1)S(1)}, u32[]{:S(2)}, u32[]{:S(2)}) async-start(bf16[8,64,384]{2,1,0:T(8,128)(2,1)} %bitcast.172), calls=%async_computation.3 | async-start | bytes 786432 | tf_op jit(solution)/shard_map/all_to_all | solution.py:504
  555.7 156.8 %all-to-all-start.3 = ((bf16[8,64,1408]{2,1,0:T(8,128)(2,1)}), bf16[8,64,1408]{2,1,0:T(8,128)(2,1)S(1)}, u32[]{:S(2)}, u32[]{:S(2)}) async-start(bf16[8,64,1408]{2,1,0:T(8,128)(2,1)} %bitcast.42), calls=%async_computation.6 | async-start | bytes 2883584 | tf_op jit(solution)/shard_map/all_to_all | solution.py:504
  631.1 52.0 %copy-start.5 = (bf16[1,128,2048]{2,1,0:T(8,128)(2,1)S(1)}, bf16[1,128,2048]{2,1,0:T(8,128)(2,1)}, u32[]{:S(2)}) copy-start(bf16[1,128,2048]{2,1,0:T(8,128)(2,1)} %param.11) | copy-start | bytes 1572868
  631.1 56.1 %copy-start.1 = (f32[128,2048]{1,0:T(8,128)S(1)}, f32[128,2048]{1,0:T(8,128)}, u32[]{:S(2)}) copy-start(f32[128,2048]{1,0:T(8,128)} %scatter_seq.3) | copy-start | bytes 3145732
  631.1 56.1 %copy-start.8 = (bf16[1,128,2048]{2,1,0:T(8,128)(2,1)S(1)}, bf16[1,128,2048]{2,1,0:T(8,128)(2,1)}, u32[]{:S(2)}) copy-start(bf16[1,128,2048]{2,1,0:T(8,128)(2,1)} %param.21) | copy-start | bytes 1572868
  685.2 21.9 %copy-start.19 = (bf16[8,64,384]{2,1,0:T(8,128)(2,1)S(1)}, bf16[8,64,384]{2,1,0:T(8,128)(2,1)}, u32[]{:S(2)}) copy-start(bf16[8,64,384]{2,1,0:T(8,128)(2,1)} %copy-done.18) | copy-start | bytes 1179652
  685.2 21.0 %collective-permute-start.1 = (bf16[64,2048]{1,0:T(8,128)(2,1)}, bf16[64,2048]{1,0:T(8,128)(2,1)S(1)}, u32[]{:S(2)}, u32[]{:S(2)}) collective-permute-start(bf16[64,2048]{1,0:T(8,128)(2,1)} %reduce-scatter.7.cloned.1.call-done), channel_id=1, source_target_pairs={{0,0},{8,1},{16,2},{24,3},{1,4},{9,5},{17,6},{25,7},{2,8},{10,9},{... | collective-permute-start | bytes 786440 | tf_op jit(solution)/shard_map/ppermute | solution.py:688
  (27 other events, 137.4 us)
Sparse Core Ops, SparseCore 0:
  26.2 19.3 all-gather.4
  47.8 17.9 all-gather.6
  67.3 27.0 all-gather.10
  95.8 46.3 all-gather.8
  461.6 29.0 reduce-scatter.4
  493.0 58.8 reduce-scatter.8
  555.0 24.7 reduce-scatter.6
  582.4 36.1 reduce-scatter.10

commit v4 on v3

--- a/solution.py
+++ b/solution.py
@@ -49,20 +49,42 @@
     me = lax.axis_index("seq")
     return me // 2, me % 2
 
-def greet(z, y, Z):
+def hello(barrier, peer, axis):
+    pl.semaphore_signal(
+        barrier, inc=1, device_id={axis: peer}, device_id_type=pl.DeviceIdType.MESH
+    )
+
+
+def greet(z, y, Z, dp=None):
     barrier = pltpu.get_barrier_semaphore()
-    def hello(peer):
-        pl.semaphore_signal(barrier, inc=1, device_id={"seq": peer}, device_id_type=pl.DeviceIdType.MESH)
-    hello(z * 2 + 1 - y)
+    hello(barrier, z * 2 + 1 - y, "seq")
+
     @pl.when(z > 0)
-    def _(): hello(z * 2 + y - 2)
+    def _():
+        hello(barrier, z * 2 + y - 2, "seq")
+
     @pl.when(z < Z - 1)
-    def _(): hello(z * 2 + y + 2)
-    pl.semaphore_wait(barrier, 1 + (z + Z - 1) // Z + (2 * Z - 2 - z) // Z)
-
-def send(src, dst, ssem, rsem, peer):
-    return pltpu.make_async_remote_copy(src_ref=src, dst_ref=dst, send_sem=ssem, recv_sem=rsem,
-        device_id={"seq": peer}, device_id_type=pl.DeviceIdType.MESH)
+    def _():
+        hello(barrier, z * 2 + y + 2, "seq")
+
+    count = 1 + (z + Z - 1) // Z + (2 * Z - 2 - z) // Z
+    if dp is not None:
+        hello(barrier, dp + 1 - 2 * (dp % 2), "dp")
+        hello(barrier, dp + 2 - 4 * (dp // 2), "dp")
+        count = count + 2
+    pl.semaphore_wait(barrier, count)
+
+
+def send(src, dst, ssem, rsem, peer, axis="seq"):
+    return pltpu.make_async_remote_copy(
+        src_ref=src,
+        dst_ref=dst,
+        send_sem=ssem,
+        recv_sem=rsem,
+        device_id={axis: peer},
+        device_id_type=pl.DeviceIdType.MESH,
+    )
+
 
 def gather_kernel(Z, T, x_ref, out_ref, up_sem, dn_sem, y_sem, recv_sem, own_sem):
     z, y = seq_place()
@@ -203,6 +225,14 @@
     return ref.at[pl.ds(pl.multiple_of(start, size), size)]
 
 
+def in_chunks(rows, chunk, step):
+    def body(i, carry):
+        step(pl.ds(pl.multiple_of(i * chunk, chunk), chunk))
+        return carry
+
+    lax.fori_loop(0, rows // chunk, body, 0)
+
+
 class Gather:
     def __init__(self, z, y, T, own, full, up_sem, dn_sem, y_sem, recv_sem, own_sem):
         self.z, self.y, self.T, self.own, self.full = z, y, T, own, full
@@ -285,9 +315,9 @@
 
 
 class Scatter:
-    def __init__(self, z, y, T, part, ybuf, rbuf, stage, y_s, y_r, z_s, z_r):
+    def __init__(self, z, y, T, part, ybuf, rbuf, y_s, y_r, z_s, z_r):
         self.z, self.y, self.T, self.part = z, y, T, part
-        self.ybuf, self.rbuf, self.stage = ybuf, rbuf, stage
+        self.ybuf, self.rbuf = ybuf, rbuf
         self.y_s, self.y_r, self.z_s, self.z_r = y_s, y_r, z_s, z_r
 
     def rows(self, zz, yy):
@@ -302,7 +332,7 @@
     def z_copy(self, d, up):
         slot = d + up
         peer = self.z * 2 + self.y + 4 * up - 2
-        return send(self.stage.at[d], self.rbuf.at[slot], self.z_s.at[d], self.z_r.at[slot], peer)
+        return send(self.ybuf.at[d], self.rbuf.at[slot], self.z_s.at[d], self.z_r.at[slot], peer)
 
     def start(self, d):
         self.y_copy(d).start()
@@ -311,34 +341,55 @@
         z = self.z
         up = above(d, z)
         self.y_copy(d).wait_recv()
-        total = self.rows(d, self.y)[...].astype(f32) + self.ybuf[d].astype(f32)
+        mine, slot = self.rows(d, self.y), self.ybuf.at[d]
         inner = (z > 0) & (z < 3)
 
         @pl.when(inner)
         def _():
             self.z_copy(d, up).wait_recv()
-            self.stage[d] = (total + self.rbuf[d + up].astype(f32)).astype(bf16)
+            far = self.rbuf.at[d + up]
+
+            def step(c):
+                slot[c] = (
+                    mine[c].astype(f32) + slot[c].astype(f32) + far[c].astype(f32)
+                ).astype(bf16)
+
+            in_chunks(self.T, 32, step)
 
         @pl.when(jnp.logical_not(inner))
         def _():
-            self.stage[d] = total.astype(bf16)
+            def step(c):
+                slot[c] = (mine[c].astype(f32) + slot[c].astype(f32)).astype(bf16)
+
+            in_chunks(self.T, 32, step)
 
         self.z_copy(d, up).start()
 
     def finish(self, out_ref):
         z = self.z
         self.y_copy(z).wait_recv()
-        out_ref[...] = self.rows(z, self.y)[...].astype(f32) + self.ybuf[z].astype(f32)
+        mine, slot = self.rows(z, self.y), self.ybuf.at[z]
+
+        def first(c):
+            out_ref[c] = mine[c].astype(f32) + slot[c].astype(f32)
+
+        in_chunks(self.T, 32, first)
+
+        def more(slot):
+            def step(c):
+                out_ref[c] += slot[c].astype(f32)
+
+            in_chunks(self.T, 32, step)
 
         @pl.when(z > 0)
         def _():
             self.z_copy(z, 1).wait_recv()
-            out_ref[...] += self.rbuf[z + 1].astype(f32)
+            more(self.rbuf.at[z + 1])
 
         @pl.when(z < 3)
         def _():
             self.z_copy(z, 0).wait_recv()
-            out_ref[...] += self.rbuf[z].astype(f32)
+            more(self.rbuf.at[z])
 
         for d in range(4):
             self.y_copy(d).wait_send()
@@ -359,7 +410,6 @@
     return [
         pltpu.VMEM((4, T, width), bf16),
         pltpu.VMEM((5, T, width), bf16),
-        pltpu.VMEM((4, T, width), bf16),
         pltpu.SemaphoreType.DMA((4,)),
         pltpu.SemaphoreType.DMA((4,)),
         pltpu.SemaphoreType.DMA((4,)),
@@ -367,16 +417,88 @@
     ]
 
 
+class DpSum:
+    def __init__(self, src, size, abuf, bbuf, a_s, a_r, b_s, b_r):
+        dp = lax.axis_index("dp")
+        self.core, self.far = dp % 2, dp // 2
+        self.partner, self.across = dp + 1 - 2 * (dp % 2), dp + 2 - 4 * (dp // 2)
+        self.src, self.size = src, size
+        self.abuf, self.bbuf = abuf, bbuf
+        self.a_s, self.a_r, self.b_s, self.b_r = a_s, a_r, b_s, b_r
+
+    def rows(self, d):
+        return rows_of(self.src, d * self.size, self.size)
+
+    def a_copy(self, j):
+        return send(
+            self.rows(2 * j + 1 - self.core),
+            self.abuf.at[j],
+            self.a_s.at[j],
+            self.a_r.at[j],
+            self.partner,
+            "dp",
+        )
+
+    def b_copy(self):
+        return send(self.abuf.at[1 - self.far], self.bbuf, self.b_s, self.b_r, self.across, "dp")
+
+    def start(self):
+        self.a_copy(0).start()
+        self.a_copy(1).start()
+
+    def middle(self):
+        self.a_copy(0).wait_recv()
+        self.a_copy(1).wait_recv()
+        j = 1 - self.far
+        mine, slot = self.rows(2 * j + self.core), self.abuf.at[j]
+
+        def step(c):
+            slot[c] = (mine[c].astype(f32) + slot[c].astype(f32)).astype(bf16)
+
+        in_chunks(self.size, 16, step)
+        self.b_copy().start()
+
+    def finish(self, out_ref):
+        self.b_copy().wait_recv()
+        mine, slot = self.rows(2 * self.far + self.core), self.abuf.at[self.far]
+
+        def step(c):
+            out_ref[c] = (
+                mine[c].astype(f32) + slot[c].astype(f32) + self.bbuf[c].astype(f32)
+            ).astype(out_ref.dtype)
+
+        in_chunks(self.size, 16, step)
+        self.a_copy(0).wait_send()
+        self.a_copy(1).wait_send()
+        self.b_copy().wait_send()
+
+
+def dp_scratch(size, width):
+    return [
+        pltpu.VMEM((2, size, width), bf16),
+        pltpu.VMEM((size, width), bf16),
+        pltpu.SemaphoreType.DMA((2,)),
+        pltpu.SemaphoreType.DMA((2,)),
+        pltpu.SemaphoreType.DMA,
+        pltpu.SemaphoreType.DMA,
+    ]
+
+
 def feedforward_kernel(
     T, x_ref, dy_ref, wgu_ref, wd_ref, pout_ref, e2_ref, ggu_ref, gd_ref,
-    full, hid, dgu, part, up_sem, dn_sem, ag_y, ag_r, own_sem,
-    ybuf, rbuf, stage, y_s, y_r, z_s, z_r,
+    full, hid, dgu, part, ggu, gdown, up_sem, dn_sem, ag_y, ag_r, own_sem,
+    ybuf, rbuf, y_s, y_r, z_s, z_r,
+    ga, gb, ga_s, ga_r, gb_s, gb_r,
+    da, db, da_s, da_r, db_s, db_r,
 ):
     z, y = seq_place()
+    dp = lax.axis_index("dp")
     F = hid.shape[1]
-    greet(z, y, 4)
+    greet(z, y, 4, dp)
     gather = Gather(z, y, T, x_ref, full, up_sem, dn_sem, ag_y, ag_r, own_sem)
-    scatter = Scatter(z, y, T, part, ybuf, rbuf, stage, y_s, y_r, z_s, z_r)
+    scatter = Scatter(z, y, T, part, ybuf, rbuf, y_s, y_r, z_s, z_r)
+    sum_gu = DpSum(ggu, ggu.shape[0] // 4, ga, gb, ga_s, ga_r, gb_s, gb_r)
+    sum_down = DpSum(gdown, gd_ref.shape[0], da, db, da_s, da_r, db_s, db_r)
     gather.start()
     gather.own_ready()
 
@@ -414,25 +536,30 @@
 
     def gate_up_tile(i, carry):
         r = pl.ds(pl.multiple_of(i * 256, 256), 256)
-        ggu_ref[r, :] = mm_tn(full[:, r], dgu[...]).astype(bf16)
+        ggu[r, :] = mm_tn(full[:, r], dgu[...]).astype(bf16)
         return carry
 
     def down_tile(i, carry):
         r = pl.ds(pl.multiple_of(i * 256, 256), 256)
-        gd_ref[r, :] = mm_tn(hid[:, r], dy_ref[...]).astype(bf16)
+        gdown[r, :] = mm_tn(hid[:, r], dy_ref[...]).astype(bf16)
         return carry
 
-    lax.fori_loop(0, 4, gate_up_tile, 0)
+    lax.fori_loop(0, 8, gate_up_tile, 0)
+    sum_gu.start()
     scatter.pass_on(line_rank(3, z))
-    lax.fori_loop(4, 8, gate_up_tile, 0)
+    lax.fori_loop(0, F // 256, down_tile, 0)
+    sum_down.start()
+    sum_gu.middle()
     scatter.pass_on(line_rank(2, z))
-    lax.fori_loop(0, F // 256, down_tile, 0)
+    sum_down.middle()
     scatter.pass_on(line_rank(1, z))
+    sum_gu.finish(ggu_ref)
+    sum_down.finish(gd_ref)
     scatter.finish(e2_ref)
     gather.finish()
 
 
-def feedforward(x, dy_all, w_gu, w_d, cid=3):
+def feedforward(x, dy_all, w_gu, w_d, down_rows, cid=3):
     T, width = x.shape
     L, F = dy_all.shape[0], w_d.shape[0]
     vmem = pl.BlockSpec(memory_space=pltpu.VMEM)
@@ -441,8 +568,8 @@
         out_shape=(
             jax.ShapeDtypeStruct((L, width), bf16),
             jax.ShapeDtypeStruct((T, width), f32),
-            jax.ShapeDtypeStruct((width, 2 * F), bf16),
-            jax.ShapeDtypeStruct((F, width), bf16),
+            jax.ShapeDtypeStruct((width // 4, 2 * F), bf16),
+            jax.ShapeDtypeStruct((down_rows, width), f32),
         ),
         in_specs=[vmem] * 4,
         out_specs=(vmem,) * 4,
@@ -451,14 +578,241 @@
             pltpu.VMEM((L, F), bf16),
             pltpu.VMEM((L, 2 * F), bf16),
             pltpu.VMEM((L, width), bf16),
+            pltpu.VMEM((width, 2 * F), bf16),
+            pltpu.VMEM((F, width), bf16),
         ]
         + line_sems(4)
-        + sum_scratch(T, width),
+        + sum_scratch(T, width)
+        + dp_scratch(width // 4, 2 * F)
+        + dp_scratch(down_rows, width),
         compiler_params=pltpu.CompilerParams(
             collective_id=cid, has_side_effects=True, vmem_limit_bytes=67000000
         ),
         name="feedforward",
     )(x, dy_all, w_gu, w_d)
+
+
+def attention_back_kernel(
+    T, heads, dm_ref, q_ref, k_ref, kz_ref, vz_ref, lse_ref, att_ref, s1_ref, wqkv_ref, wo_ref, table_ref,
+    e1_ref, got_ref, go_ref,
+    full, grads, probs, dprobs, dk, dv, dqkv, part, gqkv, go_part, gsum,
+    up_sem, dn_sem, ag_y, ag_r, own_sem,
+    ybuf, rbuf, y_s, y_r, z_s, z_r,
+    qa, qb, qa_s, qa_r, qb_s, qb_r,
+    oa, ob, oa_s, oa_r, ob_s, ob_r,
+    ex_s, ex_r, ex_own,
+):
+    z, y = seq_place()
+    me = z * 2 + y
+    dp = lax.axis_index("dp")
+    rows = got_ref.shape[1]
+    barrier = pltpu.get_barrier_semaphore()
+    for step in range(1, 8):
+        hello(barrier, (me + step) % 8, "seq")
+    hello(barrier, dp + 1 - 2 * (dp % 2), "dp")
+    hello(barrier, dp + 2 - 4 * (dp // 2), "dp")
+    pl.semaphore_wait(barrier, 9)
+    gather = Gather(z, y, T, dm_ref, full, up_sem, dn_sem, ag_y, ag_r, own_sem)
+    scatter = Scatter(z, y, T, part, ybuf, rbuf, y_s, y_r, z_s, z_r)
+    sum_qkv = DpSum(gqkv, gqkv.shape[0] // 4, qa, qb, qa_s, qa_r, qb_s, qb_r)
+    sum_o = DpSum(go_part, go_part.shape[0] // 4, oa, ob, oa_s, oa_r, ob_s, ob_r)
+    gather.start()
+    dk[...] = jnp.zeros_like(dk)
+    dv[...] = jnp.zeros_like(dv)
+    gather.own_ready()
+    U = 2 * T
+    low_lanes = lax.broadcasted_iota(jnp.int32, (U, 128), 1) < HEAD
+    scale = HEAD ** (-0.5)
+
+    def both(product, table):
+        turned = product * table
+        return turned + pltpu.roll(turned, HEAD, 1)
+
+    def unit(i, carry):
+        for h in range(1, 4):
+
+            @pl.when(i == h - 1)
+            def _():
+                gather.hop(h)
+
+        u = line_rank(i, z)
+        gather.pair_ready(u)
+        r = pl.ds(pl.multiple_of(u * U, U), U)
+        d_att = mm_nt(full[r, :], wo_ref[...]).astype(bf16)
+        for h in range(heads):
+            grads[h] = d_att[:, h * 128 : (h + 1) * 128]
+        g = grads[...].reshape(heads * U, 128)
+        q = q_ref[:, r, :].reshape(heads * U, 128)
+        lse = lse_ref[:, r, :].reshape(heads * U, 1)
+
+        def scores(j, inner):
+            c = pl.ds(pl.multiple_of(j * U, U), U)
+            s = mm_nt(q, kz_ref[c, :]) * scale
+            row = lax.broadcasted_iota(jnp.int32, (heads, U, U), 1).reshape(heads * U, U)
+            col = lax.broadcasted_iota(jnp.int32, (heads * U, U), 1)
+            s = jnp.where(col + (j - u) * U <= row, s, masked)
+            p = jnp.exp(s - lse)
+            dp_ = mm_nt(g, vz_ref[c, :])
+            probs[j] = p
+            dprobs[j] = dp_
+            return inner + jnp.sum(p * dp_, axis=1, keepdims=True)
+
+        inner = lax.fori_loop(0, u + 1, scores, jnp.zeros((heads * U, 1), f32))
+
+        def products(j, dq):
+            c = pl.ds(pl.multiple_of(j * U, U), U)
+            p = probs[j]
+            ds = (p * (dprobs[j] - inner)).astype(bf16)
+            dk[c, :] += mm_tn(ds, q)
+            dv[c, :] += mm_tn(p.astype(bf16), g)
+            return dq + mm(ds, k_ref[c, :])
+
+        dq = lax.fori_loop(0, u + 1, products, jnp.zeros((heads * U, 128), f32))
+        table = table_ref[r, :]
+        for h in range(0, heads, 2):
+            first = both(dq[h * U : (h + 1) * U], table)
+            second = both(dq[(h + 1) * U : (h + 2) * U], table)
+            dqkv[r, h * HEAD : (h + 2) * HEAD] = jnp.where(low_lanes, first, second).astype(bf16)
+        return carry
+
+    lax.fori_loop(0, 4, unit, 0)
+
+    def part_rows(i):
+        u = line_rank(i, z)
+        r = pl.ds(pl.multiple_of(u * U, U), U)
+        d_key = both(dk[r, :], table_ref[r, :])
+        dqkv[r, heads * HEAD :] = jnp.where(low_lanes, d_key, pltpu.roll(dv[r, :], HEAD, 1)).astype(bf16)
+        part[r, :] = mm_nt(dqkv[r, :], wqkv_ref[...]).astype(bf16)
+        scatter.start(u)
+
+    def part_loop(i, carry):
+        part_rows(3 - i)
+        return carry
+
+    lax.fori_loop(0, 4, part_loop, 0)
+
+    def qkv_tile(i, carry):
+        r = pl.ds(pl.multiple_of(i * 256, 256), 256)
+        gqkv[r, :] = mm_tn(s1_ref[:, r], dqkv[...]).astype(bf16)
+        return carry
+
+    lax.fori_loop(0, gqkv.shape[0] // 256, qkv_tile, 0)
+    sum_qkv.start()
+    scatter.pass_on(line_rank(3, z))
+    sum_qkv.middle()
+    go_part[...] = mm_tn(att_ref[...], full[...]).astype(bf16)
+    sum_o.start()
+    scatter.pass_on(line_rank(2, z))
+    sum_qkv.finish(gsum)
+
+    def piece(peer):
+        return rows_of(gsum, peer * rows, rows)
+
+    def exchange(peer):
+        return send(piece(peer), got_ref.at[me], ex_s.at[peer], ex_r.at[me], peer)
+
+    own = pltpu.make_async_copy(piece(me), got_ref.at[me], ex_own)
+    own.start()
+    for step in range(1, 8):
+        exchange((me + step) % 8).start()
+    sum_o.middle()
+    scatter.pass_on(line_rank(1, z))
+    sum_o.finish(go_ref)
+    scatter.finish(e1_ref)
+    own.wait()
+    for step in range(1, 8):
+        peer = (me + step) % 8
+        send(piece(me), got_ref.at[peer], ex_s.at[peer], ex_r.at[peer], peer).wait_recv()
+        exchange(peer).wait_send()
+    gather.finish()
+
+
+def attention_back(dm, q2, k2, kz, vz, lse, attended, s1_all, w_qkv, w_o2, table, rows, cid=4):
+    T, width = dm.shape
+    heads, L, _ = q2.shape
+    cols = w_qkv.shape[1]
+    vmem = pl.BlockSpec(memory_space=pltpu.VMEM)
+    U = 2 * T
+    return pl.pallas_call(
+        functools.partial(attention_back_kernel, T, heads),
+        out_shape=(
+            jax.ShapeDtypeStruct((T, width), f32),
+            jax.ShapeDtypeStruct((8, rows, cols), bf16),
+            jax.ShapeDtypeStruct((rows, width), f32),
+        ),
+        in_specs=[vmem] * 11,
+        out_specs=(vmem,) * 3,
+        scratch_shapes=[
+            pltpu.VMEM((L, width), bf16),
+            pltpu.VMEM((heads, U, 128), bf16),
+            pltpu.VMEM((L // U, heads * U, U), f32),
+            pltpu.VMEM((L // U, heads * U, U), f32),
+            pltpu.VMEM((L, 128), f32),
+            pltpu.VMEM((L, 128), f32),
+            pltpu.VMEM((L, cols), bf16),
+            pltpu.VMEM((L, width), bf16),
+            pltpu.VMEM((width, cols), bf16),
+            pltpu.VMEM((heads * HEAD, width), bf16),
+            pltpu.VMEM((width // 4, cols), bf16),
+        ]
+        + line_sems(4)
+        + sum_scratch(T, width)
+        + dp_scratch(width // 4, cols)
+        + dp_scratch(rows, width)
+        + [pltpu.SemaphoreType.DMA((8,)), pltpu.SemaphoreType.DMA((8,)), pltpu.SemaphoreType.DMA],
+        compiler_params=pltpu.CompilerParams(
+            collective_id=cid, has_side_effects=True, vmem_limit_bytes=67000000
+        ),
+        name="attention_back",
+    )(dm, q2, k2, kz, vz, lse, attended, s1_all, w_qkv, w_o2, table)
+
+
+def spread_kernel(
+    down_rows, repeats, gu_ref, qkv_ref, wg_ref, wu_ref, wq_ref, wk_ref, wv_ref, one_ref, two_ref,
+    gate_ref, up_ref, query_ref, key_ref, value_ref, gain1_ref, gain2_ref,
+):
+    S, rows, wide = gu_ref.shape
+    F = wide // 2
+    Dp = gate_ref.shape[1] // (S * down_rows)
+    q_cols = query_ref.shape[1] // S
+    for s in range(S):
+        for d in range(Dp):
+            to = pl.ds((d * S + s) * down_rows, down_rows)
+            gate_ref[:, to] = gu_ref[s, :, d * down_rows : (d + 1) * down_rows].astype(f32)
+            up_ref[:, to] = gu_ref[s, :, F + d * down_rows : F + (d + 1) * down_rows].astype(f32)
+        query_ref[:, s * q_cols : (s + 1) * q_cols] = qkv_ref[s, :, :q_cols].astype(f32)
+    for j in range(S // repeats):
+        total = qkv_ref[j * repeats, :, q_cols:].astype(f32)
+        for s in range(j * repeats + 1, (j + 1) * repeats):
+            total = total + qkv_ref[s, :, q_cols:].astype(f32)
+        key_ref[:, j * HEAD : (j + 1) * HEAD] = total[:, :HEAD]
+        value_ref[:, j * HEAD : (j + 1) * HEAD] = total[:, HEAD:]
+
+    def close(pairs, gain_ref, out_ref):
+        total = jnp.zeros((rows, 1), f32)
+        for weight_ref, grad_ref in pairs:
+            grad = grad_ref[...]
+            total = total + jnp.sum(weight_ref[...].astype(f32) * grad, axis=1, keepdims=True)
+            grad_ref[...] = grad * gain_ref[...]
+        out_ref[...] = total
+
+    close(((wg_ref, gate_ref), (wu_ref, up_ref)), two_ref, gain2_ref)
+    close(((wq_ref, query_ref), (wk_ref, key_ref), (wv_ref, value_ref)), one_ref, gain1_ref)
+
+
+def spread(gu, qkv, weights, gains, down_rows, repeats):
+    rows = gu.shape[1]
+    outs = [jax.ShapeDtypeStruct(w.shape, f32) for w in weights]
+    outs += [jax.ShapeDtypeStruct((rows, 1), f32)] * 2
+    vmem = pl.BlockSpec(memory_space=pltpu.VMEM)
+    return pl.pallas_call(
+        functools.partial(spread_kernel, down_rows, repeats),
+        out_shape=tuple(outs),
+        in_specs=[vmem] * 9,
+        out_specs=(vmem,) * 7,
+        compiler_params=pltpu.CompilerParams(vmem_limit_bytes=40 << 20),
+        name="spread",
+    )(gu, qkv, *weights, *gains)
 
 
 def gather_seq(rows):
@@ -487,8 +841,8 @@
     return (
         mm(hid, w_d).astype(bf16),
         scatter_seq(mm_nt(d_gu, w_gu).astype(bf16)),
-        mm_tn(s2_all, d_gu).astype(bf16),
-        mm_tn(hid, dy_all).astype(bf16),
+        scatter_dp(mm_tn(s2_all, d_gu).astype(bf16)),
+        scatter_dp(mm_tn(hid, dy_all).astype(bf16)).astype(f32),
     )
 
 
@@ -630,7 +984,7 @@
         ],
         axis=2,
     )
-    line = S == 8
+    line = S == 8 and Dp == 4
     width_f = -(-hidden // 256) * 256 if line else hidden
 
     def padded(part, axis):
@@ -662,36 +1016,86 @@
     s2 = middle * r2
     dy = cotangent.reshape(tokens, width)
     dy_all = gather_seq(dy)
-    block = feedforward if line else feedforward_plain
-    out_part, e2, g_gu, g_down = block(s2.astype(bf16), dy_all, w_gu, w_d)
+    if line:
+        out_part, e2, g_gu, down_grad = feedforward(
+            s2.astype(bf16), dy_all, w_gu, w_d, down_rows
+        )
+    else:
+        out_part, e2, g_gu, down_grad = feedforward_plain(s2.astype(bf16), dy_all, w_gu, w_d)
+
+    g_gu = exchange_seq(g_gu.reshape(S, rows, 2 * width_f))
+    d_middle = dy.astype(f32) + r2 * (e2 - s2 * jnp.mean(e2 * s2, axis=-1, keepdims=True))
+    if line:
+        table = jnp.concatenate([cosine, cosine, sine, -sine], axis=-1)[:, 0] * HEAD ** (-0.5)
+        half = HEAD // 2
+
+        def with_swapped(u):
+            return jnp.concatenate([u, u[..., half:], u[..., :half]], axis=-1)
+
+        def with_zeros(u):
+            return jnp.concatenate([u, jnp.zeros_like(u)], axis=-1)
+
+        w_o2 = with_zeros(w_o.reshape(heads, 1, HEAD, width).swapaxes(2, 3)).swapaxes(2, 3)
+        e1, g_qkv, g_o = attention_back(
+            d_middle.astype(bf16),
+            with_swapped(queries),
+            with_swapped(keys),
+            with_zeros(keys),
+            with_zeros(values),
+            totals,
+            attended,
+            s1_all,
+            w_qkv,
+            w_o2.reshape(2 * q_cols, width),
+            table,
+            rows,
+        )
+        g_o = g_o.astype(bf16)
+    else:
+        dm_all = gather_seq(d_middle.astype(bf16))
+        d_att = heads_first(mm_nt(dm_all, w_o).astype(bf16), heads)
+        d_q, d_k, d_v = attention_backward(queries, keys, values, d_att, totals, block_rows)
+        d_q = jnp.transpose(d_q, (1, 0, 2))
+        d_qkv = jnp.concatenate(
+            [
+                rotate(d_q, cosine, -sine).reshape(length, q_cols).astype(bf16),
+                rotate(d_k[:, None], cosine, -sine)[:, 0].astype(bf16),
+                d_v.astype(bf16),
+            ],
+            axis=1,
+        )
+        e1 = scatter_seq(mm_nt(d_qkv, w_qkv).astype(bf16))
+        g_o = scatter_dp(mm_tn(attended, dm_all).astype(bf16))
+        g_qkv = scatter_dp(mm_tn(s1_all, d_qkv).astype(bf16))
+        g_qkv = exchange_seq(g_qkv.reshape(S, rows, q_cols + 2 * HEAD))
     output = (middle + scatter_seq(out_part)).astype(bf16)
-
-    d_middle = dy.astype(f32) + r2 * (e2 - s2 * jnp.mean(e2 * s2, axis=-1, keepdims=True))
-    dm_all = gather_seq(d_middle.astype(bf16))
-    d_att = heads_first(mm_nt(dm_all, w_o).astype(bf16), heads)
-    d_q, d_k, d_v = attention_backward(queries, keys, values, d_att, totals, block_rows)
-    d_q = jnp.transpose(d_q, (1, 0, 2))
-    d_qkv = jnp.concatenate(
-        [
-            rotate(d_q, cosine, -sine).reshape(length, q_cols).astype(bf16),
-            rotate(d_k[:, None], cosine, -sine)[:, 0].astype(bf16),
-            d_v.astype(bf16),
-        ],
-        axis=1,
-    )
-    e1 = scatter_seq(mm_nt(d_qkv, w_qkv).astype(bf16))
     input_grad = d_middle + r1 * (e1 - s1 * jnp.mean(e1 * s1, axis=-1, keepdims=True))
-
-    down_grad = scatter_dp(g_down[:hidden]).astype(f32)
-    g_gu = scatter_dp(g_gu)
-    g_gu = jnp.concatenate([g_gu[:, :hidden], g_gu[:, width_f : width_f + hidden]], axis=1)
-    output_grad = lax.ppermute(
-        scatter_dp(mm_tn(attended, dm_all).astype(bf16)), ("dp", "seq"), backward_perm
-    ).astype(f32)
-    g_qkv = scatter_dp(mm_tn(s1_all, d_qkv).astype(bf16))
-
-    g_gu = exchange_seq(g_gu.reshape(S, rows, 2 * hidden)).astype(f32)
-    g_qkv = exchange_seq(g_qkv.reshape(S, rows, q_cols + 2 * HEAD)).astype(f32)
+    output_grad = lax.ppermute(g_o, ("dp", "seq"), backward_perm).astype(f32)
+
+    if line:
+        g_gate, g_up, g_query, g_key, g_value, gain_one_grad, gain_two_grad = spread(
+            g_gu,
+            g_qkv,
+            (gate_weight, up_weight, query_weight, key_weight, value_weight),
+            (gain_one, gain_two),
+            down_rows,
+            repeats,
+        )
+        return (
+            output.reshape(sequences, tokens, width),
+            input_grad.reshape(sequences, tokens, width),
+            gain_one_grad[:, 0],
+            g_query,
+            g_key,
+            g_value,
+            output_grad,
+            gain_two_grad[:, 0],
+            g_gate,
+            g_up,
+            down_grad,
+        )
+
+    g_gu, g_qkv = g_gu.astype(f32), g_qkv.astype(f32)
 
     def back_hidden(part):
         return jnp.transpose(part.reshape(S, rows, Dp, down_rows), (1, 2, 0, 3)).reshape(rows, -1)

time: 752 us -> 671 us (0.89)
  waiting for transfers between devices: 106 us -> 24.3 us
  matrix products: 46.2 us -> 14 us
  Pallas kernels: 422 us -> 449 us
    pallas_call x0 -> x2, Pallas kernels: none -> 120 us  [the longest x1 115 us: attention_back(): pl.pallas_call(functools.partial(attention_back_kernel, T, heads), out_sh...]
    reduce_scatter x4 -> x0, waiting for transfers between devices: 75.2 us -> none  [scatter_dp(): return lax.psum_scatter(rows, 'dp', scatter_dimension=0, tiled=True)]
    pallas_call x3 -> x2, Pallas kernels: 165 us -> 101 us  [scatter_line(): pl.pallas_call(functools.partial(scatter_kernel, Z, T), out_shape=jax.Sha...]
    pallas_call x3 -> x2, Pallas kernels: 143 us -> 96.5 us  [gather_line(): pl.pallas_call(functools.partial(gather_kernel, Z, T), out_shape=jax.Shap...]
    dot_general x12 -> x0, matrix products: 30.7 us -> none  [the longest x2 9.36 us: mm_nt(): lax.dot_general(a, b, (((1,), (1,)), ((), ())), preferred_element_type=f32)]
    pallas_call x1, Pallas kernels: 115 us -> 132 us  [feedforward(): pl.pallas_call(functools.partial(feedforward_kernel, T), out_shape=(jax.S...]
    reshape x9 -> x2, local copies, waits for them, and re-layouts: 16.4 us -> 1.02 us  [the longest x1 1 us: heads_last(): return jnp.transpose(stacked, (1, 0, 2)).reshape(stacked.shape[1], -1)]
    reduce_sum x2, other arithmetic: 3.37 us -> 16.3 us  [attention_forward(): jnp.sum(jnp.exp(scores - row_max), axis=-1, keepdims=True)]
  transfers between devices with their start and end apart: 12 -> 7, of which waited for: 4 -> 2; matrix products, arithmetic and copies ran while one was open for 9% -> 14% of each run, Pallas kernels for 35% -> 47%
where the time goes in v4:
time: 671 us; the launch traced here: 662 us
  Pallas kernels  449 us (67%)
  blocking collectives  52.4 us (8%)
  other arithmetic  50.1 us (7%)
  local copies, waits for them, and re-layouts  37.3 us (6%)
  waiting for transfers between devices  24.3 us (4%)
  starting transfers between devices  19.7 us (3%)
  between operations  14.9 us (2%)
  matrix products  14 us (2%)
    pallas_call x1, Pallas kernels, feedforward(): pl.pallas_call(functools.partial(feedforward_kernel, T), out_shape=(jax.S...  132 us
    pallas_call x1, Pallas kernels, attention_back(): pl.pallas_call(functools.partial(attention_back_kernel, T, heads), out_sh...  115 us
    pallas_call x2, Pallas kernels, scatter_line(): pl.pallas_call(functools.partial(scatter_kernel, Z, T), out_shape=jax.Sha...  101 us
    pallas_call x2, Pallas kernels, gather_line(): pl.pallas_call(functools.partial(gather_kernel, Z, T), out_shape=jax.Shap...  96.5 us
    all_to_all x2, blocking collectives, exchange_seq(): lax.all_to_all(pieces, 'seq', split_axis=0, concat_axis=0, tiled=True)  52.4 us
    reduce_sum x2, other arithmetic, attention_forward(): jnp.sum(jnp.exp(scores - row_max), axis=-1, keepdims=True)  16.3 us
    all_to_all x1, starting transfers between devices, exchange_seq(): lax.all_to_all(pieces, 'seq', split_axis=0, concat_axis=0, tiled=True)  14.2 us
    ppermute x1, waiting for transfers between devices, shards(): w_o = gather_dp(lax.ppermute(output_weight, ('dp', 'seq'), forward_perm))  13.5 us
  transfers between devices with their start and end apart: 7, of which 2 were waited for; matrix products, arithmetic and copies ran while one was open for 14% of the time, Pallas kernels for 47%

profile of v4, /device:TPU:26, one launch (start us, length us, event | category | flops | bytes accessed | tf_op | source)
XLA Modules:
  0.0 661.6 jit_solution(6654893364776017330)
XLA Ops:
  7.3 3.4 collective-permute-start
  10.7 13.5 %collective-permute-done = bf16[64,2048]{1,0:T(8,128)(2,1)S(1)} collective-permute-done((bf16[64,2048]{1,0:T(8,128)(2,1)}, bf16[64,2048]{1,0:T(8,128)(2,1)S(1)}, u32[]{:S(2)}, u32[]{:S(2)}) %collective-permute-start) | collective-permute-done | bytes 262176 | tf_op jit(solution)/shard_map/ppermute | solution.py:979
  28.0 14.8 %all_to_all.15 = bf16[8,64,384]{2,1,0:T(8,128)(2,1)} all-to-all(bf16[8,64,384]{2,1,0:T(8,128)(2,1)S(1)} %maximum_bitcast_fusion.1), channel_id=1, replica_groups=mesh['dp'=4,'seq'=8] {'seq'}, dimensions={0} | all-to-all | bytes 786432 | tf_op jit(solution)/shard_map/all_to_all | solution.py:858
  48.2 3.0 reshape.290
  53.0 37.6 %all_to_all.16 = bf16[8,64,1408]{2,1,0:T(8,128)(2,1)S(1)} all-to-all(bf16[8,64,1408]{2,1,0:T(8,128)(2,1)S(1)} %pad_maximum_fusion), channel_id=1, replica_groups=mesh['dp'=4,'seq'=8] {'seq'}, dimensions={0} | all-to-all | bytes 2883584 | tf_op jit(solution)/shard_map/all_to_all | solution.py:858
  94.2 49.4 %gather_seq.2.s1_ref = bf16[1024,2048]{1,0:T(8,128)(2,1)} custom-call(bf16[128,2048]{1,0:T(8,128)(2,1)} %fusion.10.x_ref), custom_call_target="tpu_custom_call" | custom-call | tf_op jit(solution)/shard_map/gather_seq/pallas_call | solution.py:133
  143.6 47.0 %gather_seq.3.dy_ref = bf16[1024,2048]{1,0:T(8,128)(2,1)} custom-call(bf16[128,2048]{1,0:T(8,128)(2,1)} %bitcast.95), custom_call_target="tpu_custom_call" | custom-call | tf_op jit(solution)/shard_map/gather_seq/pallas_call | solution.py:133
  192.7 2.8 fusion.29
  195.5 2.9 concatenate.72
  198.4 4.5 fusion.44
  209.0 3.0 copy.91
  214.1 3.0 fusion.26
  224.2 15.4 %exponential_reduce_fusion = f32[4,512]{1,0:T(4,128)S(1)} fusion(f32[4,512,1024]{2,1,0:T(8,128)S(1)} %get-tuple-element.65, f32[4,512]{1,0:T(4,128)S(1)} %get-tuple-element.64, pred[512,1024]{1,0:T(8,128)(4,1)S(1)} %iota_compare_fusion.1), kind=kLoop, calls=%fused_computation.1 | loop fusion | flops 8386560 | bytes 8929280 | tf_op jit(solution)/shard_map/reduce_sum | solution.py:874
  244.2 3.3 convolution_convert_fusion.p_ref
  247.5 48.9 %scatter_seq.2 = f32[128,2048]{1,0:T(8,128)} custom-call(bf16[1024,2048]{1,0:T(8,128)(2,1)} %convolution_convert_fusion.p_ref), custom_call_target="tpu_custom_call" | custom-call | tf_op jit(solution)/shard_map/scatter_seq/pallas_call | solution.py:202
  300.1 4.0 pad.16.wd_ref
  304.1 131.9 %feedforward.1 = (bf16[1024,2048]{1,0:T(8,128)(2,1)}, f32[128,2048]{1,0:T(8,128)}, bf16[512,1536]{1,0:T(8,128)(2,1)}, f32[176,2048]{1,0:T(8,128)}) custom-call(bf16[128,2048]{1,0:T(8,128)(2,1)} %multiply_convert_fusion.2.x_ref, bf16[1024,2048]{1,0:T(8,128)(2,1)} %gather_seq.3.dy_ref, bf16[2048,1536]{1,0:T(8,128)(2,1)} %all-gather.9.cloned.1.call-done.wgu_ref, ...), custom_call_target="tpu_custom_call" | custom-call | tf_op jit(solution)/shard_map/feedforward/pallas_call | solution.py:566
  436.1 14.2 %all-to-all-start.2 = ((bf16[8,64,1536]{2,1,0:T(8,128)(2,1)}), bf16[8,64,1536]{2,1,0:T(8,128)(2,1)}, u32[]{:S(2)}, u32[]{:S(2)}) async-start(bf16[8,64,1536]{2,1,0:T(8,128)(2,1)} %bitcast.104), calls=%async_computation.2 | async-start | bytes 3145728 | tf_op jit(solution)/shard_map/all_to_all | solution.py:858
  457.8 51.7 %scatter_seq.3 = f32[128,2048]{1,0:T(8,128)} custom-call(bf16[1024,2048]{1,0:T(8,128)(2,1)} %get-tuple-element.25.p_ref), custom_call_target="tpu_custom_call" | custom-call | tf_op jit(solution)/shard_map/scatter_seq/pallas_call | solution.py:202
  511.0 115.3 %attention_back.1 = (f32[128,2048]{1,0:T(8,128)}, bf16[8,64,384]{2,1,0:T(8,128)(2,1)}, f32[64,2048]{1,0:T(8,128)}) custom-call(bf16[128,2048]{1,0:T(8,128)(2,1)} %fusion.41.dm_ref, bf16[4,1024,128]{2,1,0:T(8,128)(2,1)} %pad_maximum_fusion.1.q_ref, bf16[1024,128]{1,0:T(8,128)(2,1)} %pad_maximum_fusion.4.k_ref, bf16[1024,128]{1,0:T(8,128)(2,1)} %concatenate.69.kz_ref, ...), custom_call_target="tpu_custom_call" | custom-call | tf_op jit(solution)/shard_map/attention_back/pallas_call | solution.py:736
  631.1 4.4 fusion.17
  635.5 10.1 %collective-permute-done.1 = bf16[64,2048]{1,0:T(8,128)(2,1)S(1)} collective-permute-done((bf16[64,2048]{1,0:T(8,128)(2,1)S(1)}, bf16[64,2048]{1,0:T(8,128)(2,1)S(1)}, u32[]{:S(2)}, u32[]{:S(2)}) %collective-permute-start.1) | collective-permute-done | bytes 262176 | tf_op jit(solution)/shard_map/ppermute | solution.py:1073
  646.5 4.3 spread.1
  652.0 2.6 copy.97
  (166 shorter events, 55.4 us)
Async XLA Ops:
  7.2 36.4 %copy-start.40 = (bf16[64]{0:T(256)(128)(2,1)S(1)}, bf16[64]{0:T(256)(128)(2,1)}, u32[]{:S(2)}) copy-start(bf16[64]{0:T(256)(128)(2,1)} %param.17) | copy-start | bytes 388
  7.2 36.5 %copy-start = (bf16[64,5632]{1,0:T(8,128)(2,1)S(1)}, bf16[64,5632]{1,0:T(8,128)(2,1)}, u32[]{:S(2)}) copy-start(bf16[64,5632]{1,0:T(8,128)(2,1)} %wg_ref.1) | copy-start | bytes 2162692
  7.2 36.5 %copy-start.2 = (bf16[64,5632]{1,0:T(8,128)(2,1)S(1)}, bf16[64,5632]{1,0:T(8,128)(2,1)}, u32[]{:S(2)}) copy-start(bf16[64,5632]{1,0:T(8,128)(2,1)} %wu_ref.1) | copy-start | bytes 2162692
  7.2 188.3 %all-gather.7.cloned.1.call-start = ((), (), s32[]{:S(2)}) async-start(), calls=%async_computation.4 | async-start | bytes 1310720 | tf_op jit(solution)/shard_map/all_gather | solution.py:850
  7.3 16.9 %collective-permute-start = (bf16[64,2048]{1,0:T(8,128)(2,1)}, bf16[64,2048]{1,0:T(8,128)(2,1)S(1)}, u32[]{:S(2)}, u32[]{:S(2)}) collective-permute-start(bf16[64,2048]{1,0:T(8,128)(2,1)} %param.16), channel_id=1, source_target_pairs={{0,0},{1,8},{2,16},{3,24},{4,1},{5,9},{6,17},{7,25},{8,2},{9,10},{... | collective-permute-start | bytes 786440 | tf_op jit(solution)/shard_map/ppermute | solution.py:979
  24.9 173.4 %all-gather.5.cloned.1.call-start = ((), (), s32[]{:S(2)}) async-start(), calls=%async_computation.3 | async-start | bytes 1966080 | tf_op jit(solution)/shard_map/all_gather | solution.py:850
  42.8 257.2 %all-gather.11.cloned.1.call-start = ((), (), s32[]{:S(2)}) async-start(), calls=%async_computation.6 | async-start | bytes 3604480 | tf_op jit(solution)/shard_map/all_gather | solution.py:850
  43.6 260.5 %all-gather.9.cloned.1.call-start = ((), (), s32[]{:S(2)}) async-start(), calls=%async_computation.5 | async-start | bytes 7864320 | tf_op jit(solution)/shard_map/all_gather | solution.py:850
  52.5 38.5 %copy-start.39 = (pred[768]{0:T(1024)(128)(4,1)S(1)}, pred[768]{0:T(1024)(128)(4,1)}, u32[]{:S(2)}) copy-start(pred[768]{0:T(1024)(128)(4,1)} %constant.32.clone.1) | copy-start | bytes 2308
  436.0 16.3 %copy-start.30 = (bf16[1024,64]{1,0:T(8,128)(2,1)S(1)}, bf16[1024,64]{1,0:T(8,128)(2,1)}, u32[]{:S(2)}) copy-start(bf16[1024,64]{1,0:T(8,128)(2,1)} %slice.78) | copy-start | bytes 393220
  436.0 17.1 %copy-start.21 = (bf16[1024,1,32]{2,0,1:T(8,128)(2,1)S(1)}, bf16[1024,1,32]{2,0,1:T(8,128)(2,1)}, u32[]{:S(2)}) copy-start(bf16[1024,1,32]{2,0,1:T(8,128)(2,1)} %copy-done.20) | copy-start | bytes 196612
  436.0 17.1 %copy-start.23 = (bf16[1024,1,32]{2,0,1:T(8,128)(2,1)S(1)}, bf16[1024,1,32]{2,0,1:T(8,128)(2,1)}, u32[]{:S(2)}) copy-start(bf16[1024,1,32]{2,0,1:T(8,128)(2,1)} %copy-done.22) | copy-start | bytes 196612
  436.1 18.1 %copy-start.27 = (f32[1024,1,32]{2,0,1:T(8,128)S(1)}, f32[1024,1,32]{2,0,1:T(8,128)}, u32[]{:S(2)}) copy-start(f32[1024,1,32]{2,0,1:T(8,128)} %get-tuple-element.53) | copy-start | bytes 393220
  436.1 18.1 %copy-start.28 = (f32[1024,1,32]{2,0,1:T(8,128)S(1)}, f32[1024,1,32]{2,0,1:T(8,128)}, u32[]{:S(2)}) copy-start(f32[1024,1,32]{2,0,1:T(8,128)} %get-tuple-element.54) | copy-start | bytes 393220
  436.1 18.1 %copy-start.29 = (f32[1024,1,32]{2,0,1:T(8,128)S(1)}, f32[1024,1,32]{2,0,1:T(8,128)}, u32[]{:S(2)}) copy-start(f32[1024,1,32]{2,0,1:T(8,128)} %get-tuple-element.55) | copy-start | bytes 393220
  436.1 210.3 %all-to-all-start.2 = ((bf16[8,64,1536]{2,1,0:T(8,128)(2,1)}), bf16[8,64,1536]{2,1,0:T(8,128)(2,1)}, u32[]{:S(2)}, u32[]{:S(2)}) async-start(bf16[8,64,1536]{2,1,0:T(8,128)(2,1)} %bitcast.104), calls=%async_computation.2 | async-start | bytes 3145728 | tf_op jit(solution)/shard_map/all_to_all | solution.py:858
  457.7 51.8 %copy-start.9 = (f32[128,2048]{1,0:T(8,128)S(1)}, f32[128,2048]{1,0:T(8,128)}, u32[]{:S(2)}) copy-start(f32[128,2048]{1,0:T(8,128)} %scatter_seq.2) | copy-start | bytes 3145732
  457.8 51.8 %copy-start.11 = (bf16[1,128,2048]{2,1,0:T(8,128)(2,1)S(1)}, bf16[1,128,2048]{2,1,0:T(8,128)(2,1)}, u32[]{:S(2)}) copy-start(bf16[1,128,2048]{2,1,0:T(8,128)(2,1)} %param.11) | copy-start | bytes 1572868
  457.8 51.8 %copy-start.14 = (f32[128,2048]{1,0:T(8,128)S(1)}, f32[128,2048]{1,0:T(8,128)}, u32[]{:S(2)}) copy-start(f32[128,2048]{1,0:T(8,128)} %get-tuple-element.26) | copy-start | bytes 3145732
  457.8 51.8 %copy-start.35 = (f32[128]{0:T(128)S(1)}, f32[128]{0:T(128)}, u32[]{:S(2)}) copy-start(f32[128]{0:T(128)} %copy-done.34) | copy-start | bytes 1540
  457.8 52.1 %copy-start.17 = (bf16[1,128,2048]{2,1,0:T(8,128)(2,1)S(1)}, bf16[1,128,2048]{2,1,0:T(8,128)(2,1)}, u32[]{:S(2)}) copy-start(bf16[1,128,2048]{2,1,0:T(8,128)(2,1)} %param.21) | copy-start | bytes 1572868
  511.0 118.4 %copy-start.37 = (f32[128]{0:T(128)S(1)}, f32[128]{0:T(128)}, u32[]{:S(2)}) copy-start(f32[128]{0:T(128)} %copy-done.36) | copy-start | bytes 1540
  627.5 18.1 %collective-permute-start.1 = (bf16[64,2048]{1,0:T(8,128)(2,1)S(1)}, bf16[64,2048]{1,0:T(8,128)(2,1)S(1)}, u32[]{:S(2)}, u32[]{:S(2)}) collective-permute-start(bf16[64,2048]{1,0:T(8,128)(2,1)S(1)} %convert_element_type.119), channel_id=1, source_target_pairs={{0,0},{8,1},{16,2},{24,3},{1,4},{9,5},{17,6},{25,7},{2,8},{10,9},{... | collective-permute-start | bytes 786440 | tf_op jit(solution)/shard_map/ppermute | solution.py:1073
  631.1 15.4 %copy-start.1 = (bf16[64,5632]{1,0:T(8,128)(2,1)S(1)}, bf16[64,5632]{1,0:T(8,128)(2,1)}, u32[]{:S(2)}) copy-start(bf16[64,5632]{1,0:T(8,128)(2,1)} %wg_ref.1) | copy-start | bytes 2162692
  (24 other events, 155.6 us)
Sparse Core Ops, SparseCore 0:
  25.0 15.7 all-gather.6
  43.0 19.4 all-gather.4
  64.0 27.0 all-gather.10
  92.6 46.1 all-gather.8

commit v5 on v4

--- a/solution.py
+++ b/solution.py
@@ -299,19 +299,22 @@
             b, b, self.sems["y"].at[zz], self.recv_sem.at[zz * 2 + 1 - self.y], self.peers["y"]
         ).wait_recv()
 
+    def finish_one(self, zz):
+        z = self.z
+        src = self.block(zz, self.y)
+        self.copy(src, zz, "y").wait_send()
+
+        @pl.when((zz <= z) & (z < 3))
+        def _():
+            self.copy(src, zz, "up").wait_send()
+
+        @pl.when((zz >= z) & (z > 0))
+        def _():
+            self.copy(src, zz, "dn").wait_send()
+
     def finish(self):
-        z = self.z
         for zz in range(4):
-            src = self.block(zz, self.y)
-            self.copy(src, zz, "y").wait_send()
-
-            @pl.when((zz <= z) & (z < 3))
-            def _():
-                self.copy(src, zz, "up").wait_send()
-
-            @pl.when((zz >= z) & (z > 0))
-            def _():
-                self.copy(src, zz, "dn").wait_send()
+            self.finish_one(zz)
 
 
 class Scatter:
@@ -471,6 +474,40 @@
         self.a_copy(0).wait_send()
         self.a_copy(1).wait_send()
         self.b_copy().wait_send()
+
+
+class DpGather:
+    def __init__(self, own, full, size, s_sem, r_sem):
+        dp = lax.axis_index("dp")
+        self.dp, self.partner, self.across = dp, dp + 1 - 2 * (dp % 2), dp + 2 - 4 * (dp // 2)
+        self.diagonal = 3 - dp
+        self.own, self.full, self.size = own, full, size
+        self.s_sem, self.r_sem = s_sem, r_sem
+
+    def block(self, d):
+        return rows_of(self.full, d * self.size, self.size)
+
+    def copy(self, src, d, k, peer):
+        return send(src, self.block(d), self.s_sem.at[k], self.r_sem.at[k], peer, "dp")
+
+    def start(self):
+        self.copy(self.own, self.dp, 0, self.across).start()
+        self.copy(self.own, self.dp, 1, self.partner).start()
+
+    def relay(self):
+        far = self.block(self.across)
+        self.copy(far, self.across, 0, self.across).wait_recv()
+        self.copy(far, self.across, 2, self.partner).start()
+
+    def ready(self):
+        near, diagonal = self.block(self.partner), self.block(self.diagonal)
+        self.copy(near, self.partner, 1, self.partner).wait_recv()
+        self.copy(diagonal, self.diagonal, 2, self.partner).wait_recv()
+
+    def finish(self):
+        self.copy(self.own, self.dp, 0, self.across).wait_send()
+        self.copy(self.own, self.dp, 1, self.partner).wait_send()
+        self.copy(self.block(self.across), self.across, 2, self.partner).wait_send()
 
 
 def dp_scratch(size, width):
@@ -590,6 +627,210 @@
         ),
         name="feedforward",
     )(x, dy_all, w_gu, w_d)
+
+
+def attention_front_kernel(
+    T, heads, s1_ref, piece_ref, wo_piece_ref, dy_ref, table_ref,
+    mid_ref, s1_all, dy_all, wqkv, wo, q_out, k2_ref, kz_ref, vz_ref, lse_ref, att_ref,
+    score, part,
+    up_sem, dn_sem, ag_y, ag_r, own_sem,
+    up_sem2, dn_sem2, ag_y2, ag_r2, own_sem2,
+    ybuf, rbuf, y_s, y_r, z_s, z_r,
+    w_s, w_r, o_s, o_r, ex_s, ex_r, ex_own, wo_own,
+):
+    z, y = seq_place()
+    me = z * 2 + y
+    dp = lax.axis_index("dp")
+    rows, out_rows = piece_ref.shape[1], wo_piece_ref.shape[0]
+    barrier = pltpu.get_barrier_semaphore()
+    for step in range(1, 8):
+        hello(barrier, (me + step) % 8, "seq")
+    hello(barrier, dp + 1 - 2 * (dp % 2), "dp")
+    hello(barrier, dp + 2 - 4 * (dp // 2), "dp")
+    pl.semaphore_wait(barrier, 9)
+    gather = Gather(z, y, T, s1_ref, s1_all, up_sem, dn_sem, ag_y, ag_r, own_sem)
+    gather_dy = Gather(z, y, T, dy_ref, dy_all, up_sem2, dn_sem2, ag_y2, ag_r2, own_sem2)
+    scatter = Scatter(z, y, T, part, ybuf, rbuf, y_s, y_r, z_s, z_r)
+    w_own = rows_of(wqkv, dp * 8 * rows, 8 * rows)
+    w_all = DpGather(w_own, wqkv, 8 * rows, w_s, w_r)
+    o_all = DpGather(wo_piece_ref, wo, out_rows, o_s, o_r)
+
+    def landing(peer):
+        return rows_of(wqkv, (dp * 8 + peer) * rows, rows)
+
+    def exchange(peer):
+        return send(piece_ref.at[peer], landing(me), ex_s.at[peer], ex_r.at[me], peer)
+
+    own = pltpu.make_async_copy(piece_ref.at[me], landing(me), ex_own)
+    own.start()
+    own_o = pltpu.make_async_copy(wo_piece_ref, o_all.block(dp), wo_own)
+    own_o.start()
+    for step in range(1, 8):
+        exchange((me + step) % 8).start()
+    gather.start()
+    o_all.start()
+    own.wait()
+    own_o.wait()
+    for step in range(1, 8):
+        peer = (me + step) % 8
+        send(
+            piece_ref.at[me], landing(peer), ex_s.at[peer], ex_r.at[peer], peer
+        ).wait_recv()
+    w_all.start()
+    gather.own_ready()
+    gather.hop(1)
+    o_all.relay()
+    w_all.relay()
+    w_all.ready()
+    U = 2 * T
+    lane = lax.broadcasted_iota(jnp.int32, (U, 128), 1)
+    low_lanes = lane < HEAD
+    front = lane % HEAD < HEAD // 2
+    scale = HEAD ** (-0.5)
+
+    def swapped(u):
+        return jnp.where(front, pltpu.roll(u, 128 - HEAD // 2, 1), pltpu.roll(u, HEAD // 2, 1))
+
+    def project(i, carry):
+        for h in (2, 3):
+
+            @pl.when(i == h - 1)
+            def _():
+                gather.hop(h)
+
+        @pl.when(i == 2)
+        def _():
+            gather_dy.start()
+
+        u = line_rank(i, z)
+        gather.pair_ready(u)
+        r = pl.ds(pl.multiple_of(u * U, U), U)
+        qkv = mm(s1_all[r, :], wqkv[...])
+        cos, sin = table_ref[r, :128], table_ref[r, 128:]
+
+        def roped(tile):
+            return tile * cos + swapped(tile) * sin
+
+        for h in range(0, heads, 2):
+            turned = roped(qkv[:, h * HEAD : (h + 2) * HEAD])
+            other = swapped(turned)
+            q_out[h, r, :] = jnp.where(low_lanes, turned, pltpu.roll(other, HEAD, 1)).astype(bf16)
+            q_out[h + 1, r, :] = jnp.where(low_lanes, pltpu.roll(turned, HEAD, 1), other).astype(bf16)
+        tile = qkv[:, heads * HEAD :]
+        turned = roped(tile)
+        k2_ref[r, :] = jnp.where(low_lanes, turned, pltpu.roll(swapped(turned), HEAD, 1)).astype(bf16)
+        kz_ref[r, :] = jnp.where(low_lanes, turned, 0.0).astype(bf16)
+        vz_ref[r, :] = jnp.where(low_lanes, pltpu.roll(tile, HEAD, 1), 0.0).astype(bf16)
+        return carry
+
+    lax.fori_loop(0, 4, project, 0)
+    o_all.ready()
+    gather_dy.own_ready()
+
+    def unit(i, carry):
+        for h in range(1, 4):
+
+            @pl.when(i == h)
+            def _():
+                gather_dy.hop(h)
+
+        u = line_rank(3 - i, z)
+        r = pl.ds(pl.multiple_of(u * U, U), U)
+        q = q_out[:, r, :].reshape(heads * U, 128)
+
+        def scores(j, top):
+            c = pl.ds(pl.multiple_of(j * U, U), U)
+            s = mm_nt(q, kz_ref[c, :]) * scale
+            row = lax.broadcasted_iota(jnp.int32, (heads, U, U), 1).reshape(heads * U, U)
+            col = lax.broadcasted_iota(jnp.int32, (heads * U, U), 1)
+            s = jnp.where(col + (j - u) * U <= row, s, masked)
+            score[j] = s
+            return jnp.maximum(top, jnp.max(s, axis=1, keepdims=True))
+
+        top = lax.fori_loop(0, u + 1, scores, jnp.full((heads * U, 1), masked, f32))
+
+        def weigh(j, carry):
+            total, out = carry
+            c = pl.ds(pl.multiple_of(j * U, U), U)
+            p = jnp.exp(score[j] - top)
+            return (
+                total + jnp.sum(p, axis=1, keepdims=True),
+                out + mm(p.astype(bf16), vz_ref[c, :]),
+            )
+
+        total, out = lax.fori_loop(
+            0,
+            u + 1,
+            weigh,
+            (jnp.zeros((heads * U, 1), f32), jnp.zeros((heads * U, 128), f32)),
+        )
+        lse_ref[:, r, :] = (top + jnp.log(total)).reshape(heads, U, 1)
+        out = out / total
+        for h in range(0, heads, 2):
+            first, second = out[h * U : (h + 1) * U], out[(h + 1) * U : (h + 2) * U]
+            att_ref[r, h * HEAD : (h + 2) * HEAD] = jnp.where(
+                low_lanes, first, pltpu.roll(second, HEAD, 1)
+            ).astype(bf16)
+        part[r, :] = mm(att_ref[r, :], wo[...]).astype(bf16)
+        scatter.start(u)
+        for k in (1, 2):
+
+            @pl.when(i == k)
+            def _():
+                scatter.pass_on(line_rank(4 - k, z))
+
+        return carry
+
+    lax.fori_loop(0, 4, unit, 0)
+    scatter.pass_on(line_rank(1, z))
+    scatter.finish(mid_ref)
+    for zz in range(4):
+        gather.finish_one(zz)
+        gather_dy.pair_ready(zz)
+        gather_dy.finish_one(zz)
+    for step in range(1, 8):
+        exchange((me + step) % 8).wait_send()
+    w_all.finish()
+    o_all.finish()
+
+
+def attention_front(s1, piece, wo_piece, dy, table, heads, cid=5):
+    T, width = s1.shape
+    S, rows, cols = piece.shape
+    L, q_cols, U = S * T, heads * HEAD, 2 * T
+    vmem = pl.BlockSpec(memory_space=pltpu.VMEM)
+    return pl.pallas_call(
+        functools.partial(attention_front_kernel, T, heads),
+        out_shape=(
+            jax.ShapeDtypeStruct((T, width), f32),
+            jax.ShapeDtypeStruct((L, width), bf16),
+            jax.ShapeDtypeStruct((L, width), bf16),
+            jax.ShapeDtypeStruct((width, cols), bf16),
+            jax.ShapeDtypeStruct((q_cols, width), bf16),
+            jax.ShapeDtypeStruct((heads, L, 128), bf16),
+            jax.ShapeDtypeStruct((L, 128), bf16),
+            jax.ShapeDtypeStruct((L, 128), bf16),
+            jax.ShapeDtypeStruct((L, 128), bf16),
+            jax.ShapeDtypeStruct((heads, L, 1), f32),
+            jax.ShapeDtypeStruct((L, q_cols), bf16),
+        ),
+        in_specs=[vmem] * 5,
+        out_specs=(vmem,) * 11,
+        scratch_shapes=[
+            pltpu.VMEM((L // U, heads * U, U), f32),
+            pltpu.VMEM((L, width), bf16),
+        ]
+        + line_sems(4)
+        + line_sems(4)
+        + sum_scratch(T, width)
+        + [pltpu.SemaphoreType.DMA((3,))] * 4
+        + [pltpu.SemaphoreType.DMA((8,))] * 2
+        + [pltpu.SemaphoreType.DMA] * 2,
+        compiler_params=pltpu.CompilerParams(
+            collective_id=cid, has_side_effects=True, vmem_limit_bytes=67000000
+        ),
+        name="attention_front",
+    )(s1, piece, wo_piece, dy, table)
 
 
 def attention_back_kernel(
@@ -972,11 +1213,10 @@
         ],
         axis=2,
     )
-    packed = jnp.transpose(packed, (1, 0, 2))
-    w_qkv = gather_dp(exchange_seq(packed).reshape(S * rows, q_cols + 2 * HEAD))
+    packed_qkv = jnp.transpose(packed, (1, 0, 2))
     forward_perm = [(Dp * s + d, d * S + s) for s in range(S) for d in range(Dp)]
     backward_perm = [(b, a) for a, b in forward_perm]
-    w_o = gather_dp(lax.ppermute(output_weight, ("dp", "seq"), forward_perm))
+    w_o_piece = lax.ppermute(output_weight, ("dp", "seq"), forward_perm)
     packed = jnp.concatenate(
         [
             per_group_hidden(folded(gate_weight, gain_two)),
@@ -1002,20 +1242,31 @@
     flat = inputs.reshape(tokens, width).astype(f32)
     r1 = rms_scale(flat)
     s1 = flat * r1
-    s1_all = gather_seq(s1.astype(bf16))
     cosine, sine = rope_tables(length)
-    qkv = mm(s1_all, w_qkv)
-    queries = rotate(qkv[:, :q_cols].reshape(length, heads, HEAD), cosine, sine).astype(bf16)
-    queries = jnp.transpose(queries, (1, 0, 2))
-    keys = rotate(qkv[:, None, q_cols : q_cols + HEAD], cosine, sine).astype(bf16)[:, 0]
-    values = qkv[:, q_cols + HEAD :].astype(bf16)
-    attended, totals = attention_forward(queries, keys, values, block_rows)
-    attended = heads_last(attended)
-    middle = flat + scatter_seq(mm(attended, w_o).astype(bf16))
+    dy = cotangent.reshape(tokens, width)
+    if line:
+        turn = jnp.concatenate(
+            [cosine, cosine, cosine, cosine, -sine, sine, -sine, sine], axis=-1
+        )[:, 0]
+        summed, s1_all, dy_all, w_qkv, w_o, q2, k2, kz, vz, totals, attended = attention_front(
+            s1.astype(bf16), packed_qkv, w_o_piece, dy, turn, heads
+        )
+    else:
+        w_qkv = gather_dp(exchange_seq(packed_qkv).reshape(S * rows, q_cols + 2 * HEAD))
+        w_o = gather_dp(w_o_piece)
+        s1_all = gather_seq(s1.astype(bf16))
+        qkv = mm(s1_all, w_qkv)
+        queries = rotate(qkv[:, :q_cols].reshape(length, heads, HEAD), cosine, sine).astype(bf16)
+        queries = jnp.transpose(queries, (1, 0, 2))
+        keys = rotate(qkv[:, None, q_cols : q_cols + HEAD], cosine, sine).astype(bf16)[:, 0]
+        values = qkv[:, q_cols + HEAD :].astype(bf16)
+        attended, totals = attention_forward(queries, keys, values, block_rows)
+        attended = heads_last(attended)
+        summed = scatter_seq(mm(attended, w_o).astype(bf16))
+        dy_all = gather_seq(dy)
+    middle = flat + summed
     r2 = rms_scale(middle)
     s2 = middle * r2
-    dy = cotangent.reshape(tokens, width)
-    dy_all = gather_seq(dy)
     if line:
         out_part, e2, g_gu, down_grad = feedforward(
             s2.astype(bf16), dy_all, w_gu, w_d, down_rows
@@ -1027,10 +1278,6 @@
     d_middle = dy.astype(f32) + r2 * (e2 - s2 * jnp.mean(e2 * s2, axis=-1, keepdims=True))
     if line:
         table = jnp.concatenate([cosine, cosine, sine, -sine], axis=-1)[:, 0] * HEAD ** (-0.5)
-        half = HEAD // 2
-
-        def with_swapped(u):
-            return jnp.concatenate([u, u[..., half:], u[..., :half]], axis=-1)
 
         def with_zeros(u):
             return jnp.concatenate([u, jnp.zeros_like(u)], axis=-1)
@@ -1038,10 +1285,10 @@
         w_o2 = with_zeros(w_o.reshape(heads, 1, HEAD, width).swapaxes(2, 3)).swapaxes(2, 3)
         e1, g_qkv, g_o = attention_back(
             d_middle.astype(bf16),
-            with_swapped(queries),
-            with_swapped(keys),
-            with_zeros(keys),
-            with_zeros(values),
+            q2,
+            k2,
+            kz,
+            vz,
             totals,
             attended,
             s1_all,

time: 671 us -> 608 us (0.906); the launches traced: 662 us -> 607 us
  other arithmetic: 50.1 us -> 24.2 us
  Pallas kernels: 449 us -> 471 us
  blocking collectives: 52.4 us -> 37.9 us
  matrix products: 14 us -> 0 us
  local copies, waits for them, and re-layouts: 37.3 us -> 23.4 us
  waiting for transfers between devices: 24.3 us -> 15.5 us
    pallas_call x2 -> x1, Pallas kernels: 96.5 us -> 159 us  [attention_front(): pl.pallas_call(functools.partial(attention_front_kernel, T, heads), out_s...]
    pallas_call x2 -> x1, Pallas kernels: 101 us -> 56.6 us  [scatter_line(): pl.pallas_call(functools.partial(scatter_kernel, Z, T), out_shape=jax.Sha...]
    reduce_sum x2 -> x0, other arithmetic: 16.3 us -> none  [attention_forward(): jnp.sum(jnp.exp(scores - row_max), axis=-1, keepdims=True)]
    all_to_all x2 -> x1, blocking collectives: 52.4 us -> 37.9 us  [exchange_seq(): lax.all_to_all(pieces, 'seq', split_axis=0, concat_axis=0, tiled=True)]
    dot_general x6 -> x0, matrix products: 14 us -> none  [the longest x2 7.79 us: mm(): lax.dot_general(a, b, (((1,), (0,)), ((), ())), preferred_element_type=f32)]
    ppermute x1, waiting for transfers between devices: 13.5 us -> 4.72 us  [shards(): w_o_piece = lax.ppermute(output_weight, ('dp', 'seq'), forward_perm)]
  transfers between devices with their start and end apart: 7 -> 5, of which waited for: 2 -> 2; matrix products, arithmetic and copies ran while one was open for 14% -> 7% of each run, Pallas kernels for 47% -> 54%
where the time goes in v5:
time: 608 us; the launch traced here: 607 us
  Pallas kernels  471 us (77%)
  blocking collectives  37.9 us (6%)
  other arithmetic  24.2 us (4%)
  local copies, waits for them, and re-layouts  23.4 us (4%)
  starting transfers between devices  19.8 us (3%)
  waiting for transfers between devices  15.5 us (3%)
  between operations  14.6 us (2%)
    pallas_call x1, Pallas kernels, attention_front(): pl.pallas_call(functools.partial(attention_front_kernel, T, heads), out_s...  159 us
    pallas_call x1, Pallas kernels, feedforward(): pl.pallas_call(functools.partial(feedforward_kernel, T), out_shape=(jax.S...  137 us
    pallas_call x1, Pallas kernels, attention_back(): pl.pallas_call(functools.partial(attention_back_kernel, T, heads), out_sh...  114 us
    pallas_call x1, Pallas kernels, scatter_line(): pl.pallas_call(functools.partial(scatter_kernel, Z, T), out_shape=jax.Sha...  56.6 us
    all_to_all x1, blocking collectives, exchange_seq(): lax.all_to_all(pieces, 'seq', split_axis=0, concat_axis=0, tiled=True)  37.9 us
    all_to_all x1, starting transfers between devices, exchange_seq(): lax.all_to_all(pieces, 'seq', split_axis=0, concat_axis=0, tiled=True)  14.9 us
  transfers between devices with their start and end apart: 5, of which 2 were waited for; matrix products, arithmetic and copies ran while one was open for 7% of the time, Pallas kernels for 54%

profile of v5, /device:TPU:26, one launch (start us, length us, event | category | flops | bytes accessed | tf_op | source)
XLA Modules:
  0.0 606.9 jit_solution(11291937408456028463)
XLA Ops:
  9.1 2.5 multiply_convert_fusion.1
  11.6 2.0 reshape.193
  15.0 3.0 reshape.195
  19.8 37.9 %all_to_all.10 = bf16[8,64,1408]{2,1,0:T(8,128)(2,1)S(1)} all-to-all(bf16[8,64,1408]{2,1,0:T(8,128)(2,1)S(1)} %pad_maximum_fusion), channel_id=1, replica_groups=mesh['dp'=4,'seq'=8] {'seq'}, dimensions={0} | all-to-all | bytes 2883584 | tf_op jit(solution)/shard_map/all_to_all | solution.py:1099
  58.2 1.3 fusion.1
  60.5 2.9 collective-permute-start
  65.6 2.0 fusion.13
  67.6 4.2 concatenate.19
  72.7 4.7 collective-permute-done.wo_piece_ref
  77.4 159.1 %attention_front.1 = (f32[128,2048]{1,0:T(8,128)}, bf16[1024,2048]{1,0:T(8,128)(2,1)}, bf16[1024,2048]{1,0:T(8,128)(2,1)}, bf16[2048,384]{1,0:T(8,128)(2,1)}, bf...) custom-call(bf16[128,2048]{1,0:T(8,128)(2,1)} %fusion.4.s1_ref, ...), custom_call_target="tpu_custom_call" | custom-call | tf_op jit(solution)/shard_map/attention_front/pallas_call | solution.py:802
  236.5 1.7 multiply_reduce_fusion.1
  239.3 4.0 pad.14.wd_ref
  243.3 137.2 %feedforward.1 = (bf16[1024,2048]{1,0:T(8,128)(2,1)}, f32[128,2048]{1,0:T(8,128)}, bf16[512,1536]{1,0:T(8,128)(2,1)}, f32[176,2048]{1,0:T(8,128)}) custom-call(bf16[128,2048]{1,0:T(8,128)(2,1)} %multiply_convert_fusion.2.x_ref, bf16[1024,2048]{1,0:T(8,128)(2,1)} %get-tuple-element.37.dy_ref, bf16[2048,1536]{1,0:T(8,128)(2,1)} %all-gather.3.cloned.1.call-done.wgu_ref, ...), custom_call_target="tpu_custom_call" | custom-call | tf_op jit(solution)/shard_map/feedforward/pallas_call | solution.py:603
  380.6 14.9 %all-to-all-start.1 = ((bf16[8,64,1536]{2,1,0:T(8,128)(2,1)}), bf16[8,64,1536]{2,1,0:T(8,128)(2,1)}, u32[]{:S(2)}, u32[]{:S(2)}) async-start(bf16[8,64,1536]{2,1,0:T(8,128)(2,1)} %bitcast.63), calls=%async_computation.1 | async-start | bytes 3145728 | tf_op jit(solution)/shard_map/all_to_all | solution.py:1099
  396.3 1.3 fusion.12.table_ref
  397.6 1.6 concatenate.22
  399.1 56.6 %scatter_seq.1 = f32[128,2048]{1,0:T(8,128)} custom-call(bf16[1024,2048]{1,0:T(8,128)(2,1)} %get-tuple-element.38.p_ref), custom_call_target="tpu_custom_call" | custom-call | tf_op jit(solution)/shard_map/scatter_seq/pallas_call | solution.py:202
  458.0 114.2 %attention_back.1 = (f32[128,2048]{1,0:T(8,128)}, bf16[8,64,384]{2,1,0:T(8,128)(2,1)}, f32[64,2048]{1,0:T(8,128)}) custom-call(bf16[128,2048]{1,0:T(8,128)(2,1)} %fusion.16.dm_ref, bf16[4,1024,128]{2,1,0:T(8,128)(2,1)} %get-tuple-element.40.q_ref, bf16[1024,128]{1,0:T(8,128)(2,1)} %get-tuple-element.41.k_ref, bf16[1024,128]{1,0:T(8,128)(2,1)} %get-tuple-element.42.kz_ref, ...), custom_call_target="tpu_custom_call" | custom-call | tf_op jit(solution)/shard_map/attention_back/pallas_call | solution.py:977
  573.5 1.9 collective-permute-start.1
  575.4 1.6 fusion.5
  577.2 3.8 fusion.9
  581.0 10.1 %collective-permute-done.1 = bf16[64,2048]{1,0:T(8,128)(2,1)S(1)} collective-permute-done((bf16[64,2048]{1,0:T(8,128)(2,1)S(1)}, bf16[64,2048]{1,0:T(8,128)(2,1)S(1)}, u32[]{:S(2)}, u32[]{:S(2)}) %collective-permute-start.1) | collective-permute-done | bytes 262176 | tf_op jit(solution)/shard_map/ppermute | solution.py:1320
  591.9 4.3 spread.1
  597.5 2.6 copy.39
  (110 shorter events, 16.9 us)
Async XLA Ops:
  7.2 232.1 %all-gather.5.cloned.1.call-start = ((), (), s32[]{:S(2)}) async-start(), calls=%async_computation.3 | async-start | bytes 3604480 | tf_op jit(solution)/shard_map/all_gather | solution.py:1091
  7.9 235.4 %all-gather.3.cloned.1.call-start = ((), (), s32[]{:S(2)}) async-start(), calls=%async_computation.2 | async-start | bytes 7864320 | tf_op jit(solution)/shard_map/all_gather | solution.py:1091
  19.8 38.3 %copy-start.29 = (pred[768]{0:T(1024)(128)(4,1)S(1)}, pred[768]{0:T(1024)(128)(4,1)}, u32[]{:S(2)}) copy-start(pred[768]{0:T(1024)(128)(4,1)} %constant.22.clone.1) | copy-start | bytes 2308
  59.5 4.9 copy-start.10
  60.5 17.0 %collective-permute-start = (bf16[64,2048]{1,0:T(8,128)(2,1)S(1)}, bf16[64,2048]{1,0:T(8,128)(2,1)}, u32[]{:S(2)}, u32[]{:S(2)}) collective-permute-start(bf16[64,2048]{1,0:T(8,128)(2,1)S(1)} %copy-done.32), channel_id=1, source_target_pairs={{0,0},{1,8},{2,16},{3,24},{4,1},{5,9},{6,17},{7,25},{8,2},{9,10},{... | collective-permute-start | bytes 786440 | tf_op jit(solution)/shard_map/ppermute | solution.py:1219
  380.5 15.0 %copy-start.30 = (f32[64,1]{0,1:T(1,128)S(1)}, f32[64,1]{0,1:T(1,128)}, u32[]{:S(2)}) copy-start(f32[64,1]{0,1:T(1,128)} %get-tuple-element.63) | copy-start | bytes 772
  380.5 15.0 %copy-start.31 = (f32[64,1]{0,1:T(1,128)S(1)}, f32[64,1]{0,1:T(1,128)}, u32[]{:S(2)}) copy-start(f32[64,1]{0,1:T(1,128)} %get-tuple-element.65) | copy-start | bytes 772
  380.6 15.7 %copy-start.18 = (f32[1024,1,32]{2,0,1:T(8,128)S(1)}, f32[1024,1,32]{2,0,1:T(8,128)}, u32[]{:S(2)}) copy-start(f32[1024,1,32]{2,0,1:T(8,128)} %copy-done.17) | copy-start | bytes 393220
  380.6 15.7 %copy-start.21 = (f32[1024,1,32]{2,0,1:T(8,128)S(1)}, f32[1024,1,32]{2,0,1:T(8,128)}, u32[]{:S(2)}) copy-start(f32[1024,1,32]{2,0,1:T(8,128)} %copy-done.20) | copy-start | bytes 393220
  380.6 15.7 %copy-start.23 = (f32[1024,1,32]{2,0,1:T(8,128)S(1)}, f32[1024,1,32]{2,0,1:T(8,128)}, u32[]{:S(2)}) copy-start(f32[1024,1,32]{2,0,1:T(8,128)} %copy-done.22) | copy-start | bytes 393220
  380.6 211.3 %all-to-all-start.1 = ((bf16[8,64,1536]{2,1,0:T(8,128)(2,1)}), bf16[8,64,1536]{2,1,0:T(8,128)(2,1)}, u32[]{:S(2)}, u32[]{:S(2)}) async-start(bf16[8,64,1536]{2,1,0:T(8,128)(2,1)} %bitcast.63), calls=%async_computation.1 | async-start | bytes 3145728 | tf_op jit(solution)/shard_map/all_to_all | solution.py:1099
  399.1 56.6 %copy-start.12 = (bf16[1,128,2048]{2,1,0:T(8,128)(2,1)S(1)}, bf16[1,128,2048]{2,1,0:T(8,128)(2,1)}, u32[]{:S(2)}) copy-start(bf16[1,128,2048]{2,1,0:T(8,128)(2,1)} %param.11) | copy-start | bytes 1572868
  399.1 56.6 %copy-start.15 = (f32[128,2048]{1,0:T(8,128)S(1)}, f32[128,2048]{1,0:T(8,128)}, u32[]{:S(2)}) copy-start(f32[128,2048]{1,0:T(8,128)} %get-tuple-element.36) | copy-start | bytes 3145732
  399.1 56.7 %copy-start.19 = (f32[128,2048]{1,0:T(8,128)S(1)}, f32[128,2048]{1,0:T(8,128)}, u32[]{:S(2)}) copy-start(f32[128,2048]{1,0:T(8,128)} %get-tuple-element.39) | copy-start | bytes 3145732
  572.2 4.8 copy-start.13
  572.2 4.8 copy-start.16
  573.5 17.5 %collective-permute-start.1 = (bf16[64,2048]{1,0:T(8,128)(2,1)S(1)}, bf16[64,2048]{1,0:T(8,128)(2,1)S(1)}, u32[]{:S(2)}, u32[]{:S(2)}) collective-permute-start(bf16[64,2048]{1,0:T(8,128)(2,1)S(1)} %convert_element_type.87), channel_id=1, source_target_pairs={{0,0},{8,1},{16,2},{24,3},{1,4},{9,5},{17,6},{25,7},{2,8},{10,9},{... | collective-permute-start | bytes 786440 | tf_op jit(solution)/shard_map/ppermute | solution.py:1320
  577.1 14.8 %copy-start = (bf16[64,5632]{1,0:T(8,128)(2,1)S(1)}, bf16[64,5632]{1,0:T(8,128)(2,1)}, u32[]{:S(2)}) copy-start(bf16[64,5632]{1,0:T(8,128)(2,1)} %wg_ref.1) | copy-start | bytes 2162692
  577.1 14.8 %copy-start.1 = (bf16[64,5632]{1,0:T(8,128)(2,1)S(1)}, bf16[64,5632]{1,0:T(8,128)(2,1)}, u32[]{:S(2)}) copy-start(bf16[64,5632]{1,0:T(8,128)(2,1)} %wu_ref.1) | copy-start | bytes 2162692
  577.1 14.8 %copy-start.3 = (bf16[64,2048]{1,0:T(8,128)(2,1)S(1)}, bf16[64,2048]{1,0:T(8,128)(2,1)}, u32[]{:S(2)}) copy-start(bf16[64,2048]{1,0:T(8,128)(2,1)} %wq_ref.1) | copy-start | bytes 786436
  577.1 14.7 %copy-start.4 = (bf16[8,64,384]{2,1,0:T(8,128)(2,1)S(1)}, bf16[8,64,384]{2,1,0:T(8,128)(2,1)}, u32[]{:S(2)}) copy-start(bf16[8,64,384]{2,1,0:T(8,128)(2,1)} %get-tuple-element.51.qkv_ref) | copy-start | bytes 1179652
  577.2 14.7 %copy-start.5 = (f32[64,1]{1,0:T(8,128)S(1)}, f32[64,1]{1,0:T(8,128)}, u32[]{:S(2)}) copy-start(f32[64,1]{1,0:T(8,128)} %copy.33.one_ref) | copy-start | bytes 772
  577.2 14.7 %copy-start.7 = (bf16[64,256]{1,0:T(8,128)(2,1)S(1)}, bf16[64,256]{1,0:T(8,128)(2,1)}, u32[]{:S(2)}) copy-start(bf16[64,256]{1,0:T(8,128)(2,1)} %wk_ref.1) | copy-start | bytes 98308
  577.2 14.7 %copy-start.9 = (bf16[64,256]{1,0:T(8,128)(2,1)S(1)}, bf16[64,256]{1,0:T(8,128)(2,1)}, u32[]{:S(2)}) copy-start(bf16[64,256]{1,0:T(8,128)(2,1)} %wv_ref.1) | copy-start | bytes 98308
  (15 other events, 48.6 us)
Sparse Core Ops, SparseCore 0:
  9.5 27.0 all-gather.4
  59.7 60.1 all-gather.2

commit v6 on v5

--- a/solution.py
+++ b/solution.py
@@ -476,6 +476,34 @@
         self.b_copy().wait_send()
 
 
+class Exchange:
+    def __init__(self, me, src, landing, s_sem, r_sem, own_sem):
+        self.me, self.src, self.landing = me, src, landing
+        self.s_sem, self.r_sem, self.own_sem = s_sem, r_sem, own_sem
+
+    def own(self):
+        return pltpu.make_async_copy(self.src(self.me), self.landing(self.me), self.own_sem)
+
+    def copy(self, peer, sender):
+        return send(
+            self.src(peer), self.landing(sender), self.s_sem.at[peer], self.r_sem.at[sender], peer
+        )
+
+    def start(self, *steps):
+        for step in steps:
+            self.copy((self.me + step) % 8, self.me).start()
+
+    def ready(self):
+        self.own().wait()
+        for step in range(1, 8):
+            peer = (self.me + step) % 8
+            self.copy(peer, peer).wait_recv()
+
+    def finish(self):
+        for step in range(1, 8):
+            self.copy((self.me + step) % 8, self.me).wait_send()
+
+
 class DpGather:
     def __init__(self, own, full, size, s_sem, r_sem):
         dp = lax.axis_index("dp")
@@ -522,8 +550,9 @@
 
 
 def feedforward_kernel(
-    T, x_ref, dy_ref, wgu_ref, wd_ref, pout_ref, e2_ref, ggu_ref, gd_ref,
-    full, hid, dgu, part, ggu, gdown, up_sem, dn_sem, ag_y, ag_r, own_sem,
+    T, x_ref, dy_ref, wgu_ref, wd_ref, out_ref, e2_ref, ggu_ref, gd_ref,
+    full, hid, dgu, pout, part, ggu, gdown, up_sem, dn_sem, ag_y, ag_r, own_sem,
+    pybuf, prbuf, py_s, py_r, pz_s, pz_r,
     ybuf, rbuf, y_s, y_r, z_s, z_r,
     ga, gb, ga_s, ga_r, gb_s, gb_r,
     da, db, da_s, da_r, db_s, db_r,
@@ -533,11 +562,18 @@
     F = hid.shape[1]
     greet(z, y, 4, dp)
     gather = Gather(z, y, T, x_ref, full, up_sem, dn_sem, ag_y, ag_r, own_sem)
+    scatter_out = Scatter(z, y, T, pout, pybuf, prbuf, py_s, py_r, pz_s, pz_r)
     scatter = Scatter(z, y, T, part, ybuf, rbuf, y_s, y_r, z_s, z_r)
     sum_gu = DpSum(ggu, ggu.shape[0] // 4, ga, gb, ga_s, ga_r, gb_s, gb_r)
     sum_down = DpSum(gdown, gd_ref.shape[0], da, db, da_s, da_r, db_s, db_r)
     gather.start()
     gather.own_ready()
+    inner = (z > 0) & (z < 3)
+    at_end = jnp.logical_not(inner)
+
+    def pass_on(rank):
+        scatter_out.pass_on(line_rank(rank, z))
+        scatter.pass_on(line_rank(rank, z))
 
     def compute(i, carry):
         for h in range(1, 4):
@@ -549,29 +585,48 @@
         zz = line_rank(i, z)
         gather.pair_ready(zz)
 
+        @pl.when(i == 2)
+        def _():
+            scatter_out.start(line_rank(1, z))
+
         @pl.when(i == 3)
         def _():
+            scatter_out.start(line_rank(2, z))
             scatter.start(line_rank(2, z))
+
+        @pl.when((i == 3) & at_end)
+        def _():
+            scatter_out.pass_on(line_rank(1, z))
 
         r = pl.ds(pl.multiple_of(zz * 2 * T, 2 * T), 2 * T)
         gu = mm(full[r, :], wgu_ref[...])
         gate, up = gu[:, :F], gu[:, F:]
         sig = 1.0 / (1.0 + jnp.exp(-gate))
         act = gate * sig
-        h = (act * up).astype(bf16)
-        hid[r, :] = h
-        pout_ref[r, :] = mm(h, wd_ref[...]).astype(bf16)
+        hid[r, :] = (act * up).astype(bf16)
         dh = mm_nt(dy_ref[r, :], wd_ref[...])
         dgu[r, :F] = (dh * up * sig * (1.0 + gate * (1.0 - sig))).astype(bf16)
         dgu[r, F:] = (dh * act).astype(bf16)
+        pout[r, :] = mm(hid[r, :], wd_ref[...]).astype(bf16)
+
+        @pl.when(i == 3)
+        def _():
+            scatter_out.start(zz)
+
         part[r, :] = mm_nt(dgu[r, :], wgu_ref[...]).astype(bf16)
         return carry
 
     lax.fori_loop(0, 4, compute, 0)
-    for i in (3, 1, 0):
-        scatter.start(line_rank(i, z))
+    scatter.start(line_rank(3, z))
+    scatter.start(line_rank(1, z))
+    scatter_out.start(z)
+    scatter.start(z)
 
     def gate_up_tile(i, carry):
+        @pl.when((i == 4) & at_end)
+        def _():
+            pass_on(2)
+
         r = pl.ds(pl.multiple_of(i * 256, 256), 256)
         ggu[r, :] = mm_tn(full[:, r], dgu[...]).astype(bf16)
         return carry
@@ -583,15 +638,25 @@
 
     lax.fori_loop(0, 8, gate_up_tile, 0)
     sum_gu.start()
-    scatter.pass_on(line_rank(3, z))
+    pass_on(3 - (z + 1) % 4 // 2)
     lax.fori_loop(0, F // 256, down_tile, 0)
     sum_down.start()
+
+    @pl.when(inner)
+    def _():
+        pass_on(3)
+
     sum_gu.middle()
-    scatter.pass_on(line_rank(2, z))
+
+    @pl.when(inner)
+    def _():
+        scatter_out.pass_on(line_rank(1, z))
+
+    scatter.pass_on(line_rank(1, z))
     sum_down.middle()
-    scatter.pass_on(line_rank(1, z))
     sum_gu.finish(ggu_ref)
     sum_down.finish(gd_ref)
+    scatter_out.finish(out_ref)
     scatter.finish(e2_ref)
     gather.finish()
 
@@ -603,7 +668,7 @@
     return pl.pallas_call(
         functools.partial(feedforward_kernel, T),
         out_shape=(
-            jax.ShapeDtypeStruct((L, width), bf16),
+            jax.ShapeDtypeStruct((T, width), f32),
             jax.ShapeDtypeStruct((T, width), f32),
             jax.ShapeDtypeStruct((width // 4, 2 * F), bf16),
             jax.ShapeDtypeStruct((down_rows, width), f32),
@@ -615,10 +680,12 @@
             pltpu.VMEM((L, F), bf16),
             pltpu.VMEM((L, 2 * F), bf16),
             pltpu.VMEM((L, width), bf16),
+            pltpu.VMEM((L, width), bf16),
             pltpu.VMEM((width, 2 * F), bf16),
             pltpu.VMEM((F, width), bf16),
         ]
         + line_sems(4)
+        + sum_scratch(T, width)
         + sum_scratch(T, width)
         + dp_scratch(width // 4, 2 * F)
         + dp_scratch(down_rows, width),
@@ -630,13 +697,13 @@
 
 
 def attention_front_kernel(
-    T, heads, s1_ref, piece_ref, wo_piece_ref, dy_ref, table_ref,
-    mid_ref, s1_all, dy_all, wqkv, wo, q_out, k2_ref, kz_ref, vz_ref, lse_ref, att_ref,
+    T, heads, s1_ref, piece_ref, gu_ref, wo_piece_ref, dy_ref, table_ref,
+    mid_ref, s1_all, dy_all, wqkv, wgu, wo, q_out, k2_ref, kz_ref, vz_ref, lse_ref, att_ref,
     score, part,
     up_sem, dn_sem, ag_y, ag_r, own_sem,
     up_sem2, dn_sem2, ag_y2, ag_r2, own_sem2,
     ybuf, rbuf, y_s, y_r, z_s, z_r,
-    w_s, w_r, o_s, o_r, ex_s, ex_r, ex_own, wo_own,
+    w_s, w_r, o_s, o_r, g_s, g_r, ex_s, ex_r, gx_s, gx_r, ex_own, gx_own, wo_own,
 ):
     z, y = seq_place()
     me = z * 2 + y
@@ -655,27 +722,25 @@
     w_all = DpGather(w_own, wqkv, 8 * rows, w_s, w_r)
     o_all = DpGather(wo_piece_ref, wo, out_rows, o_s, o_r)
 
-    def landing(peer):
-        return rows_of(wqkv, (dp * 8 + peer) * rows, rows)
-
-    def exchange(peer):
-        return send(piece_ref.at[peer], landing(me), ex_s.at[peer], ex_r.at[me], peer)
-
-    own = pltpu.make_async_copy(piece_ref.at[me], landing(me), ex_own)
-    own.start()
+    g_own = rows_of(wgu, dp * 8 * rows, 8 * rows)
+    g_all = DpGather(g_own, wgu, 8 * rows, g_s, g_r)
+
+    def pieces(src, full, *sems):
+        return Exchange(
+            me, lambda p: src.at[p], lambda p: rows_of(full, (dp * 8 + p) * rows, rows), *sems
+        )
+
+    exchange = pieces(piece_ref, wqkv, ex_s, ex_r, ex_own)
+    exchange_gu = pieces(gu_ref, wgu, gx_s, gx_r, gx_own)
+    exchange.own().start()
+    exchange_gu.own().start()
     own_o = pltpu.make_async_copy(wo_piece_ref, o_all.block(dp), wo_own)
     own_o.start()
-    for step in range(1, 8):
-        exchange((me + step) % 8).start()
+    exchange.start(*range(1, 8))
     gather.start()
     o_all.start()
-    own.wait()
     own_o.wait()
-    for step in range(1, 8):
-        peer = (me + step) % 8
-        send(
-            piece_ref.at[me], landing(peer), ex_s.at[peer], ex_r.at[peer], peer
-        ).wait_recv()
+    exchange.ready()
     w_all.start()
     gather.own_ready()
     gather.hop(1)
@@ -701,6 +766,7 @@
         @pl.when(i == 2)
         def _():
             gather_dy.start()
+            exchange_gu.start(1, 2)
 
         u = line_rank(i, z)
         gather.pair_ready(u)
@@ -734,6 +800,12 @@
             def _():
                 gather_dy.hop(h)
 
+        for k in range(3):
+
+            @pl.when(i == k)
+            def _():
+                exchange_gu.start(*range(2 * k + 3, min(2 * k + 5, 8)))
+
         u = line_rank(3 - i, z)
         r = pl.ds(pl.multiple_of(u * U, U), U)
         q = q_out[:, r, :].reshape(heads * U, 128)
@@ -782,19 +854,24 @@
         return carry
 
     lax.fori_loop(0, 4, unit, 0)
+    exchange_gu.ready()
+    g_all.start()
     scatter.pass_on(line_rank(1, z))
     scatter.finish(mid_ref)
+    g_all.relay()
     for zz in range(4):
         gather.finish_one(zz)
         gather_dy.pair_ready(zz)
         gather_dy.finish_one(zz)
-    for step in range(1, 8):
-        exchange((me + step) % 8).wait_send()
+    exchange.finish()
+    exchange_gu.finish()
     w_all.finish()
     o_all.finish()
-
-
-def attention_front(s1, piece, wo_piece, dy, table, heads, cid=5):
+    g_all.ready()
+    g_all.finish()
+
+
+def attention_front(s1, piece, gu_piece, wo_piece, dy, table, heads, cid=5):
     T, width = s1.shape
     S, rows, cols = piece.shape
     L, q_cols, U = S * T, heads * HEAD, 2 * T
@@ -806,6 +883,7 @@
             jax.ShapeDtypeStruct((L, width), bf16),
             jax.ShapeDtypeStruct((L, width), bf16),
             jax.ShapeDtypeStruct((width, cols), bf16),
+            jax.ShapeDtypeStruct((width, gu_piece.shape[2]), bf16),
             jax.ShapeDtypeStruct((q_cols, width), bf16),
             jax.ShapeDtypeStruct((heads, L, 128), bf16),
             jax.ShapeDtypeStruct((L, 128), bf16),
@@ -814,8 +892,8 @@
             jax.ShapeDtypeStruct((heads, L, 1), f32),
             jax.ShapeDtypeStruct((L, q_cols), bf16),
         ),
-        in_specs=[vmem] * 5,
-        out_specs=(vmem,) * 11,
+        in_specs=[vmem] * 6,
+        out_specs=(vmem,) * 12,
         scratch_shapes=[
             pltpu.VMEM((L // U, heads * U, U), f32),
             pltpu.VMEM((L, width), bf16),
@@ -823,25 +901,25 @@
         + line_sems(4)
         + line_sems(4)
         + sum_scratch(T, width)
-        + [pltpu.SemaphoreType.DMA((3,))] * 4
-        + [pltpu.SemaphoreType.DMA((8,))] * 2
-        + [pltpu.SemaphoreType.DMA] * 2,
+        + [pltpu.SemaphoreType.DMA((3,))] * 6
+        + [pltpu.SemaphoreType.DMA((8,))] * 4
+        + [pltpu.SemaphoreType.DMA] * 3,
         compiler_params=pltpu.CompilerParams(
             collective_id=cid, has_side_effects=True, vmem_limit_bytes=67000000
         ),
         name="attention_front",
-    )(s1, piece, wo_piece, dy, table)
+    )(s1, piece, gu_piece, wo_piece, dy, table)
 
 
 def attention_back_kernel(
-    T, heads, dm_ref, q_ref, k_ref, kz_ref, vz_ref, lse_ref, att_ref, s1_ref, wqkv_ref, wo_ref, table_ref,
-    e1_ref, got_ref, go_ref,
+    T, heads, dm_ref, q_ref, k_ref, kz_ref, vz_ref, lse_ref, att_ref, s1_ref, wqkv_ref, wo_ref, table_ref, ggu_ref,
+    e1_ref, got_ref, go_ref, got_gu_ref,
     full, grads, probs, dprobs, dk, dv, dqkv, part, gqkv, go_part, gsum,
     up_sem, dn_sem, ag_y, ag_r, own_sem,
     ybuf, rbuf, y_s, y_r, z_s, z_r,
     qa, qb, qa_s, qa_r, qb_s, qb_r,
     oa, ob, oa_s, oa_r, ob_s, ob_r,
-    ex_s, ex_r, ex_own,
+    ex_s, ex_r, gx_s, gx_r, ex_own, gx_own,
 ):
     z, y = seq_place()
     me = z * 2 + y
@@ -857,7 +935,14 @@
     scatter = Scatter(z, y, T, part, ybuf, rbuf, y_s, y_r, z_s, z_r)
     sum_qkv = DpSum(gqkv, gqkv.shape[0] // 4, qa, qb, qa_s, qa_r, qb_s, qb_r)
     sum_o = DpSum(go_part, go_part.shape[0] // 4, oa, ob, oa_s, oa_r, ob_s, ob_r)
+    exchange = Exchange(
+        me, lambda p: rows_of(gsum, p * rows, rows), lambda p: got_ref.at[p], ex_s, ex_r, ex_own
+    )
+    exchange_gu = Exchange(
+        me, lambda p: rows_of(ggu_ref, p * rows, rows), lambda p: got_gu_ref.at[p], gx_s, gx_r, gx_own
+    )
     gather.start()
+    exchange_gu.own().start()
     dk[...] = jnp.zeros_like(dk)
     dv[...] = jnp.zeros_like(dv)
     gather.own_ready()
@@ -875,6 +960,14 @@
             @pl.when(i == h - 1)
             def _():
                 gather.hop(h)
+
+        @pl.when(i == 2)
+        def _():
+            exchange_gu.start(1, 2, 3)
+
+        @pl.when(i == 3)
+        def _():
+            exchange_gu.start(4, 5, 6, 7)
 
         u = line_rank(i, z)
         gather.pair_ready(u)
@@ -946,29 +1039,19 @@
     scatter.pass_on(line_rank(2, z))
     sum_qkv.finish(gsum)
 
-    def piece(peer):
-        return rows_of(gsum, peer * rows, rows)
-
-    def exchange(peer):
-        return send(piece(peer), got_ref.at[me], ex_s.at[peer], ex_r.at[me], peer)
-
-    own = pltpu.make_async_copy(piece(me), got_ref.at[me], ex_own)
-    own.start()
-    for step in range(1, 8):
-        exchange((me + step) % 8).start()
+    exchange.own().start()
+    exchange.start(*range(1, 8))
     sum_o.middle()
     scatter.pass_on(line_rank(1, z))
     sum_o.finish(go_ref)
     scatter.finish(e1_ref)
-    own.wait()
-    for step in range(1, 8):
-        peer = (me + step) % 8
-        send(piece(me), got_ref.at[peer], ex_s.at[peer], ex_r.at[peer], peer).wait_recv()
-        exchange(peer).wait_send()
+    for moved in (exchange, exchange_gu):
+        moved.ready()
+        moved.finish()
     gather.finish()
 
 
-def attention_back(dm, q2, k2, kz, vz, lse, attended, s1_all, w_qkv, w_o2, table, rows, cid=4):
+def attention_back(dm, q2, k2, kz, vz, lse, attended, s1_all, w_qkv, w_o2, table, g_gu, rows, cid=4):
     T, width = dm.shape
     heads, L, _ = q2.shape
     cols = w_qkv.shape[1]
@@ -980,9 +1063,10 @@
             jax.ShapeDtypeStruct((T, width), f32),
             jax.ShapeDtypeStruct((8, rows, cols), bf16),
             jax.ShapeDtypeStruct((rows, width), f32),
+            jax.ShapeDtypeStruct((8, rows, g_gu.shape[1]), bf16),
         ),
-        in_specs=[vmem] * 11,
-        out_specs=(vmem,) * 3,
+        in_specs=[vmem] * 12,
+        out_specs=(vmem,) * 4,
         scratch_shapes=[
             pltpu.VMEM((L, width), bf16),
             pltpu.VMEM((heads, U, 128), bf16),
@@ -1000,12 +1084,13 @@
         + sum_scratch(T, width)
         + dp_scratch(width // 4, cols)
         + dp_scratch(rows, width)
-        + [pltpu.SemaphoreType.DMA((8,)), pltpu.SemaphoreType.DMA((8,)), pltpu.SemaphoreType.DMA],
+        + [pltpu.SemaphoreType.DMA((8,))] * 4
+        + [pltpu.SemaphoreType.DMA] * 2,
         compiler_params=pltpu.CompilerParams(
             collective_id=cid, has_side_effects=True, vmem_limit_bytes=67000000
         ),
         name="attention_back",
-    )(dm, q2, k2, kz, vz, lse, attended, s1_all, w_qkv, w_o2, table)
+    )(dm, q2, k2, kz, vz, lse, attended, s1_all, w_qkv, w_o2, table, g_gu)
 
 
 def spread_kernel(
@@ -1080,7 +1165,7 @@
     d_up = (d_hid * (gate * sig)).astype(bf16)
     d_gu = jnp.concatenate([d_gate, d_up], axis=1)
     return (
-        mm(hid, w_d).astype(bf16),
+        scatter_seq(mm(hid, w_d).astype(bf16)),
         scatter_seq(mm_nt(d_gu, w_gu).astype(bf16)),
         scatter_dp(mm_tn(s2_all, d_gu).astype(bf16)),
         scatter_dp(mm_tn(hid, dy_all).astype(bf16)).astype(f32),
@@ -1217,13 +1302,6 @@
     forward_perm = [(Dp * s + d, d * S + s) for s in range(S) for d in range(Dp)]
     backward_perm = [(b, a) for a, b in forward_perm]
     w_o_piece = lax.ppermute(output_weight, ("dp", "seq"), forward_perm)
-    packed = jnp.concatenate(
-        [
-            per_group_hidden(folded(gate_weight, gain_two)),
-            per_group_hidden(folded(up_weight, gain_two)),
-        ],
-        axis=2,
-    )
     line = S == 8 and Dp == 4
     width_f = -(-hidden // 256) * 256 if line else hidden
 
@@ -1232,11 +1310,13 @@
         pads[axis] = (0, width_f - hidden)
         return jnp.pad(part, pads)
 
-    packed = exchange_seq(packed).reshape(S * rows, 2 * hidden)
-    packed = jnp.concatenate(
-        [padded(packed[:, :hidden], 1), padded(packed[:, hidden:], 1)], axis=1
+    packed_gu = jnp.concatenate(
+        [
+            padded(per_group_hidden(folded(gate_weight, gain_two)), 2),
+            padded(per_group_hidden(folded(up_weight, gain_two)), 2),
+        ],
+        axis=2,
     )
-    w_gu = gather_dp(packed)
     w_d = padded(gather_dp(down_weight), 0)
 
     flat = inputs.reshape(tokens, width).astype(f32)
@@ -1248,11 +1328,12 @@
         turn = jnp.concatenate(
             [cosine, cosine, cosine, cosine, -sine, sine, -sine, sine], axis=-1
         )[:, 0]
-        summed, s1_all, dy_all, w_qkv, w_o, q2, k2, kz, vz, totals, attended = attention_front(
-            s1.astype(bf16), packed_qkv, w_o_piece, dy, turn, heads
+        summed, s1_all, dy_all, w_qkv, w_gu, w_o, q2, k2, kz, vz, totals, attended = attention_front(
+            s1.astype(bf16), packed_qkv, packed_gu, w_o_piece, dy, turn, heads
         )
     else:
         w_qkv = gather_dp(exchange_seq(packed_qkv).reshape(S * rows, q_cols + 2 * HEAD))
+        w_gu = gather_dp(exchange_seq(packed_gu).reshape(S * rows, 2 * hidden))
         w_o = gather_dp(w_o_piece)
         s1_all = gather_seq(s1.astype(bf16))
         qkv = mm(s1_all, w_qkv)
@@ -1268,13 +1349,12 @@
     r2 = rms_scale(middle)
     s2 = middle * r2
     if line:
-        out_part, e2, g_gu, down_grad = feedforward(
+        out_sum, e2, g_gu, down_grad = feedforward(
             s2.astype(bf16), dy_all, w_gu, w_d, down_rows
         )
     else:
-        out_part, e2, g_gu, down_grad = feedforward_plain(s2.astype(bf16), dy_all, w_gu, w_d)
-
-    g_gu = exchange_seq(g_gu.reshape(S, rows, 2 * width_f))
+        out_sum, e2, g_gu, down_grad = feedforward_plain(s2.astype(bf16), dy_all, w_gu, w_d)
+
     d_middle = dy.astype(f32) + r2 * (e2 - s2 * jnp.mean(e2 * s2, axis=-1, keepdims=True))
     if line:
         table = jnp.concatenate([cosine, cosine, sine, -sine], axis=-1)[:, 0] * HEAD ** (-0.5)
@@ -1283,7 +1363,7 @@
             return jnp.concatenate([u, jnp.zeros_like(u)], axis=-1)
 
         w_o2 = with_zeros(w_o.reshape(heads, 1, HEAD, width).swapaxes(2, 3)).swapaxes(2, 3)
-        e1, g_qkv, g_o = attention_back(
+        e1, g_qkv, g_o, g_gu = attention_back(
             d_middle.astype(bf16),
             q2,
             k2,
@@ -1295,10 +1375,12 @@
             w_qkv,
             w_o2.reshape(2 * q_cols, width),
             table,
+            g_gu,
             rows,
         )
         g_o = g_o.astype(bf16)
     else:
+        g_gu = exchange_seq(g_gu.reshape(S, rows, 2 * width_f))
         dm_all = gather_seq(d_middle.astype(bf16))
         d_att = heads_first(mm_nt(dm_all, w_o).astype(bf16), heads)
         d_q, d_k, d_v = attention_backward(queries, keys, values, d_att, totals, block_rows)
@@ -1315,7 +1397,7 @@
         g_o = scatter_dp(mm_tn(attended, dm_all).astype(bf16))
         g_qkv = scatter_dp(mm_tn(s1_all, d_qkv).astype(bf16))
         g_qkv = exchange_seq(g_qkv.reshape(S, rows, q_cols + 2 * HEAD))
-    output = (middle + scatter_seq(out_part)).astype(bf16)
+    output = (middle + out_sum).astype(bf16)
     input_grad = d_middle + r1 * (e1 - s1 * jnp.mean(e1 * s1, axis=-1, keepdims=True))
     output_grad = lax.ppermute(g_o, ("dp", "seq"), backward_perm).astype(f32)
 

time: 608 us -> 574 us (0.944)
  blocking collectives: 37.9 us -> 0 us
  Pallas kernels: 471 us -> 497 us
  starting transfers between devices: 19.8 us -> 5.27 us
  waiting for transfers between devices: 15.5 us -> 9.34 us
    pallas_call x1 -> x0, Pallas kernels: 56.6 us -> none  [scatter_line(): pl.pallas_call(functools.partial(scatter_kernel, Z, T), out_shape=jax.Sha...]
    pallas_call x1, Pallas kernels: 137 us -> 179 us  [feedforward(): pl.pallas_call(functools.partial(feedforward_kernel, T), out_shape=(jax.S...]
    all_to_all x1 -> x0, blocking collectives: 37.9 us -> none  [exchange_seq(): lax.all_to_all(pieces, 'seq', split_axis=0, concat_axis=0, tiled=True)]
    pallas_call x1, Pallas kernels: 159 us -> 180 us  [attention_front(): pl.pallas_call(functools.partial(attention_front_kernel, T, heads), out_s...]
    pallas_call x1, Pallas kernels: 114 us -> 135 us  [attention_back(): pl.pallas_call(functools.partial(attention_back_kernel, T, heads), out_sh...]
    all_to_all x1 -> x0, starting transfers between devices: 14.9 us -> none  [exchange_seq(): lax.all_to_all(pieces, 'seq', split_axis=0, concat_axis=0, tiled=True)]
  transfers between devices with their start and end apart: 5 -> 3, of which waited for: 2 -> 1; matrix products, arithmetic and copies ran while one was open for 7% -> 6% of each run, Pallas kernels for 54% -> 32%
where the time goes in v6:
time: 574 us
  Pallas kernels  497 us (87%)
  other arithmetic  25.2 us (4%)
  local copies, waits for them, and re-layouts  22.4 us (4%)
  between operations  14.5 us (3%)
  waiting for transfers between devices  9.34 us (2%)
    pallas_call x1, Pallas kernels, attention_front(): pl.pallas_call(functools.partial(attention_front_kernel, T, heads), out_s...  180 us
    pallas_call x1, Pallas kernels, feedforward(): pl.pallas_call(functools.partial(feedforward_kernel, T), out_shape=(jax.S...  179 us
    pallas_call x1, Pallas kernels, attention_back(): pl.pallas_call(functools.partial(attention_back_kernel, T, heads), out_sh...  135 us
  transfers between devices with their start and end apart: 3, of which 1 were waited for; matrix products, arithmetic and copies ran while one was open for 6% of the time, Pallas kernels for 32%

profile of v6, /device:TPU:26, one launch (start us, length us, event | category | flops | bytes accessed | tf_op | source)
XLA Modules:
  0.0 573.7 jit_solution(13785776581668810766)
XLA Ops:
  7.9 3.3 collective-permute-start
  14.5 1.1 multiply_convert_fusion.3
  15.6 1.2 multiply_convert_fusion.1
  16.8 2.0 reshape.186
  20.1 3.2 reshape.188
  23.8 1.8 reshape.189
  25.5 2.0 fusion.14
  27.5 4.2 concatenate.17
  32.6 1.3 fusion.13.table_ref
  35.0 1.3 fusion.2.gu_ref
  36.3 180.2 %attention_front.1 = (f32[128,2048]{1,0:T(8,128)}, bf16[1024,2048]{1,0:T(8,128)(2,1)}, bf16[1024,2048]{1,0:T(8,128)(2,1)}, bf16[2048,384]{1,0:T(8,128)(2,1)}, bf...) custom-call(bf16[128,2048]{1,0:T(8,128)(2,1)} %fusion.5.s1_ref, ...), custom_call_target="tpu_custom_call" | custom-call | tf_op jit(solution)/shard_map/attention_front/pallas_call | solution.py:879
  216.5 2.9 concatenate.18
  220.6 3.9 pad.14.wd_ref
  224.6 179.1 %feedforward.1 = (f32[128,2048]{1,0:T(8,128)}, f32[128,2048]{1,0:T(8,128)}, bf16[512,1536]{1,0:T(8,128)(2,1)}, f32[176,2048]{1,0:T(8,128)}) custom-call(bf16[128,2048]{1,0:T(8,128)(2,1)} %multiply_convert_fusion.2.x_ref, bf16[1024,2048]{1,0:T(8,128)(2,1)} %get-tuple-element.39.dy_ref, bf16[2048,1536]{1,0:T(8,128)(2,1)} %get-tuple-element.40.wgu_ref, ...), custom_call_target="tpu_custom_call" | custom-call | tf_op jit(solution)/shard_map/feedforward/pallas_call | solution.py:668
  403.7 2.1 multiply_reduce_fusion
  406.2 2.3 fusion.17.dm_ref
  408.5 134.8 %attention_back.1 = (f32[128,2048]{1,0:T(8,128)}, bf16[8,64,384]{2,1,0:T(8,128)(2,1)}, f32[64,2048]{1,0:T(8,128)}, bf16[8,64,1536]{2,1,0:T(8,128)(2,1)}) custom-call(bf16[128,2048]{1,0:T(8,128)(2,1)} %fusion.17.dm_ref, bf16[4,1024,128]{2,1,0:T(8,128)(2,1)} %get-tuple-element.43.q_ref, bf16[1024,128]{1,0:T(8,128)(2,1)} %get-tuple-element.44.k_ref, ...), custom_call_target="tpu_custom_call" | custom-call | tf_op jit(solution)/shard_map/attention_back/pallas_call | solution.py:1060
  543.3 1.8 fusion.6
  545.1 1.1 convert_element_type.87
  546.2 1.9 collective-permute-start.1
  548.3 3.8 fusion.10
  552.1 2.9 spread.1
  556.3 8.7 %collective-permute-done.1 = bf16[64,2048]{1,0:T(8,128)(2,1)S(1)} collective-permute-done((bf16[64,2048]{1,0:T(8,128)(2,1)S(1)}, bf16[64,2048]{1,0:T(8,128)(2,1)S(1)}, u32[]{:S(2)}, u32[]{:S(2)}) %collective-permute-start.1) | collective-permute-done | bytes 262176 | tf_op jit(solution)/shard_map/ppermute | solution.py:1402
  565.8 1.1 copy.43
  (78 shorter events, 11.4 us)
Async XLA Ops:
  7.2 8.4 %copy-start.2 = (bf16[64,5632]{1,0:T(8,128)(2,1)S(1)}, bf16[64,5632]{1,0:T(8,128)(2,1)}, u32[]{:S(2)}) copy-start(bf16[64,5632]{1,0:T(8,128)(2,1)} %wu_ref.1) | copy-start | bytes 2162692
  7.2 8.4 %copy-start = (bf16[64,5632]{1,0:T(8,128)(2,1)S(1)}, bf16[64,5632]{1,0:T(8,128)(2,1)}, u32[]{:S(2)}) copy-start(bf16[64,5632]{1,0:T(8,128)(2,1)} %wg_ref.1) | copy-start | bytes 2162692
  7.2 213.4 %all-gather.2.cloned.1.call-start = ((), (), s32[]{:S(2)}) async-start(), calls=%async_computation | async-start | bytes 3604480 | tf_op jit(solution)/shard_map/all_gather | solution.py:1176
  7.9 28.4 %collective-permute-start = (bf16[64,2048]{1,0:T(8,128)(2,1)}, bf16[64,2048]{1,0:T(8,128)(2,1)}, u32[]{:S(2)}, u32[]{:S(2)}) collective-permute-start(bf16[64,2048]{1,0:T(8,128)(2,1)} %param.16), channel_id=1, source_target_pairs={{0,0},{1,8},{2,16},{3,24},{4,1},{5,9},{6,17},{7,25},{8,2},{9,10},{... | collective-permute-start | bytes 786440 | tf_op jit(solution)/shard_map/ppermute | solution.py:1304
  32.6 2.4 copy-start.19
  216.5 3.0 copy-start.11
  216.5 2.9 copy-start.14
  403.7 2.2 copy-start.15
  403.7 2.5 copy-start.17
  406.2 2.3 copy-start.21
  543.3 4.8 copy-start.13
  543.3 4.8 copy-start.16
  543.3 4.8 copy-start.18
  543.3 4.8 copy-start.22
  546.2 18.7 %collective-permute-start.1 = (bf16[64,2048]{1,0:T(8,128)(2,1)S(1)}, bf16[64,2048]{1,0:T(8,128)(2,1)S(1)}, u32[]{:S(2)}, u32[]{:S(2)}) collective-permute-start(bf16[64,2048]{1,0:T(8,128)(2,1)S(1)} %convert_element_type.87), channel_id=1, source_target_pairs={{0,0},{8,1},{16,2},{24,3},{1,4},{9,5},{17,6},{25,7},{2,8},{10,9},{... | collective-permute-start | bytes 786440 | tf_op jit(solution)/shard_map/ppermute | solution.py:1402
  548.2 3.9 copy-start.1
  548.2 3.9 copy-start.3
  548.2 3.9 copy-start.4
  548.2 3.9 copy-start.5
  548.2 3.9 copy-start.6
  548.2 3.9 copy-start.7
  548.2 3.9 copy-start.8
  548.3 3.9 copy-start.9
  552.1 13.6 %copy-start.20 = (f32[176,2048]{1,0:T(8,128)S(1)}, f32[176,2048]{1,0:T(8,128)}, u32[]{:S(2)}) copy-start(f32[176,2048]{1,0:T(8,128)} %get-tuple-element.99) | copy-start | bytes 4325380
  (2 other events, 4.3 us)
Sparse Core Ops, SparseCore 0:
  9.6 27.0 all-gather.1

commit v7 on v6

--- a/solution.py
+++ b/solution.py
@@ -697,30 +697,86 @@
 
 
 def attention_front_kernel(
-    T, heads, s1_ref, piece_ref, gu_ref, wo_piece_ref, dy_ref, table_ref,
-    mid_ref, s1_all, dy_all, wqkv, wgu, wo, q_out, k2_ref, kz_ref, vz_ref, lse_ref, att_ref,
-    score, part,
+    T, heads, repeats, s1_ref, wq_ref, wk_ref, wv_ref, wg_ref, wu_ref, one_ref, two_ref,
+    wo_piece_ref, wd_piece_ref, dy_ref, cos_ref, sin_ref,
+    mid_ref, s1_all, dy_all, wqkv, wgu, wd, wo, q_out, k2_ref, kz_ref, vz_ref, lse_ref, att_ref,
+    score, part, piece_ref, gu_ref,
     up_sem, dn_sem, ag_y, ag_r, own_sem,
     up_sem2, dn_sem2, ag_y2, ag_r2, own_sem2,
     ybuf, rbuf, y_s, y_r, z_s, z_r,
-    w_s, w_r, o_s, o_r, g_s, g_r, ex_s, ex_r, gx_s, gx_r, ex_own, gx_own, wo_own,
+    w_s, w_r, o_s, o_r, g_s, g_r, d_s, d_r, ex_s, ex_r, gx_s, gx_r, ex_own, gx_own, wo_own, wd_own, turn_s, turn_r,
 ):
     z, y = seq_place()
     me = z * 2 + y
     dp = lax.axis_index("dp")
-    rows, out_rows = piece_ref.shape[1], wo_piece_ref.shape[0]
+    rows, out_rows, down_rows = piece_ref.shape[1], wo_piece_ref.shape[0], wd_piece_ref.shape[0]
+    q_cols, F = heads * HEAD, gu_ref.shape[2] // 2
+    here, there = dp * 8 + me, me * 4 + dp
+    stays = here == there
     barrier = pltpu.get_barrier_semaphore()
+
+    def greet_at(place):
+        pl.semaphore_signal(
+            barrier,
+            inc=1,
+            device_id={"dp": place[0], "seq": place[1]},
+            device_id_type=pl.DeviceIdType.MESH,
+        )
+
     for step in range(1, 8):
         hello(barrier, (me + step) % 8, "seq")
     hello(barrier, dp + 1 - 2 * (dp % 2), "dp")
     hello(barrier, dp + 2 - 4 * (dp // 2), "dp")
-    pl.semaphore_wait(barrier, 9)
+
+    @pl.when(jnp.logical_not(stays))
+    def _():
+        greet_at((here % 4, here // 4))
+        greet_at((there // 8, there % 8))
+
+    gain = one_ref[...]
+    for s in range(8):
+        kv = pl.ds(s // repeats * HEAD, HEAD)
+        q = wq_ref[:, s * q_cols : (s + 1) * q_cols].astype(f32) * gain
+        k, v = wk_ref[:, kv].astype(f32) * gain, wv_ref[:, kv].astype(f32) * gain
+        piece_ref[s, :, :q_cols] = q.astype(bf16)
+        piece_ref[s, :, q_cols:] = jnp.concatenate([k, v], axis=1).astype(bf16)
+
+    @pl.when(stays)
+    def _():
+        pl.semaphore_wait(barrier, 9)
+
+    @pl.when(jnp.logical_not(stays))
+    def _():
+        pl.semaphore_wait(barrier, 11)
+
     gather = Gather(z, y, T, s1_ref, s1_all, up_sem, dn_sem, ag_y, ag_r, own_sem)
     gather_dy = Gather(z, y, T, dy_ref, dy_all, up_sem2, dn_sem2, ag_y2, ag_r2, own_sem2)
     scatter = Scatter(z, y, T, part, ybuf, rbuf, y_s, y_r, z_s, z_r)
     w_own = rows_of(wqkv, dp * 8 * rows, 8 * rows)
     w_all = DpGather(w_own, wqkv, 8 * rows, w_s, w_r)
-    o_all = DpGather(wo_piece_ref, wo, out_rows, o_s, o_r)
+    o_all = DpGather(rows_of(wo, dp * out_rows, out_rows), wo, out_rows, o_s, o_r)
+    d_all = DpGather(wd_piece_ref, wd, down_rows, d_s, d_r)
+
+    def turned_copy():
+        return pltpu.make_async_remote_copy(
+            src_ref=wo_piece_ref,
+            dst_ref=rows_of(wo, here % 4 * out_rows, out_rows),
+            send_sem=turn_s,
+            recv_sem=turn_r,
+            device_id={"dp": here % 4, "seq": here // 4},
+            device_id_type=pl.DeviceIdType.MESH,
+        )
+
+    def landed():
+        mine = o_all.block(dp)
+        return pltpu.make_async_remote_copy(
+            src_ref=mine,
+            dst_ref=mine,
+            send_sem=turn_s,
+            recv_sem=turn_r,
+            device_id={"dp": here % 4, "seq": here // 4},
+            device_id_type=pl.DeviceIdType.MESH,
+        )
 
     g_own = rows_of(wgu, dp * 8 * rows, 8 * rows)
     g_all = DpGather(g_own, wgu, 8 * rows, g_s, g_r)
@@ -732,20 +788,48 @@
 
     exchange = pieces(piece_ref, wqkv, ex_s, ex_r, ex_own)
     exchange_gu = pieces(gu_ref, wgu, gx_s, gx_r, gx_own)
+    gather.start()
     exchange.own().start()
+    exchange.start(*range(1, 8))
+    own_o = pltpu.make_async_copy(wo_piece_ref, o_all.block(dp), wo_own)
+    own_d = pltpu.make_async_copy(wd_piece_ref, d_all.block(dp), wd_own)
+    own_d.start()
+
+    @pl.when(stays)
+    def _():
+        own_o.start()
+
+    @pl.when(jnp.logical_not(stays))
+    def _():
+        turned_copy().start()
+
+    gain_two = two_ref[...]
+    for s in range(8):
+        for half, weight_ref in ((0, wg_ref), (F, wu_ref)):
+            units = [
+                weight_ref[:, pl.ds((d * 8 + s) * down_rows, down_rows)].astype(f32) * gain_two
+                for d in range(4)
+            ]
+            units.append(jnp.zeros((rows, F - 4 * down_rows), f32))
+            gu_ref[s, :, half : half + F] = jnp.concatenate(units, axis=1).astype(bf16)
+    wd[4 * down_rows :, :] = jnp.zeros((F - 4 * down_rows, wd.shape[1]), bf16)
     exchange_gu.own().start()
-    own_o = pltpu.make_async_copy(wo_piece_ref, o_all.block(dp), wo_own)
-    own_o.start()
-    exchange.start(*range(1, 8))
-    gather.start()
-    o_all.start()
-    own_o.wait()
     exchange.ready()
     w_all.start()
     gather.own_ready()
     gather.hop(1)
-    o_all.relay()
+
+    @pl.when(stays)
+    def _():
+        own_o.wait()
+
+    @pl.when(jnp.logical_not(stays))
+    def _():
+        landed().wait_recv()
+
     w_all.relay()
+    o_all.start()
+    d_all.start()
     w_all.ready()
     U = 2 * T
     lane = lax.broadcasted_iota(jnp.int32, (U, 128), 1)
@@ -772,7 +856,7 @@
         gather.pair_ready(u)
         r = pl.ds(pl.multiple_of(u * U, U), U)
         qkv = mm(s1_all[r, :], wqkv[...])
-        cos, sin = table_ref[r, :128], table_ref[r, 128:]
+        cos, sin = cos_ref[r, :], sin_ref[r, :]
 
         def roped(tile):
             return tile * cos + swapped(tile) * sin
@@ -790,7 +874,9 @@
         return carry
 
     lax.fori_loop(0, 4, project, 0)
+    o_all.relay()
     o_all.ready()
+    d_all.relay()
     gather_dy.own_ready()
 
     def unit(i, carry):
@@ -867,23 +953,34 @@
     exchange_gu.finish()
     w_all.finish()
     o_all.finish()
+    own_d.wait()
+    d_all.ready()
+    d_all.finish()
+
+    @pl.when(jnp.logical_not(stays))
+    def _():
+        turned_copy().wait_send()
+
     g_all.ready()
     g_all.finish()
 
 
-def attention_front(s1, piece, gu_piece, wo_piece, dy, table, heads, cid=5):
+def attention_front(s1, weights, gains, wo_piece, wd_piece, dy, cos, sin, F, repeats, cid=5):
     T, width = s1.shape
-    S, rows, cols = piece.shape
+    S = lax.axis_size("seq")
+    heads, rows = H // S, wo_piece.shape[0]
     L, q_cols, U = S * T, heads * HEAD, 2 * T
+    cols = q_cols + 2 * HEAD
     vmem = pl.BlockSpec(memory_space=pltpu.VMEM)
     return pl.pallas_call(
-        functools.partial(attention_front_kernel, T, heads),
+        functools.partial(attention_front_kernel, T, heads, repeats),
         out_shape=(
             jax.ShapeDtypeStruct((T, width), f32),
             jax.ShapeDtypeStruct((L, width), bf16),
             jax.ShapeDtypeStruct((L, width), bf16),
             jax.ShapeDtypeStruct((width, cols), bf16),
-            jax.ShapeDtypeStruct((width, gu_piece.shape[2]), bf16),
+            jax.ShapeDtypeStruct((width, 2 * F), bf16),
+            jax.ShapeDtypeStruct((F, width), bf16),
             jax.ShapeDtypeStruct((q_cols, width), bf16),
             jax.ShapeDtypeStruct((heads, L, 128), bf16),
             jax.ShapeDtypeStruct((L, 128), bf16),
@@ -892,23 +989,25 @@
             jax.ShapeDtypeStruct((heads, L, 1), f32),
             jax.ShapeDtypeStruct((L, q_cols), bf16),
         ),
-        in_specs=[vmem] * 6,
-        out_specs=(vmem,) * 12,
+        in_specs=[vmem] * 13,
+        out_specs=(vmem,) * 13,
         scratch_shapes=[
             pltpu.VMEM((L // U, heads * U, U), f32),
             pltpu.VMEM((L, width), bf16),
+            pltpu.VMEM((S, rows, cols), bf16),
+            pltpu.VMEM((S, rows, 2 * F), bf16),
         ]
         + line_sems(4)
         + line_sems(4)
         + sum_scratch(T, width)
-        + [pltpu.SemaphoreType.DMA((3,))] * 6
+        + [pltpu.SemaphoreType.DMA((3,))] * 8
         + [pltpu.SemaphoreType.DMA((8,))] * 4
-        + [pltpu.SemaphoreType.DMA] * 3,
+        + [pltpu.SemaphoreType.DMA] * 6,
         compiler_params=pltpu.CompilerParams(
             collective_id=cid, has_side_effects=True, vmem_limit_bytes=67000000
         ),
         name="attention_front",
-    )(s1, piece, gu_piece, wo_piece, dy, table)
+    )(s1, *weights, *gains, wo_piece, wd_piece, dy, cos, sin)
 
 
 def attention_back_kernel(
@@ -1301,7 +1400,6 @@
     packed_qkv = jnp.transpose(packed, (1, 0, 2))
     forward_perm = [(Dp * s + d, d * S + s) for s in range(S) for d in range(Dp)]
     backward_perm = [(b, a) for a, b in forward_perm]
-    w_o_piece = lax.ppermute(output_weight, ("dp", "seq"), forward_perm)
     line = S == 8 and Dp == 4
     width_f = -(-hidden // 256) * 256 if line else hidden
 
@@ -1317,7 +1415,6 @@
         ],
         axis=2,
     )
-    w_d = padded(gather_dp(down_weight), 0)
 
     flat = inputs.reshape(tokens, width).astype(f32)
     r1 = rms_scale(flat)
@@ -1325,16 +1422,29 @@
     cosine, sine = rope_tables(length)
     dy = cotangent.reshape(tokens, width)
     if line:
-        turn = jnp.concatenate(
-            [cosine, cosine, cosine, cosine, -sine, sine, -sine, sine], axis=-1
-        )[:, 0]
-        summed, s1_all, dy_all, w_qkv, w_gu, w_o, q2, k2, kz, vz, totals, attended = attention_front(
-            s1.astype(bf16), packed_qkv, packed_gu, w_o_piece, dy, turn, heads
-        )
+        lane = jnp.arange(128)[None, :]
+        frequency = 10000.0 ** (-((lane % (HEAD // 2)).astype(f32) * 2.0) / HEAD)
+        angles = jnp.arange(length, dtype=f32)[:, None] * frequency
+        turn_cos = jnp.cos(angles)
+        turn_sin = jnp.where(lane % HEAD < HEAD // 2, -1.0, 1.0) * jnp.sin(angles)
+        outs = attention_front(
+            s1.astype(bf16),
+            (query_weight, key_weight, value_weight, gate_weight, up_weight),
+            (gain_one, gain_two),
+            output_weight,
+            down_weight,
+            dy,
+            turn_cos,
+            turn_sin,
+            width_f,
+            repeats,
+        )
+        summed, s1_all, dy_all, w_qkv, w_gu, w_d, w_o, q2, k2, kz, vz, totals, attended = outs
     else:
         w_qkv = gather_dp(exchange_seq(packed_qkv).reshape(S * rows, q_cols + 2 * HEAD))
         w_gu = gather_dp(exchange_seq(packed_gu).reshape(S * rows, 2 * hidden))
-        w_o = gather_dp(w_o_piece)
+        w_o = gather_dp(lax.ppermute(output_weight, ("dp", "seq"), forward_perm))
+        w_d = gather_dp(down_weight)
         s1_all = gather_seq(s1.astype(bf16))
         qkv = mm(s1_all, w_qkv)
         queries = rotate(qkv[:, :q_cols].reshape(length, heads, HEAD), cosine, sine).astype(bf16)
@@ -1357,7 +1467,7 @@
 
     d_middle = dy.astype(f32) + r2 * (e2 - s2 * jnp.mean(e2 * s2, axis=-1, keepdims=True))
     if line:
-        table = jnp.concatenate([cosine, cosine, sine, -sine], axis=-1)[:, 0] * HEAD ** (-0.5)
+        table = jnp.where(lane < HEAD, turn_cos, -turn_sin) * HEAD ** (-0.5)
 
         def with_zeros(u):
             return jnp.concatenate([u, jnp.zeros_like(u)], axis=-1)

time: 574 us -> 544 us (0.948)
  local copies, waits for them, and re-layouts: 22.4 us -> 4.67 us
  between operations: 14.5 us -> 0.93 us
  Pallas kernels: 497 us -> 508 us
    pallas_call x1, Pallas kernels: 180 us -> 192 us  [attention_front(): pl.pallas_call(functools.partial(attention_front_kernel, T, heads, repeat...]
    reshape x11 -> x0, local copies, waits for them, and re-layouts: 8.97 us -> none  [the longest x4 6.06 us: per_group_hidden(): weight.reshape(rows, Dp, S, down_rows)]
  transfers between devices with their start and end apart: 3 -> 1, of which waited for: 1 -> 1; matrix products, arithmetic and copies ran while one was open for 6% -> 1% of each run, Pallas kernels for 32% -> 1%
where the time goes in v7:
time: 544 us
  Pallas kernels  508 us (93%)
  other arithmetic  23.3 us (4%)
    pallas_call x1, Pallas kernels, attention_front(): pl.pallas_call(functools.partial(attention_front_kernel, T, heads, repeat...  192 us
    pallas_call x1, Pallas kernels, feedforward(): pl.pallas_call(functools.partial(feedforward_kernel, T), out_shape=(jax.S...  175 us
    pallas_call x1, Pallas kernels, attention_back(): pl.pallas_call(functools.partial(attention_back_kernel, T, heads), out_sh...  138 us
  transfers between devices with their start and end apart: 1, of which 1 were waited for; matrix products, arithmetic and copies ran while one was open for 1% of the time, Pallas kernels for 1%

profile of v7, /device:TPU:26, one launch (start us, length us, event | category | flops | bytes accessed | tf_op | source)
XLA Modules:
  0.0 543.8 jit_solution(9330781771694277348)
XLA Ops:
  0.7 0.7 bitcast_convert_fusion.1
  1.3 0.7 bitcast_convert_fusion
  2.0 1.2 fusion.8
  3.2 0.7 copy.27.two_ref
  3.9 0.7 copy.26.one_ref
  4.6 2.0 fusion.2.s1_ref
  6.6 3.0 select_multiply_fusion
  9.6 192.1 %attention_front.1 = (f32[128,2048]{1,0:T(8,128)}, bf16[1024,2048]{1,0:T(8,128)(2,1)}, bf16[1024,2048]{1,0:T(8,128)(2,1)}, bf16[2048,384]{1,0:T(8,128)(2,1)}, bf...) custom-call(bf16[128,2048]{1,0:T(8,128)(2,1)} %fusion.2.s1_ref, ...), custom_call_target="tpu_custom_call" | custom-call | tf_op jit(solution)/shard_map/attention_front/pallas_call | solution.py:975
  201.7 1.7 multiply_reduce_fusion.1
  203.6 0.9 multiply_convert_fusion.x_ref
  204.5 174.8 %feedforward.1 = (f32[128,2048]{1,0:T(8,128)}, f32[128,2048]{1,0:T(8,128)}, bf16[512,1536]{1,0:T(8,128)(2,1)}, f32[176,2048]{1,0:T(8,128)}) custom-call(bf16[128,2048]{1,0:T(8,128)(2,1)} %multiply_convert_fusion.x_ref, bf16[1024,2048]{1,0:T(8,128)(2,1)} %get-tuple-element.40.dy_ref, bf16[2048,1536]{1,0:T(8,128)(2,1)} %get-tuple-element.41.wgu_ref, ...), custom_call_target="tpu_custom_call" | custom-call | tf_op jit(solution)/shard_map/feedforward/pallas_call | solution.py:668
  379.4 2.1 multiply_reduce_fusion
  381.9 2.3 fusion.16.dm_ref
  384.2 1.6 concatenate.3
  385.8 138.4 %attention_back.1 = (f32[128,2048]{1,0:T(8,128)}, bf16[8,64,384]{2,1,0:T(8,128)(2,1)}, f32[64,2048]{1,0:T(8,128)}, bf16[8,64,1536]{2,1,0:T(8,128)(2,1)}) custom-call(bf16[128,2048]{1,0:T(8,128)(2,1)} %fusion.16.dm_ref, bf16[4,1024,128]{2,1,0:T(8,128)(2,1)} %get-tuple-element.45.q_ref, bf16[1024,128]{1,0:T(8,128)(2,1)} %get-tuple-element.46.k_ref, ...), custom_call_target="tpu_custom_call" | custom-call | tf_op jit(solution)/shard_map/attention_back/pallas_call | solution.py:1159
  524.2 1.2 convert_element_type.49
  525.4 1.9 collective-permute-start
  527.3 1.6 fusion.3
  529.1 3.8 fusion.7
  533.0 2.9 spread.1
  535.9 0.6 reduce
  537.2 4.8 collective-permute-done
  541.9 0.8 convert_element_type.50
  542.7 1.1 copy.31
  (45 shorter events, 1.2 us)
Async XLA Ops:
  201.7 1.7 copy-start.9
  201.7 1.9 copy-start.12
  379.4 2.1 copy-start.10
  379.4 2.2 copy-start.13
  379.4 2.5 copy-start.15
  381.9 2.3 copy-start.18
  524.2 4.8 copy-start.11
  524.2 4.8 copy-start.14
  524.2 4.8 copy-start.16
  525.4 16.5 %collective-permute-start = (bf16[64,2048]{1,0:T(8,128)(2,1)S(1)}, bf16[64,2048]{1,0:T(8,128)(2,1)S(1)}, u32[]{:S(2)}, u32[]{:S(2)}) collective-permute-start(bf16[64,2048]{1,0:T(8,128)(2,1)S(1)} %convert_element_type.49), channel_id=1, source_target_pairs={{0,0},{8,1},{16,2},{24,3},{1,4},{9,5},{17,6},{25,7},{2,8},{10,9},{... | collective-permute-start | bytes 786440 | tf_op jit(solution)/shard_map/ppermute | solution.py:1512
  529.0 3.9 copy-start
  529.0 3.9 copy-start.1
  529.0 3.9 copy-start.2
  529.1 3.9 copy-start.3
  529.1 3.9 copy-start.4
  529.1 3.9 copy-start.5
  529.1 3.9 copy-start.6
  529.1 3.9 copy-start.7
  529.1 3.9 copy-start.8
  533.0 9.8 %copy-start.17 = (f32[176,2048]{1,0:T(8,128)S(1)}, f32[176,2048]{1,0:T(8,128)}, u32[]{:S(2)}) copy-start(f32[176,2048]{1,0:T(8,128)} %get-tuple-element.95) | copy-start | bytes 4325380

commit v8 on v7

--- a/solution.py
+++ b/solution.py
@@ -589,11 +589,6 @@
         def _():
             scatter_out.start(line_rank(1, z))
 
-        @pl.when(i == 3)
-        def _():
-            scatter_out.start(line_rank(2, z))
-            scatter.start(line_rank(2, z))
-
         @pl.when((i == 3) & at_end)
         def _():
             scatter_out.pass_on(line_rank(1, z))
@@ -609,11 +604,16 @@
         dgu[r, F:] = (dh * act).astype(bf16)
         pout[r, :] = mm(hid[r, :], wd_ref[...]).astype(bf16)
 
-        @pl.when(i == 3)
+        @pl.when(i >= 2)
         def _():
             scatter_out.start(zz)
 
         part[r, :] = mm_nt(dgu[r, :], wgu_ref[...]).astype(bf16)
+
+        @pl.when(i == 2)
+        def _():
+            scatter.start(zz)
+
         return carry
 
     lax.fori_loop(0, 4, compute, 0)
@@ -871,6 +871,11 @@
         k2_ref[r, :] = jnp.where(low_lanes, turned, pltpu.roll(swapped(turned), HEAD, 1)).astype(bf16)
         kz_ref[r, :] = jnp.where(low_lanes, turned, 0.0).astype(bf16)
         vz_ref[r, :] = jnp.where(low_lanes, pltpu.roll(tile, HEAD, 1), 0.0).astype(bf16)
+
+        @pl.when(i == 3)
+        def _():
+            exchange_gu.start(3, 4, 5)
+
         return carry
 
     lax.fori_loop(0, 4, project, 0)
@@ -886,11 +891,14 @@
             def _():
                 gather_dy.hop(h)
 
-        for k in range(3):
-
-            @pl.when(i == k)
-            def _():
-                exchange_gu.start(*range(2 * k + 3, min(2 * k + 5, 8)))
+        @pl.when(i == 0)
+        def _():
+            exchange_gu.start(6, 7)
+
+        @pl.when(i == 3)
+        def _():
+            exchange_gu.ready()
+            g_all.start()
 
         u = line_rank(3 - i, z)
         r = pl.ds(pl.multiple_of(u * U, U), U)
@@ -940,8 +948,6 @@
         return carry
 
     lax.fori_loop(0, 4, unit, 0)
-    exchange_gu.ready()
-    g_all.start()
     scatter.pass_on(line_rank(1, z))
     scatter.finish(mid_ref)
     g_all.relay()
@@ -1161,7 +1167,7 @@
         out_shape=(
             jax.ShapeDtypeStruct((T, width), f32),
             jax.ShapeDtypeStruct((8, rows, cols), bf16),
-            jax.ShapeDtypeStruct((rows, width), f32),
+            jax.ShapeDtypeStruct((rows, width), bf16),
             jax.ShapeDtypeStruct((8, rows, g_gu.shape[1]), bf16),
         ),
         in_specs=[vmem] * 12,
@@ -1488,7 +1494,6 @@
             g_gu,
             rows,
         )
-        g_o = g_o.astype(bf16)
     else:
         g_gu = exchange_seq(g_gu.reshape(S, rows, 2 * width_f))
         dm_all = gather_seq(d_middle.astype(bf16))

time: 544 us -> 542 us (level)
  no operation moved by 1% of the time
where the time goes in v8:
time: 542 us; the launch traced here: 541 us
  Pallas kernels  505 us (93%)
  other arithmetic  22.3 us (4%)
  waiting for transfers between devices  6.49 us (1%)
    pallas_call x1, Pallas kernels, attention_front(): pl.pallas_call(functools.partial(attention_front_kernel, T, heads, repeat...  191 us
    pallas_call x1, Pallas kernels, feedforward(): pl.pallas_call(functools.partial(feedforward_kernel, T), out_shape=(jax.S...  170 us
    pallas_call x1, Pallas kernels, attention_back(): pl.pallas_call(functools.partial(attention_back_kernel, T, heads), out_sh...  141 us
  transfers between devices with their start and end apart: 1, of which 1 were waited for; matrix products, arithmetic and copies ran while one was open for 1% of the time, Pallas kernels for 1%

profile of v8, /device:TPU:26, one launch (start us, length us, event | category | flops | bytes accessed | tf_op | source)
XLA Modules:
  0.0 541.4 jit_solution(5562247316318268222)
XLA Ops:
  0.7 0.7 bitcast_convert_fusion.1
  1.3 0.7 bitcast_convert_fusion
  2.0 1.2 fusion.8
  3.2 0.7 copy.27.two_ref
  3.9 0.7 copy.26.one_ref
  4.6 2.0 fusion.2.s1_ref
  6.6 3.0 select_multiply_fusion
  9.6 191.3 %attention_front.1 = (f32[128,2048]{1,0:T(8,128)}, bf16[1024,2048]{1,0:T(8,128)(2,1)}, bf16[1024,2048]{1,0:T(8,128)(2,1)}, bf16[2048,384]{1,0:T(8,128)(2,1)}, bf...) custom-call(bf16[128,2048]{1,0:T(8,128)(2,1)} %fusion.2.s1_ref, ...), custom_call_target="tpu_custom_call" | custom-call | tf_op jit(solution)/shard_map/attention_front/pallas_call | solution.py:981
  200.9 1.7 multiply_reduce_fusion.1
  202.7 0.9 multiply_convert_fusion.x_ref
  203.7 169.7 %feedforward.1 = (f32[128,2048]{1,0:T(8,128)}, f32[128,2048]{1,0:T(8,128)}, bf16[512,1536]{1,0:T(8,128)(2,1)}, f32[176,2048]{1,0:T(8,128)}) custom-call(bf16[128,2048]{1,0:T(8,128)(2,1)} %multiply_convert_fusion.x_ref, bf16[1024,2048]{1,0:T(8,128)(2,1)} %get-tuple-element.40.dy_ref, bf16[2048,1536]{1,0:T(8,128)(2,1)} %get-tuple-element.41.wgu_ref, ...), custom_call_target="tpu_custom_call" | custom-call | tf_op jit(solution)/shard_map/feedforward/pallas_call | solution.py:668
  373.4 2.1 multiply_reduce_fusion
  375.9 2.3 fusion.16.dm_ref
  378.2 1.6 concatenate.3
  379.8 141.1 %attention_back.1 = (f32[128,2048]{1,0:T(8,128)}, bf16[8,64,384]{2,1,0:T(8,128)(2,1)}, bf16[64,2048]{1,0:T(8,128)(2,1)}, bf16[8,64,1536]{2,1,0:T(8,128)(2,1)}) custom-call(bf16[128,2048]{1,0:T(8,128)(2,1)} %fusion.16.dm_ref, bf16[4,1024,128]{2,1,0:T(8,128)(2,1)} %get-tuple-element.45.q_ref, bf16[1024,128]{1,0:T(8,128)(2,1)} %get-tuple-element.46.k_ref, ...), custom_call_target="tpu_custom_call" | custom-call | tf_op jit(solution)/shard_map/attention_back/pallas_call | solution.py:1165
  521.0 2.1 collective-permute-start
  523.0 1.6 fusion.3
  524.8 4.0 fusion.7
  528.8 2.9 spread.1
  531.7 0.6 reduce
  532.4 0.6 reduce.1
  533.0 6.5 %collective-permute-done = bf16[64,2048]{1,0:T(8,128)(2,1)S(1)} collective-permute-done((bf16[64,2048]{1,0:T(8,128)(2,1)}, bf16[64,2048]{1,0:T(8,128)(2,1)S(1)}, u32[]{:S(2)}, u32[]{:S(2)}) %collective-permute-start) | collective-permute-done | bytes 262176 | tf_op jit(solution)/shard_map/ppermute | solution.py:1517
  539.5 0.8 convert_element_type.46
  540.3 1.1 copy.31
  (42 shorter events, 0.6 us)
Async XLA Ops:
  200.9 1.7 copy-start.9
  200.9 1.9 copy-start.12
  373.4 2.1 copy-start.10
  373.4 2.2 copy-start.13
  373.4 2.5 copy-start.15
  375.9 2.3 copy-start.17
  520.9 3.7 copy-start.11
  521.0 3.7 copy-start.14
  521.0 18.5 %collective-permute-start = (bf16[64,2048]{1,0:T(8,128)(2,1)}, bf16[64,2048]{1,0:T(8,128)(2,1)S(1)}, u32[]{:S(2)}, u32[]{:S(2)}) collective-permute-start(bf16[64,2048]{1,0:T(8,128)(2,1)} %get-tuple-element.62), channel_id=1, source_target_pairs={{0,0},{8,1},{16,2},{24,3},{1,4},{9,5},{17,6},{25,7},{2,8},{10,9},{... | collective-permute-start | bytes 786440 | tf_op jit(solution)/shard_map/ppermute | solution.py:1517
  524.7 4.1 copy-start
  524.7 4.1 copy-start.1
  524.7 4.0 copy-start.2
  524.7 4.0 copy-start.3
  524.7 4.0 copy-start.4
  524.8 4.0 copy-start.5
  524.8 4.0 copy-start.6
  524.8 4.0 copy-start.7
  524.8 4.0 copy-start.8
  528.8 11.5 %copy-start.16 = (f32[176,2048]{1,0:T(8,128)S(1)}, f32[176,2048]{1,0:T(8,128)}, u32[]{:S(2)}) copy-start(f32[176,2048]{1,0:T(8,128)} %get-tuple-element.95) | copy-start | bytes 4325380
